TPU v7x, 256 devices: a whole 4x4x8 slice. The times are simulated.
256 devices in a mesh: gx: 16 (over z, core), gy: 4 (over x), gz: 4 (over y).
Axes of the slice: x: 4, y: 4, z: 8, core: 2. Of those that a mesh axis runs over, the one named last changes fastest.
Arguments:
- velocity: float32 [3, 1024, 64, 512], P(None, 'gx', 'gy', 'gz'), may hold values from -6 to 6
- viscosity: float32 [1024, 64, 512], P('gx', 'gy', 'gz'), may hold values from 0.01 to 0.3
- point_force: float32 [3, 262144], P(None, ('gx', 'gy', 'gz')), may hold values from -300 to 300
- point_offset: float32 [3, 262144], P(None, ('gx', 'gy', 'gz')), may hold values from 0 to 1
- point_cell: int32 [262144], P(('gx', 'gy', 'gz')), may hold values from 0 to 131071, as said below
- point_tile: int32 [262144, 1], P(('gx', 'gy', 'gz')), may hold values from 0 to 255, as said below
Outputs:
- new_velocity: float32 [3, 1024, 64, 512], P(None, 'gx', 'gy', 'gz')
- point_velocity: float32 [3, 262144], P(None, ('gx', 'gy', 'gz'))
Inputs may be any that keep to these rules, and one draw needn't show every extreme that they name: `point_tile`: the 1024 points of one device form 8 runs of 128 points in a row; each run names one tile, the 8 tiles of a device differ, the first is the device's own tile and the others differ from it by at most one in each of the three tile coordinates. `point_cell`: the cell's flat index (i * 16 + j) * 128 + k within its tile.
All inputs are finite; a program needn't handle non-finite values.
Results may differ from a plain program's by a relative error of at most 0.0003.
Values sent between devices are 32-bit elements; how exact they have to be, the bound alone decides.
No kernel may reach another device: no remote copies, remote signals or barrier semaphores. Data moves between devices by JAX's collectives and lax.ppermute only.
A program may use at most 64 MiB of HBM per device.

v0:
```python
import functools

import jax
import jax.numpy as jnp
from jax import lax
from jax.experimental import pallas as pl
from jax.experimental.pallas import tpu as pltpu
from jax.sharding import PartitionSpec as P

DT = 0.1
CI, CJ, CK = 64, 16, 128
NS = 3 * CI
CAP = 128
RUNS = 8
NY_DEV, NZ_DEV = 4, 4
PAD_ROWS = 32
F32 = jnp.float32
BF16 = jnp.bfloat16


def vmem():
    return pl.BlockSpec(memory_space=pltpu.VMEM)


def smem():
    return pl.BlockSpec(memory_space=pltpu.SMEM)


def shape(*dims):
    return jax.ShapeDtypeStruct(dims, F32)


def params():
    return pltpu.CompilerParams(vmem_limit_bytes=40 * 1024 * 1024)


def run_code(tile_ref, run):
    target = tile_ref[run * CAP]
    step_a = target // (NY_DEV * NZ_DEV) - lax.axis_index("gx")
    step_b = (target // NZ_DEV) % NY_DEV - lax.axis_index("gy")
    step_c = target % NZ_DEV - lax.axis_index("gz")
    return ((step_a + 1) * 3 + step_b + 1) * 3 + step_c + 1


def pack_y(rows_ref, forward_ref, backward_ref):
    for r in range(2):
        for s in range(0, NS, 8):
            forward_ref[r * NS + s : r * NS + s + 8, :] = rows_ref[
                pl.ds(s * CJ + CJ - 2 + r, 8, stride=CJ), :
            ]
            backward_ref[r * NS + s : r * NS + s + 8, :] = rows_ref[
                pl.ds(s * CJ + r, 8, stride=CJ), :
            ]


def pack_x(rows_ref, forward_ref, backward_ref):
    for c in range(3):
        first = c * CI * CJ
        forward_ref[c * 2 * CJ : (c + 1) * 2 * CJ, :] = rows_ref[
            first + (CI - 2) * CJ : first + CI * CJ, :
        ]
        backward_ref[c * 2 * CJ : (c + 1) * 2 * CJ, :] = rows_ref[first : first + 2 * CJ, :]


def z_masks():
    lane = lax.broadcasted_iota(jnp.int32, (CJ, CK), 1)
    return lane


def pack_z(rows_ref, out_ref):
    lane = z_masks()
    group = lane // 4

    def step(u, blocks):
        shift = lax.rem(2 + 4 * u, CK)
        fresh = []
        for b in range(6):
            first = pl.multiple_of((b * 32 + u) * CJ, CJ)
            turned = pltpu.roll(rows_ref[pl.ds(first, CJ), :], shift, 1)
            fresh.append(jnp.where(group == u, turned, blocks[b]))
        return tuple(fresh)

    zero = jnp.zeros((CJ, CK), F32)
    blocks = lax.fori_loop(0, 32, step, (zero,) * 6)
    for b in range(6):
        out_ref[b * CJ : (b + 1) * CJ, :] = blocks[b]


def pack_kernel(
    tile_ref, force_ref, offset_ref, cell_ref, rows_ref,
    points_ref, xf_ref, xb_ref, yf_ref, yb_ref, zp_ref,
):
    points_ref[...] = jnp.zeros_like(points_ref)
    for run in range(RUNS):
        code = run_code(tile_ref, run)
        lanes = slice(run * CAP, (run + 1) * CAP)
        block = jnp.concatenate(
            [
                force_ref[:, lanes],
                offset_ref[:, lanes],
                cell_ref[run : run + 1, :].astype(F32),
                jnp.ones((1, CAP), F32),
            ],
            axis=0,
        )
        points_ref[code] = block
    pack_y(rows_ref, yf_ref, yb_ref)
    pack_x(rows_ref, xf_ref, xb_ref)
    pack_z(rows_ref, zp_ref)


def weights_along(centre, count):
    middle = lax.broadcasted_iota(jnp.int32, (count, centre.shape[1]), 0).astype(F32) + 0.5
    scaled = (middle - centre) * 0.5
    raw = jnp.exp(-scaled * scaled)
    return raw * (1.0 / jnp.sum(raw, axis=0, keepdims=True))


def point_weights(block):
    cell = block[6:7, :].astype(jnp.int32)
    first = (cell // (CJ * CK)).astype(F32) + block[3:4, :]
    second = ((cell // CK) % CJ).astype(F32) + block[4:5, :]
    third = (cell % CK).astype(F32) + block[5:6, :]
    return weights_along(first, CI), weights_along(second, CJ), weights_along(third, CK)


def halves(value):
    high = value.astype(BF16)
    return high, (value - high.astype(F32)).astype(BF16)


def gather_slots(zlo_ref, zmid_ref, zhi_ref, slots, order):
    filled = jnp.zeros((1, CAP), jnp.int32)
    for group, ref in enumerate((zlo_ref, zmid_ref, zhi_ref)):
        for t in range(9):
            s = group * 9 + t
            value = ref[t]
            slots[s] = value
            filled = filled + jnp.where(value[7:8, :] > 0.5, 1 << s, 0)
    slots[27] = jnp.zeros((8, CAP), F32)
    mask = jnp.max(filled)
    count = jnp.int32(0)
    for s in range(27):
        order[count] = s
        count = count + ((mask >> s) & 1)
    order[count] = 27
    return count


def pair_block(slots, order, pair):
    return jnp.concatenate([slots[order[2 * pair]], slots[order[2 * pair + 1]]], axis=1)


NT = (((1,), (1,)), ((), ()))
NN = (((1,), (0,)), ((), ()))


def spread(slots, order, count, acc):
    acc[...] = jnp.zeros_like(acc)

    def one_pair(pair, carry):
        block = pair_block(slots, order, pair)
        wx, wy, wz = point_weights(block)
        ah, al = halves(jnp.concatenate([block[c : c + 1, :] * wx for c in range(3)], axis=0))
        for j in range(0, CJ, 2):
            plane = jnp.concatenate([wz * wy[j : j + 1, :], wz * wy[j + 1 : j + 2, :]], axis=0)
            bh, bl = halves(plane)
            total = lax.dot_general(ah, bh, NT, preferred_element_type=F32)
            total = total + lax.dot_general(ah, bl, NT, preferred_element_type=F32)
            total = total + lax.dot_general(al, bh, NT, preferred_element_type=F32)
            acc[:, j * CK : (j + 2) * CK] += total
        return carry

    lax.fori_loop(0, (count + 1) // 2, one_pair, 0)


def edge_flags():
    ax, ay, az = (lax.axis_index(n) for n in ("gx", "gy", "gz"))
    nx, ny, nz = (lax.axis_size(n) for n in ("gx", "gy", "gz"))
    return (
        (ax > 0, ax < nx - 1),
        (ay > 0, ay < ny - 1),
        (az > 0, az < nz - 1),
    )


def stage(alpha, beta, rows_ref, base_ref, visc_ref, forcing_ref, halos, padded, zsc, out_ref):
    xlo, xhi, ylo, yhi, zlo, zhi = halos
    (x0, x1), (y0, y1), (z0, z1) = edge_flags()
    step_rows = (CI + 4) * PAD_ROWS
    for c in range(3):
        for n, (ref, ok) in enumerate(((xlo, x0), (xhi, x1))):
            for r in range(2):
                value = ref[(c * 2 + r) * CJ : (c * 2 + r + 1) * CJ, :]
                first = c * step_rows + (n * (CI + 2) + r) * PAD_ROWS + 8
                padded[first : first + CJ, :] = jnp.where(ok, value, 0.0)
        for i in range(0, CI, 8):
            for n, (ref, ok) in enumerate(((ylo, y0), (yhi, y1))):
                for r in range(2):
                    value = ref[r * NS + c * CI + i : r * NS + c * CI + i + 8, :]
                    first = c * step_rows + (i + 2) * PAD_ROWS + (6 + r if n == 0 else 24 + r)
                    padded[pl.ds(first, 8, stride=PAD_ROWS), :] = jnp.where(ok, value, 0.0)
    lane = z_masks()
    low_part = lane % 4 < 2
    for b in range(6):
        part = slice(b * CJ, (b + 1) * CJ)
        zsc[part, :] = jnp.where(
            low_part, jnp.where(z0, zlo[part, :], 0.0), jnp.where(z1, zhi[part, :], 0.0)
        )

    def fill(i, carry):
        for c in range(3):
            source = pl.multiple_of((c * CI + i) * CJ, CJ)
            target = pl.multiple_of(c * step_rows + (i + 2) * PAD_ROWS + 8, 8)
            padded[pl.ds(target, CJ), :] = rows_ref[pl.ds(source, CJ), :]
        return carry

    lax.fori_loop(0, CI, fill, 0)

    at0, at01 = lane == 0, lane < 2
    at127, at126 = lane == CK - 1, lane >= CK - 2

    def one_plane(i, carry):
        shift = lax.rem(2 * CK - 2 - 4 * lax.rem(i, 32), CK)
        visc = visc_ref[pl.ds(pl.multiple_of(i * CJ, CJ), CJ), :]

        def at(c, di, dj):
            first = c * step_rows + (i + 2 + di) * PAD_ROWS + 8 + dj
            return padded[pl.ds(first, CJ), :]

        centre = [at(c, 0, 0) for c in range(3)]
        for c in range(3):
            here = centre[c]
            block = pl.multiple_of((2 * c + i // 32) * CJ, CJ)
            side = pltpu.roll(zsc[pl.ds(block, CJ), :], shift, 1)
            za1 = pltpu.roll(jnp.where(at0, side, here), CK - 1, 1)
            za2 = pltpu.roll(jnp.where(at01, side, here), CK - 2, 1)
            zb1 = pltpu.roll(jnp.where(at127, side, here), 1, 1)
            zb2 = pltpu.roll(jnp.where(at126, side, here), 2, 1)
            xa1, xb1, xa2, xb2 = at(c, 1, 0), at(c, -1, 0), at(c, 2, 0), at(c, -2, 0)
            ya1, yb1, ya2, yb2 = at(c, 0, 1), at(c, 0, -1), at(c, 0, 2), at(c, 0, -2)
            advect = centre[0] * (8.0 * (xa1 - xb1) - (xa2 - xb2))
            advect = advect + centre[1] * (8.0 * (ya1 - yb1) - (ya2 - yb2))
            advect = advect + centre[2] * (8.0 * (za1 - zb1) - (za2 - zb2))
            diffuse = ((xa1 + xb1) + (ya1 + yb1)) + ((za1 + zb1) - 6.0 * here)
            where = pl.ds(pl.multiple_of((c * CI + i) * CJ, CJ), CJ)
            rate = visc * diffuse - advect * (1.0 / 12.0) + forcing_ref[where, :]
            fresh = beta * (here + DT * rate)
            if alpha:
                fresh = fresh + alpha * base_ref[where, :]
            out_ref[where, :] = fresh
        return carry

    lax.fori_loop(0, CI, one_plane, 0)


def first_kernel(
    zlo_p, zmid_p, zhi_p, rows_ref, visc_ref, xlo, xhi, ylo, yhi, zlo, zhi,
    out_ref, forcing_ref, xf_ref, xb_ref, yf_ref, yb_ref, zp_ref,
    slots, order, acc, padded, zsc,
):
    count = gather_slots(zlo_p, zmid_p, zhi_p, slots, order)
    spread(slots, order, count, acc)
    for s in range(0, NS, 8):
        for j in range(CJ):
            forcing_ref[pl.ds(s * CJ + j, 8, stride=CJ), :] = acc[s : s + 8, j * CK : (j + 1) * CK]
    stage(
        0.0, 1.0, rows_ref, rows_ref, visc_ref, forcing_ref,
        (xlo, xhi, ylo, yhi, zlo, zhi), padded, zsc, out_ref,
    )
    pack_y(out_ref, yf_ref, yb_ref)
    pack_x(out_ref, xf_ref, xb_ref)
    pack_z(out_ref, zp_ref)


def second_kernel(
    rows_ref, base_ref, visc_ref, forcing_ref, xlo, xhi, ylo, yhi, zlo, zhi,
    out_ref, xf_ref, xb_ref, yf_ref, yb_ref, zp_ref, padded, zsc,
):
    stage(
        0.75, 0.25, rows_ref, base_ref, visc_ref, forcing_ref,
        (xlo, xhi, ylo, yhi, zlo, zhi), padded, zsc, out_ref,
    )
    pack_y(out_ref, yf_ref, yb_ref)
    pack_x(out_ref, xf_ref, xb_ref)
    pack_z(out_ref, zp_ref)


def third_kernel(
    zlo_p, zmid_p, zhi_p, rows_ref, base_ref, visc_ref, forcing_ref, xlo, xhi, ylo, yhi, zlo, zhi,
    out_ref, sampled_ref, slots, order, padded, zsc, field_high, field_low,
):
    stage(
        1.0 / 3.0, 2.0 / 3.0, rows_ref, base_ref, visc_ref, forcing_ref,
        (xlo, xhi, ylo, yhi, zlo, zhi), padded, zsc, out_ref,
    )
    for j in range(CJ):
        for s in range(0, NS, 16):
            value = jnp.concatenate(
                [
                    out_ref[pl.ds(s * CJ + j, 8, stride=CJ), :],
                    out_ref[pl.ds((s + 8) * CJ + j, 8, stride=CJ), :],
                ],
                axis=0,
            )
            high, low = halves(value)
            field_high[s : s + 16, j * CK : (j + 1) * CK] = high
            field_low[s : s + 16, j * CK : (j + 1) * CK] = low
    count = gather_slots(zlo_p, zmid_p, zhi_p, slots, order)
    sampled_ref[...] = jnp.zeros_like(sampled_ref)

    def one_pair(pair, carry):
        block = pair_block(slots, order, pair)
        wx, wy, wz = point_weights(block)
        total = jnp.zeros((NS, 2 * CAP), F32)
        for j in range(0, CJ, 2):
            plane = jnp.concatenate([wz * wy[j : j + 1, :], wz * wy[j + 1 : j + 2, :]], axis=0)
            bh, bl = halves(plane)
            vh = field_high[:, j * CK : (j + 2) * CK]
            vl = field_low[:, j * CK : (j + 2) * CK]
            total = total + lax.dot_general(vh, bh, NN, preferred_element_type=F32)
            total = total + lax.dot_general(vh, bl, NN, preferred_element_type=F32)
            total = total + lax.dot_general(vl, bh, NN, preferred_element_type=F32)
        result = jnp.concatenate(
            [
                jnp.sum(total[c * CI : (c + 1) * CI, :] * wx, axis=0, keepdims=True)
                for c in range(3)
            ]
            + [jnp.zeros((5, 2 * CAP), F32)],
            axis=0,
        )
        sampled_ref[order[2 * pair]] = result[:, :CAP]
        sampled_ref[order[2 * pair + 1]] = result[:, CAP:]
        return carry

    lax.fori_loop(0, (count + 1) // 2, one_pair, 0)


def pick_kernel(tile_ref, low_ref, mid_ref, high_ref, out_ref, slots):
    slots[0:9] = low_ref[...]
    slots[9:18] = mid_ref[...]
    slots[18:27] = high_ref[...]
    for run in range(RUNS):
        code = run_code(tile_ref, run)
        out_ref[:, run * CAP : (run + 1) * CAP] = slots[code, 0:3, :]


def exchanged(forward, backward, axis):
    count = lax.axis_size(axis)
    up = [(i, (i + 1) % count) for i in range(count)]
    down = [(target, source) for source, target in up]
    return lax.ppermute(forward, axis, up), lax.ppermute(backward, axis, down)


def halos_of(xf, xb, yf, yb, zp):
    ylo, yhi = exchanged(yf, yb, "gy")
    xlo, xhi = exchanged(xf, xb, "gx")
    zlo, zhi = exchanged(zp, zp, "gz")
    return xlo, xhi, ylo, yhi, zlo, zhi


FACES = (
    shape(6 * CJ, CK), shape(6 * CJ, CK), shape(2 * NS, CK), shape(2 * NS, CK), shape(6 * CJ, CK),
)
STENCIL_SCRATCH = [
    pltpu.VMEM((3 * (CI + 4) * PAD_ROWS, CK), F32),
    pltpu.VMEM((6 * CJ, CK), F32),
]
SLOT_SCRATCH = [pltpu.VMEM((28, 8, CAP), F32), pltpu.SMEM((32,), jnp.int32)]


def call(kernel, outs, scratch, *args, scalars=0):
    return pl.pallas_call(
        kernel,
        out_shape=outs,
        in_specs=[smem()] * scalars + [vmem()] * (len(args) - scalars),
        out_specs=jax.tree.map(lambda _: vmem(), outs),
        scratch_shapes=scratch,
        compiler_params=params(),
    )(*args)


def per_device(velocity, viscosity, point_force, point_offset, point_cell, point_tile):
    tiles = point_tile.reshape(-1)
    rows = velocity.reshape(NS * CJ, CK)
    visc = viscosity.reshape(CI * CJ, CK)
    cells = point_cell.reshape(RUNS, CAP)

    points, *faces = call(
        pack_kernel, (shape(27, 8, CAP),) + FACES, [],
        tiles, point_force, point_offset, cells, rows, scalars=1,
    )

    halos = halos_of(*faces)
    from_low, from_high = exchanged(points[18:], points[:9], "gx")
    held = jnp.stack([from_low, points[9:18], from_high]).reshape(3, 3, 3, 8, CAP)
    from_low, from_high = exchanged(held[:, 2], held[:, 0], "gy")
    held = jnp.stack([from_low, held[:, 1], from_high])
    mine = held[:, :, 1].reshape(9, 8, CAP)
    from_low, from_high = exchanged(
        held[:, :, 2].reshape(9, 8, CAP), held[:, :, 0].reshape(9, 8, CAP), "gz"
    )
    arrived = (from_low, mine, from_high)

    section_one, forcing, *faces = call(
        first_kernel, (shape(NS * CJ, CK), shape(NS * CJ, CK)) + FACES,
        SLOT_SCRATCH + [pltpu.VMEM((NS, CJ * CK), F32)] + STENCIL_SCRATCH,
        *arrived, rows, visc, *halos,
    )
    section_two, *faces = call(
        second_kernel, (shape(NS * CJ, CK),) + FACES, STENCIL_SCRATCH,
        section_one, rows, visc, forcing, *halos_of(*faces),
    )
    fresh, sampled = call(
        third_kernel, (shape(NS * CJ, CK), shape(28, 8, CAP)),
        SLOT_SCRATCH + STENCIL_SCRATCH + [pltpu.VMEM((NS, CJ * CK), BF16)] * 2,
        *arrived, section_two, rows, visc, forcing, *halos_of(*faces),
    )

    back = sampled[:27].reshape(3, 9, 8, CAP)
    from_low, from_high = exchanged(back[2], back[0], "gz")
    held = jnp.stack([from_low, back[1], from_high]).reshape(3, 3, 3, 8, CAP)
    from_low, from_high = exchanged(held[:, 2], held[:, 0], "gy")
    held = jnp.stack([from_low, held[:, 1], from_high])
    mine = held[:, :, 1].reshape(9, 8, CAP)
    from_low, from_high = exchanged(
        held[:, :, 2].reshape(9, 8, CAP), held[:, :, 0].reshape(9, 8, CAP), "gx"
    )
    point_velocity = call(
        pick_kernel, shape(3, RUNS * CAP), [pltpu.VMEM((27, 8, CAP), F32)],
        tiles, from_low, mine, from_high, scalars=1,
    )
    return fresh.reshape(velocity.shape), point_velocity


def solution(mesh):
    in_specs = (
        P(None, "gx", "gy", "gz"),
        P("gx", "gy", "gz"),
        P(None, ("gx", "gy", "gz")),
        P(None, ("gx", "gy", "gz")),
        P(("gx", "gy", "gz")),
        P(("gx", "gy", "gz"), None),
    )
    out_specs = (P(None, "gx", "gy", "gz"), P(None, ("gx", "gy", "gz")))
    return jax.shard_map(
        per_device, mesh=mesh, in_specs=in_specs, out_specs=out_specs, check_vma=False
    )
```

profile of v0, /device:TPU:30, one launch (start us, length us, event | category | flops | bytes accessed | tf_op | source)
XLA Modules:
  0.0 129.0 jit_solution(14610930253809074111)
XLA Ops:
  0.6 1.4 %copy-done = f32[3,64,16,128]{3,2,1,0:T(8,128)S(1)} copy-done((f32[3,64,16,128]{3,2,1,0:T(8,128)S(1)}, f32[3,64,16,128]{3,2,1,0:T(8,128)}, u32[]{:S(2)}) %copy-start) | copy-done | bytes 1572888
  4.9 3.4 %shard_map.77 = (f32[27,8,128]{2,1,0:T(8,128)S(1)}, f32[96,128]{1,0:T(8,128)S(1)}, f32[96,128]{1,0:T(8,128)S(1)}, f32[384,128]{1,0:T(8,128)S(1)}, f32[384,128]{1,0:T(8,128)S(1)}, /*index=5*/f32[96,128]{1,0:T(8,128)S(1)}) custom-call(s32[1024]{0:T(1024)S(1)} %bitcast.63, f32[3,1024]{1,0:T(4,128)S(1)} %copy-done.3, f32[3,1024]{1,0:T(4,128)S(1)} %copy-done.4, ...), custom_call_target="tpu_custom_call" | custom-call | tf_op jit(solution)/shard_map/pallas_call | solution.py:373
  8.3 5.3 %collective-permute-start.1 = (f32[9,8,128]{2,1,0:T(8,128)S(1)}, f32[9,8,128]{2,1,0:T(8,128)S(1)}, u32[]{:S(2)}, u32[]{:S(2)}) collective-permute-start(f32[9,8,128]{2,1,0:T(8,128)S(1)} %get-tuple-element.60), channel_id=1, source_target_pairs={{16,0},{32,16},{48,32},{64,48},{80,64},{96,80},{112,96},{128,112},... | collective-permute-start | bytes 110600 | tf_op jit(solution)/shard_map/ppermute | solution.py:352
  13.6 1.6 %collective-permute-done = f32[9,8,128]{2,1,0:T(8,128)S(1)} collective-permute-done((f32[9,8,128]{2,1,0:T(8,128)S(1)}, f32[9,8,128]{2,1,0:T(8,128)S(1)}, u32[]{:S(2)}, u32[]{:S(2)}) %collective-permute-start) | collective-permute-done | bytes 36896 | tf_op jit(solution)/shard_map/ppermute | solution.py:352
  15.9 1.5 %collective-permute-start.3 = (f32[3,3,8,128]{3,2,0,1:T(8,128)S(1)}, f32[3,3,8,128]{3,2,0,1:T(8,128)S(1)}, u32[]{:S(2)}, u32[]{:S(2)}) collective-permute-start(f32[3,3,8,128]{3,2,0,1:T(8,128)S(1)} %get-tuple-element.57), channel_id=1, source_target_pairs={{4,0},{8,4},{12,8},{0,12},{5,1},{9,5},{13,9},{1,13},{6,2},{10,6},{... | collective-permute-start | bytes 110600 | tf_op jit(solution)/shard_map/ppermute | solution.py:352
  18.2 2.5 %collective-permute-start.10 = (f32[96,128]{1,0:T(8,128)S(1)}, f32[96,128]{1,0:T(8,128)S(1)}, u32[]{:S(2)}, u32[]{:S(2)}) collective-permute-start(f32[96,128]{1,0:T(8,128)S(1)} %get-tuple-element.28), channel_id=1, source_target_pairs={{0,1},{1,2},{2,3},{3,0},{4,5},{5,6},{6,7},{7,4},{8,9},{9,10},{10,1... | collective-permute-start | bytes 147464 | tf_op jit(solution)/shard_map/ppermute | solution.py:352
  20.7 3.0 %collective-permute-start.7 = (f32[96,128]{1,0:T(8,128)S(1)}, f32[96,128]{1,0:T(8,128)S(1)}, u32[]{:S(2)}, u32[]{:S(2)}) collective-permute-start(f32[96,128]{1,0:T(8,128)S(1)} %get-tuple-element.25), channel_id=1, source_target_pairs={{16,0},{32,16},{48,32},{64,48},{80,64},{96,80},{112,96},{128,112},... | collective-permute-start | bytes 147464 | tf_op jit(solution)/shard_map/ppermute | solution.py:352
  23.6 1.7 %collective-permute-start.8 = (f32[384,128]{1,0:T(8,128)S(1)}, f32[384,128]{1,0:T(8,128)S(1)}, u32[]{:S(2)}, u32[]{:S(2)}) collective-permute-start(f32[384,128]{1,0:T(8,128)S(1)} %get-tuple-element.26), channel_id=1, source_target_pairs={{0,4},{4,8},{8,12},{12,0},{1,5},{5,9},{9,13},{13,1},{2,6},{6,10},{... | collective-permute-start | bytes 589832 | tf_op jit(solution)/shard_map/ppermute | solution.py:352
  26.3 3.2 %collective-permute-start.4 = (f32[9,8,128]{2,1,0:T(8,128)S(1)}, f32[9,8,128]{2,1,0:T(8,128)S(1)}, u32[]{:S(2)}, u32[]{:S(2)}) collective-permute-start(f32[9,8,128]{2,1,0:T(8,128)S(1)} %bitcast.70), channel_id=1, source_target_pairs={{0,1},{1,2},{2,3},{3,0},{4,5},{5,6},{6,7},{7,4},{8,9},{9,10},{10,1... | collective-permute-start | bytes 110600 | tf_op jit(solution)/shard_map/ppermute | solution.py:352
  29.5 1.9 %collective-permute-done.5.zhi_p = f32[9,8,128]{2,1,0:T(8,128)S(1)} collective-permute-done((f32[9,8,128]{2,1,0:T(8,128)S(1)}, f32[9,8,128]{2,1,0:T(8,128)S(1)}, u32[]{:S(2)}, u32[]{:S(2)}) %collective-permute-start.5) | collective-permute-done | bytes 36896 | tf_op jit(solution)/shard_map/ppermute | solution.py:352
  32.3 18.0 %shard_map.78 = (f32[3072,128]{1,0:T(8,128)S(1)}, f32[3072,128]{1,0:T(8,128)S(1)}, f32[96,128]{1,0:T(8,128)S(1)}, f32[96,128]{1,0:T(8,128)S(1)}, f32[384,128]{1,...) custom-call(f32[9,8,128]{2,1,0:T(8,128)S(1)} %collective-permute-done.4.zlo_p, f32[9,8,128]{2,1,0:T(8,128)S(1)} %bitcast.60, ...), custom_call_target="tpu_custom_call" | custom-call | tf_op jit(solution)/shard_map/pallas_call | solution.py:373
  50.2 1.7 %collective-permute-start.14 = (f32[384,128]{1,0:T(8,128)S(1)}, f32[384,128]{1,0:T(8,128)S(1)}, u32[]{:S(2)}, u32[]{:S(2)}) collective-permute-start(f32[384,128]{1,0:T(8,128)S(1)} %get-tuple-element.33), channel_id=1, source_target_pairs={{0,4},{4,8},{8,12},{12,0},{1,5},{5,9},{9,13},{13,1},{2,6},{6,10},{... | collective-permute-start | bytes 589832 | tf_op jit(solution)/shard_map/ppermute | solution.py:352
  52.4 3.0 %collective-permute-start.13 = (f32[96,128]{1,0:T(8,128)S(1)}, f32[96,128]{1,0:T(8,128)S(1)}, u32[]{:S(2)}, u32[]{:S(2)}) collective-permute-start(f32[96,128]{1,0:T(8,128)S(1)} %get-tuple-element.32), channel_id=1, source_target_pairs={{16,0},{32,16},{48,32},{64,48},{80,64},{96,80},{112,96},{128,112},... | collective-permute-start | bytes 147464 | tf_op jit(solution)/shard_map/ppermute | solution.py:352
  55.3 2.3 %collective-permute-start.17 = (f32[96,128]{1,0:T(8,128)S(1)}, f32[96,128]{1,0:T(8,128)S(1)}, u32[]{:S(2)}, u32[]{:S(2)}) collective-permute-start(f32[96,128]{1,0:T(8,128)S(1)} %get-tuple-element.35), channel_id=1, source_target_pairs={{1,0},{2,1},{3,2},{0,3},{5,4},{6,5},{7,6},{4,7},{9,8},{10,9},{11,1... | collective-permute-start | bytes 147464 | tf_op jit(solution)/shard_map/ppermute | solution.py:352
  57.6 4.3 %collective-permute-start.16 = (f32[96,128]{1,0:T(8,128)S(1)}, f32[96,128]{1,0:T(8,128)S(1)}, u32[]{:S(2)}, u32[]{:S(2)}) collective-permute-start(f32[96,128]{1,0:T(8,128)S(1)} %get-tuple-element.35), channel_id=1, source_target_pairs={{0,1},{1,2},{2,3},{3,0},{4,5},{5,6},{6,7},{7,4},{8,9},{9,10},{10,1... | collective-permute-start | bytes 147464 | tf_op jit(solution)/shard_map/ppermute | solution.py:352
  62.3 1.5 %collective-permute-done.16.zlo = f32[96,128]{1,0:T(8,128)S(1)} collective-permute-done((f32[96,128]{1,0:T(8,128)S(1)}, f32[96,128]{1,0:T(8,128)S(1)}, u32[]{:S(2)}, u32[]{:S(2)}) %collective-permute-start.16) | collective-permute-done | bytes 49184 | tf_op jit(solution)/shard_map/ppermute | solution.py:352
  63.7 14.8 %shard_map.79 = (f32[3072,128]{1,0:T(8,128)S(1)}, f32[96,128]{1,0:T(8,128)S(1)}, f32[96,128]{1,0:T(8,128)S(1)}, f32[384,128]{1,0:T(8,128)S(1)}, f32[384,128]{1,0:T(8,128)S(1)}, /*index=5*/f32[96,128]{1,0:T(8,128)S(1)}) custom-call(f32[3072,128]{1,0:T(8,128)S(1)} %get-tuple-element.29.rows_ref, f32[3072,128]{1,0:T(8,128)S(1)} %bitcast.55, ...), custom_call_target="tpu_custom_call" | custom-call | tf_op jit(solution)/shard_map/pallas_call | solution.py:373
  78.5 1.3 collective-permute-start.20
  80.6 3.0 %collective-permute-start.19 = (f32[96,128]{1,0:T(8,128)S(1)}, f32[96,128]{1,0:T(8,128)S(1)}, u32[]{:S(2)}, u32[]{:S(2)}) collective-permute-start(f32[96,128]{1,0:T(8,128)S(1)} %get-tuple-element.38), channel_id=1, source_target_pairs={{16,0},{32,16},{48,32},{64,48},{80,64},{96,80},{112,96},{128,112},... | collective-permute-start | bytes 147464 | tf_op jit(solution)/shard_map/ppermute | solution.py:352
  85.3 3.5 %collective-permute-start.22 = (f32[96,128]{1,0:T(8,128)S(1)}, f32[96,128]{1,0:T(8,128)S(1)}, u32[]{:S(2)}, u32[]{:S(2)}) collective-permute-start(f32[96,128]{1,0:T(8,128)S(1)} %get-tuple-element.41), channel_id=1, source_target_pairs={{0,1},{1,2},{2,3},{3,0},{4,5},{5,6},{6,7},{7,4},{8,9},{9,10},{10,1... | collective-permute-start | bytes 147464 | tf_op jit(solution)/shard_map/ppermute | solution.py:352
  89.2 1.5 %collective-permute-done.22.zlo = f32[96,128]{1,0:T(8,128)S(1)} collective-permute-done((f32[96,128]{1,0:T(8,128)S(1)}, f32[96,128]{1,0:T(8,128)S(1)}, u32[]{:S(2)}, u32[]{:S(2)}) %collective-permute-start.22) | collective-permute-done | bytes 49184 | tf_op jit(solution)/shard_map/ppermute | solution.py:352
  90.6 15.9 %shard_map.80 = (f32[3072,128]{1,0:T(8,128)}, f32[28,8,128]{2,1,0:T(8,128)S(1)}) custom-call(f32[9,8,128]{2,1,0:T(8,128)S(1)} %collective-permute-done.4.zlo_p, f32[9,8,128]{2,1,0:T(8,128)S(1)} %bitcast.61, f32[9,8,128]{2,1,0:T(8,128)S(1)} %collective-permute-done.5.zhi_p, f32[3072,128]{1,0:T(8,128)S(1)} %get-tuple-element.36.rows_ref, ...), custom_call_target="tpu_custom_call" | custom-call | tf_op jit(solution)/shard_map/pallas_call | solution.py:373
  106.5 3.6 %collective-permute-start.24 = (f32[9,8,128]{2,1,0:T(8,128)S(1)}, f32[9,8,128]{2,1,0:T(8,128)S(1)}, u32[]{:S(2)}, u32[]{:S(2)}) collective-permute-start(f32[9,8,128]{2,1,0:T(8,128)S(1)} %get-tuple-element.44), channel_id=1, source_target_pairs={{0,1},{1,2},{2,3},{3,0},{4,5},{5,6},{6,7},{7,4},{8,9},{9,10},{10,1... | collective-permute-start | bytes 110600 | tf_op jit(solution)/shard_map/ppermute | solution.py:352
  110.2 1.6 %collective-permute-done.24 = f32[9,8,128]{2,1,0:T(8,128)S(1)} collective-permute-done((f32[9,8,128]{2,1,0:T(8,128)S(1)}, f32[9,8,128]{2,1,0:T(8,128)S(1)}, u32[]{:S(2)}, u32[]{:S(2)}) %collective-permute-start.24) | collective-permute-done | bytes 36896 | tf_op jit(solution)/shard_map/ppermute | solution.py:352
  111.8 3.5 %collective-permute-done.25 = f32[9,8,128]{2,1,0:T(8,128)S(1)} collective-permute-done((f32[9,8,128]{2,1,0:T(8,128)S(1)}, f32[9,8,128]{2,1,0:T(8,128)S(1)}, u32[]{:S(2)}, u32[]{:S(2)}) %collective-permute-start.25) | collective-permute-done | bytes 36896 | tf_op jit(solution)/shard_map/ppermute | solution.py:352
  115.4 2.5 %collective-permute-start.26 = (f32[3,3,8,128]{3,2,0,1:T(8,128)S(1)}, f32[3,3,8,128]{3,2,0,1:T(8,128)S(1)}, u32[]{:S(2)}, u32[]{:S(2)}) collective-permute-start(f32[3,3,8,128]{3,2,0,1:T(8,128)S(1)} %get-tuple-element.50), channel_id=1, source_target_pairs={{0,4},{4,8},{8,12},{12,0},{1,5},{5,9},{9,13},{13,1},{2,6},{6,10},{... | collective-permute-start | bytes 110600 | tf_op jit(solution)/shard_map/ppermute | solution.py:352
  117.9 2.3 %collective-permute-start.27 = (f32[3,3,8,128]{3,2,0,1:T(8,128)S(1)}, f32[3,3,8,128]{3,2,0,1:T(8,128)S(1)}, u32[]{:S(2)}, u32[]{:S(2)}) collective-permute-start(f32[3,3,8,128]{3,2,0,1:T(8,128)S(1)} %get-tuple-element.51), channel_id=1, source_target_pairs={{4,0},{8,4},{12,8},{0,12},{5,1},{9,5},{13,9},{1,13},{6,2},{10,6},{... | collective-permute-start | bytes 110600 | tf_op jit(solution)/shard_map/ppermute | solution.py:352
  120.2 1.8 %collective-permute-done.26 = f32[3,3,8,128]{3,2,0,1:T(8,128)S(1)} collective-permute-done((f32[3,3,8,128]{3,2,0,1:T(8,128)S(1)}, f32[3,3,8,128]{3,2,0,1:T(8,128)S(1)}, u32[]{:S(2)}, u32[]{:S(2)}) %collective-permute-start.26) | collective-permute-done | bytes 36896 | tf_op jit(solution)/shard_map/ppermute | solution.py:352
  122.1 1.0 collective-permute-done.27
  123.6 1.1 collective-permute-done.29.high_ref
  124.7 3.0 %collective-permute-done.28.low_ref = f32[9,8,128]{2,1,0:T(8,128)S(1)} collective-permute-done((f32[9,8,128]{2,1,0:T(8,128)S(1)}, f32[9,8,128]{2,1,0:T(8,128)S(1)}, u32[]{:S(2)}, u32[]{:S(2)}) %collective-permute-start.28) | collective-permute-done | bytes 36896 | tf_op jit(solution)/shard_map/ppermute | solution.py:352
  127.7 1.3 %shard_map.81 = f32[3,1024]{1,0:T(4,128)} custom-call(s32[1024]{0:T(1024)S(1)} %bitcast.64, f32[9,8,128]{2,1,0:T(8,128)S(1)} %collective-permute-done.28.low_ref, f32[9,8,128]{2,1,0:T(8,128)S(1)} %bitcast.62, f32[9,8,128]{2,1,0:T(8,128)S(1)} %collective-permute-done.29.high_ref), custom_call_target="tpu_custom_call" | custom-call | tf_op jit(solution)/shard_map/pallas_call | solution.py:373
  (59 shorter events, 10.1 us)
Async XLA Ops:
  4.9 27.4 %copy-start.2 = (f32[64,16,128]{2,1,0:T(8,128)S(1)}, f32[64,16,128]{2,1,0:T(8,128)}, u32[]{:S(2)}) copy-start(f32[64,16,128]{2,1,0:T(8,128)} %param.7) | copy-start | bytes 1572868
  8.3 7.0 %collective-permute-start = (f32[9,8,128]{2,1,0:T(8,128)S(1)}, f32[9,8,128]{2,1,0:T(8,128)S(1)}, u32[]{:S(2)}, u32[]{:S(2)}) collective-permute-start(f32[9,8,128]{2,1,0:T(8,128)S(1)} %get-tuple-element.59), channel_id=1, source_target_pairs={{0,16},{16,32},{32,48},{48,64},{64,80},{80,96},{96,112},{112,128},... | collective-permute-start | bytes 110600 | tf_op jit(solution)/shard_map/ppermute | solution.py:352
  8.3 6.9 %collective-permute-start.1 = (f32[9,8,128]{2,1,0:T(8,128)S(1)}, f32[9,8,128]{2,1,0:T(8,128)S(1)}, u32[]{:S(2)}, u32[]{:S(2)}) collective-permute-start(f32[9,8,128]{2,1,0:T(8,128)S(1)} %get-tuple-element.60), channel_id=1, source_target_pairs={{16,0},{32,16},{48,32},{64,48},{80,64},{96,80},{112,96},{128,112},... | collective-permute-start | bytes 110600 | tf_op jit(solution)/shard_map/ppermute | solution.py:352
  15.3 5.3 %collective-permute-start.2 = (f32[3,3,8,128]{3,2,0,1:T(8,128)S(1)}, f32[3,3,8,128]{3,2,0,1:T(8,128)S(1)}, u32[]{:S(2)}, u32[]{:S(2)}) collective-permute-start(f32[3,3,8,128]{3,2,0,1:T(8,128)S(1)} %get-tuple-element.56), channel_id=1, source_target_pairs={{0,4},{4,8},{8,12},{12,0},{1,5},{5,9},{9,13},{13,1},{2,6},{6,10},{... | collective-permute-start | bytes 110600 | tf_op jit(solution)/shard_map/ppermute | solution.py:352
  15.9 7.7 %collective-permute-start.3 = (f32[3,3,8,128]{3,2,0,1:T(8,128)S(1)}, f32[3,3,8,128]{3,2,0,1:T(8,128)S(1)}, u32[]{:S(2)}, u32[]{:S(2)}) collective-permute-start(f32[3,3,8,128]{3,2,0,1:T(8,128)S(1)} %get-tuple-element.57), channel_id=1, source_target_pairs={{4,0},{8,4},{12,8},{0,12},{5,1},{9,5},{13,9},{1,13},{6,2},{10,6},{... | collective-permute-start | bytes 110600 | tf_op jit(solution)/shard_map/ppermute | solution.py:352
  17.4 8.9 %collective-permute-start.11 = (f32[96,128]{1,0:T(8,128)S(1)}, f32[96,128]{1,0:T(8,128)S(1)}, u32[]{:S(2)}, u32[]{:S(2)}) collective-permute-start(f32[96,128]{1,0:T(8,128)S(1)} %get-tuple-element.28), channel_id=1, source_target_pairs={{1,0},{2,1},{3,2},{0,3},{5,4},{6,5},{7,6},{4,7},{9,8},{10,9},{11,1... | collective-permute-start | bytes 147464 | tf_op jit(solution)/shard_map/ppermute | solution.py:352
  18.2 11.4 %collective-permute-start.10 = (f32[96,128]{1,0:T(8,128)S(1)}, f32[96,128]{1,0:T(8,128)S(1)}, u32[]{:S(2)}, u32[]{:S(2)}) collective-permute-start(f32[96,128]{1,0:T(8,128)S(1)} %get-tuple-element.28), channel_id=1, source_target_pairs={{0,1},{1,2},{2,3},{3,0},{4,5},{5,6},{6,7},{7,4},{8,9},{9,10},{10,1... | collective-permute-start | bytes 147464 | tf_op jit(solution)/shard_map/ppermute | solution.py:352
  20.6 4.7 %collective-permute-start.6 = (f32[96,128]{1,0:T(8,128)S(1)}, f32[96,128]{1,0:T(8,128)S(1)}, u32[]{:S(2)}, u32[]{:S(2)}) collective-permute-start(f32[96,128]{1,0:T(8,128)S(1)} %get-tuple-element.24), channel_id=1, source_target_pairs={{0,16},{16,32},{32,48},{48,64},{64,80},{80,96},{96,112},{112,128},... | collective-permute-start | bytes 147464 | tf_op jit(solution)/shard_map/ppermute | solution.py:352
  20.7 5.6 %collective-permute-start.7 = (f32[96,128]{1,0:T(8,128)S(1)}, f32[96,128]{1,0:T(8,128)S(1)}, u32[]{:S(2)}, u32[]{:S(2)}) collective-permute-start(f32[96,128]{1,0:T(8,128)S(1)} %get-tuple-element.25), channel_id=1, source_target_pairs={{16,0},{32,16},{48,32},{64,48},{80,64},{96,80},{112,96},{128,112},... | collective-permute-start | bytes 147464 | tf_op jit(solution)/shard_map/ppermute | solution.py:352
  23.6 7.9 %collective-permute-start.8 = (f32[384,128]{1,0:T(8,128)S(1)}, f32[384,128]{1,0:T(8,128)S(1)}, u32[]{:S(2)}, u32[]{:S(2)}) collective-permute-start(f32[384,128]{1,0:T(8,128)S(1)} %get-tuple-element.26), channel_id=1, source_target_pairs={{0,4},{4,8},{8,12},{12,0},{1,5},{5,9},{9,13},{13,1},{2,6},{6,10},{... | collective-permute-start | bytes 589832 | tf_op jit(solution)/shard_map/ppermute | solution.py:352
  25.4 6.9 %collective-permute-start.9 = (f32[384,128]{1,0:T(8,128)S(1)}, f32[384,128]{1,0:T(8,128)S(1)}, u32[]{:S(2)}, u32[]{:S(2)}) collective-permute-start(f32[384,128]{1,0:T(8,128)S(1)} %get-tuple-element.27), channel_id=1, source_target_pairs={{4,0},{8,4},{12,8},{0,12},{5,1},{9,5},{13,9},{1,13},{6,2},{10,6},{... | collective-permute-start | bytes 589832 | tf_op jit(solution)/shard_map/ppermute | solution.py:352
  26.2 5.2 %collective-permute-start.5 = (f32[9,8,128]{2,1,0:T(8,128)S(1)}, f32[9,8,128]{2,1,0:T(8,128)S(1)}, u32[]{:S(2)}, u32[]{:S(2)}) collective-permute-start(f32[9,8,128]{2,1,0:T(8,128)S(1)} %bitcast.71), channel_id=1, source_target_pairs={{1,0},{2,1},{3,2},{0,3},{5,4},{6,5},{7,6},{4,7},{9,8},{10,9},{11,1... | collective-permute-start | bytes 110600 | tf_op jit(solution)/shard_map/ppermute | solution.py:352
  26.3 5.1 %collective-permute-start.4 = (f32[9,8,128]{2,1,0:T(8,128)S(1)}, f32[9,8,128]{2,1,0:T(8,128)S(1)}, u32[]{:S(2)}, u32[]{:S(2)}) collective-permute-start(f32[9,8,128]{2,1,0:T(8,128)S(1)} %bitcast.70), channel_id=1, source_target_pairs={{0,1},{1,2},{2,3},{3,0},{4,5},{5,6},{6,7},{7,4},{8,9},{9,10},{10,1... | collective-permute-start | bytes 110600 | tf_op jit(solution)/shard_map/ppermute | solution.py:352
  50.2 13.5 %collective-permute-start.14 = (f32[384,128]{1,0:T(8,128)S(1)}, f32[384,128]{1,0:T(8,128)S(1)}, u32[]{:S(2)}, u32[]{:S(2)}) collective-permute-start(f32[384,128]{1,0:T(8,128)S(1)} %get-tuple-element.33), channel_id=1, source_target_pairs={{0,4},{4,8},{8,12},{12,0},{1,5},{5,9},{9,13},{13,1},{2,6},{6,10},{... | collective-permute-start | bytes 589832 | tf_op jit(solution)/shard_map/ppermute | solution.py:352
  52.0 11.7 %collective-permute-start.15 = (f32[384,128]{1,0:T(8,128)S(1)}, f32[384,128]{1,0:T(8,128)S(1)}, u32[]{:S(2)}, u32[]{:S(2)}) collective-permute-start(f32[384,128]{1,0:T(8,128)S(1)} %get-tuple-element.34), channel_id=1, source_target_pairs={{4,0},{8,4},{12,8},{0,12},{5,1},{9,5},{13,9},{1,13},{6,2},{10,6},{... | collective-permute-start | bytes 589832 | tf_op jit(solution)/shard_map/ppermute | solution.py:352
  52.4 5.3 %collective-permute-start.12 = (f32[96,128]{1,0:T(8,128)S(1)}, f32[96,128]{1,0:T(8,128)S(1)}, u32[]{:S(2)}, u32[]{:S(2)}) collective-permute-start(f32[96,128]{1,0:T(8,128)S(1)} %get-tuple-element.31), channel_id=1, source_target_pairs={{0,16},{16,32},{32,48},{48,64},{64,80},{80,96},{96,112},{112,128},... | collective-permute-start | bytes 147464 | tf_op jit(solution)/shard_map/ppermute | solution.py:352
  52.4 9.6 %collective-permute-start.13 = (f32[96,128]{1,0:T(8,128)S(1)}, f32[96,128]{1,0:T(8,128)S(1)}, u32[]{:S(2)}, u32[]{:S(2)}) collective-permute-start(f32[96,128]{1,0:T(8,128)S(1)} %get-tuple-element.32), channel_id=1, source_target_pairs={{16,0},{32,16},{48,32},{64,48},{80,64},{96,80},{112,96},{128,112},... | collective-permute-start | bytes 147464 | tf_op jit(solution)/shard_map/ppermute | solution.py:352
  55.3 7.0 %collective-permute-start.17 = (f32[96,128]{1,0:T(8,128)S(1)}, f32[96,128]{1,0:T(8,128)S(1)}, u32[]{:S(2)}, u32[]{:S(2)}) collective-permute-start(f32[96,128]{1,0:T(8,128)S(1)} %get-tuple-element.35), channel_id=1, source_target_pairs={{1,0},{2,1},{3,2},{0,3},{5,4},{6,5},{7,6},{4,7},{9,8},{10,9},{11,1... | collective-permute-start | bytes 147464 | tf_op jit(solution)/shard_map/ppermute | solution.py:352
  57.6 6.1 %collective-permute-start.16 = (f32[96,128]{1,0:T(8,128)S(1)}, f32[96,128]{1,0:T(8,128)S(1)}, u32[]{:S(2)}, u32[]{:S(2)}) collective-permute-start(f32[96,128]{1,0:T(8,128)S(1)} %get-tuple-element.35), channel_id=1, source_target_pairs={{0,1},{1,2},{2,3},{3,0},{4,5},{5,6},{6,7},{7,4},{8,9},{9,10},{10,1... | collective-permute-start | bytes 147464 | tf_op jit(solution)/shard_map/ppermute | solution.py:352
  78.5 12.1 %collective-permute-start.20 = (f32[384,128]{1,0:T(8,128)S(1)}, f32[384,128]{1,0:T(8,128)S(1)}, u32[]{:S(2)}, u32[]{:S(2)}) collective-permute-start(f32[384,128]{1,0:T(8,128)S(1)} %get-tuple-element.39), channel_id=1, source_target_pairs={{0,4},{4,8},{8,12},{12,0},{1,5},{5,9},{9,13},{13,1},{2,6},{6,10},{... | collective-permute-start | bytes 589832 | tf_op jit(solution)/shard_map/ppermute | solution.py:352
  79.8 10.9 %collective-permute-start.21 = (f32[384,128]{1,0:T(8,128)S(1)}, f32[384,128]{1,0:T(8,128)S(1)}, u32[]{:S(2)}, u32[]{:S(2)}) collective-permute-start(f32[384,128]{1,0:T(8,128)S(1)} %get-tuple-element.40), channel_id=1, source_target_pairs={{4,0},{8,4},{12,8},{0,12},{5,1},{9,5},{13,9},{1,13},{6,2},{10,6},{... | collective-permute-start | bytes 589832 | tf_op jit(solution)/shard_map/ppermute | solution.py:352
  80.6 4.7 %collective-permute-start.18 = (f32[96,128]{1,0:T(8,128)S(1)}, f32[96,128]{1,0:T(8,128)S(1)}, u32[]{:S(2)}, u32[]{:S(2)}) collective-permute-start(f32[96,128]{1,0:T(8,128)S(1)} %get-tuple-element.37), channel_id=1, source_target_pairs={{0,16},{16,32},{32,48},{48,64},{64,80},{80,96},{96,112},{112,128},... | collective-permute-start | bytes 147464 | tf_op jit(solution)/shard_map/ppermute | solution.py:352
  80.6 8.3 %collective-permute-start.19 = (f32[96,128]{1,0:T(8,128)S(1)}, f32[96,128]{1,0:T(8,128)S(1)}, u32[]{:S(2)}, u32[]{:S(2)}) collective-permute-start(f32[96,128]{1,0:T(8,128)S(1)} %get-tuple-element.38), channel_id=1, source_target_pairs={{16,0},{32,16},{48,32},{64,48},{80,64},{96,80},{112,96},{128,112},... | collective-permute-start | bytes 147464 | tf_op jit(solution)/shard_map/ppermute | solution.py:352
  83.6 5.6 %collective-permute-start.23 = (f32[96,128]{1,0:T(8,128)S(1)}, f32[96,128]{1,0:T(8,128)S(1)}, u32[]{:S(2)}, u32[]{:S(2)}) collective-permute-start(f32[96,128]{1,0:T(8,128)S(1)} %get-tuple-element.41), channel_id=1, source_target_pairs={{1,0},{2,1},{3,2},{0,3},{5,4},{6,5},{7,6},{4,7},{9,8},{10,9},{11,1... | collective-permute-start | bytes 147464 | tf_op jit(solution)/shard_map/ppermute | solution.py:352
  85.3 5.3 %collective-permute-start.22 = (f32[96,128]{1,0:T(8,128)S(1)}, f32[96,128]{1,0:T(8,128)S(1)}, u32[]{:S(2)}, u32[]{:S(2)}) collective-permute-start(f32[96,128]{1,0:T(8,128)S(1)} %get-tuple-element.41), channel_id=1, source_target_pairs={{0,1},{1,2},{2,3},{3,0},{4,5},{5,6},{6,7},{7,4},{8,9},{9,10},{10,1... | collective-permute-start | bytes 147464 | tf_op jit(solution)/shard_map/ppermute | solution.py:352
  90.6 37.1 %copy-start.6 = (s32[1024,1]{0,1:T(1,128)S(1)}, s32[1024,1]{0,1:T(1,128)}, u32[]{:S(2)}) copy-start(s32[1024,1]{0,1:T(1,128)} %param.11) | copy-start | bytes 12292
  106.5 5.3 %collective-permute-start.24 = (f32[9,8,128]{2,1,0:T(8,128)S(1)}, f32[9,8,128]{2,1,0:T(8,128)S(1)}, u32[]{:S(2)}, u32[]{:S(2)}) collective-permute-start(f32[9,8,128]{2,1,0:T(8,128)S(1)} %get-tuple-element.44), channel_id=1, source_target_pairs={{0,1},{1,2},{2,3},{3,0},{4,5},{5,6},{6,7},{7,4},{8,9},{9,10},{10,1... | collective-permute-start | bytes 110600 | tf_op jit(solution)/shard_map/ppermute | solution.py:352
  110.2 5.2 %collective-permute-start.25 = (f32[9,8,128]{2,1,0:T(8,128)S(1)}, f32[9,8,128]{2,1,0:T(8,128)S(1)}, u32[]{:S(2)}, u32[]{:S(2)}) collective-permute-start(f32[9,8,128]{2,1,0:T(8,128)S(1)} %get-tuple-element.45), channel_id=1, source_target_pairs={{1,0},{2,1},{3,2},{0,3},{5,4},{6,5},{7,6},{4,7},{9,8},{10,9},{11,1... | collective-permute-start | bytes 110600 | tf_op jit(solution)/shard_map/ppermute | solution.py:352
  115.4 6.7 %collective-permute-start.26 = (f32[3,3,8,128]{3,2,0,1:T(8,128)S(1)}, f32[3,3,8,128]{3,2,0,1:T(8,128)S(1)}, u32[]{:S(2)}, u32[]{:S(2)}) collective-permute-start(f32[3,3,8,128]{3,2,0,1:T(8,128)S(1)} %get-tuple-element.50), channel_id=1, source_target_pairs={{0,4},{4,8},{8,12},{12,0},{1,5},{5,9},{9,13},{13,1},{2,6},{6,10},{... | collective-permute-start | bytes 110600 | tf_op jit(solution)/shard_map/ppermute | solution.py:352
  117.9 5.2 %collective-permute-start.27 = (f32[3,3,8,128]{3,2,0,1:T(8,128)S(1)}, f32[3,3,8,128]{3,2,0,1:T(8,128)S(1)}, u32[]{:S(2)}, u32[]{:S(2)}) collective-permute-start(f32[3,3,8,128]{3,2,0,1:T(8,128)S(1)} %get-tuple-element.51), channel_id=1, source_target_pairs={{4,0},{8,4},{12,8},{0,12},{5,1},{9,5},{13,9},{1,13},{6,2},{10,6},{... | collective-permute-start | bytes 110600 | tf_op jit(solution)/shard_map/ppermute | solution.py:352
  123.1 1.7 %collective-permute-start.29 = (f32[9,8,128]{2,1,0:T(8,128)S(1)}, f32[9,8,128]{2,1,0:T(8,128)S(1)}, u32[]{:S(2)}, u32[]{:S(2)}) collective-permute-start(f32[9,8,128]{2,1,0:T(8,128)S(1)} %bitcast.79), channel_id=1, source_target_pairs={{16,0},{32,16},{48,32},{64,48},{80,64},{96,80},{112,96},{128,112},... | collective-permute-start | bytes 110600 | tf_op jit(solution)/shard_map/ppermute | solution.py:352
  123.1 4.6 %collective-permute-start.28 = (f32[9,8,128]{2,1,0:T(8,128)S(1)}, f32[9,8,128]{2,1,0:T(8,128)S(1)}, u32[]{:S(2)}, u32[]{:S(2)}) collective-permute-start(f32[9,8,128]{2,1,0:T(8,128)S(1)} %bitcast.75), channel_id=1, source_target_pairs={{0,16},{16,32},{32,48},{48,64},{64,80},{80,96},{96,112},{112,128},... | collective-permute-start | bytes 110600 | tf_op jit(solution)/shard_map/ppermute | solution.py:352
  (6 other events, 31.7 us)
where the time goes:
time: 131 us; the launch traced here: 129 us
  Pallas kernels  53.3 us (41%)
  starting transfers between devices  49.7 us (38%)
  waiting for transfers between devices  20.9 us (16%)
  local copies, waits for them, and re-layouts  4.28 us (3%)
    pallas_call x5, Pallas kernels, call(): pl.pallas_call(kernel, out_shape=outs, in_specs=[smem()] * scalars + [vme...  53.3 us
    ppermute x30, starting transfers between devices, exchanged(): return (lax.ppermute(forward, axis, up), lax.ppermute(backward, axis, down))  49.7 us
    ppermute x30, waiting for transfers between devices, exchanged(): return (lax.ppermute(forward, axis, up), lax.ppermute(backward, axis, down))  20.9 us
    unnamed x16, local copies, waits for them, and re-layouts  4.22 us
  transfers between devices with their start and end apart: 30, of which 15 were waited for; matrix products, arithmetic and copies ran while one was open for 0% of the time, Pallas kernels for 0%

commit v1 on v0

--- a/solution.py
+++ b/solution.py
@@ -13,6 +13,7 @@
 CAP = 128
 RUNS = 8
 NY_DEV, NZ_DEV = 4, 4
+UNROLL = 4
 PAD_ROWS = 32
 F32 = jnp.float32
 BF16 = jnp.bfloat16
@@ -39,7 +40,12 @@
     step_a = target // (NY_DEV * NZ_DEV) - lax.axis_index("gx")
     step_b = (target // NZ_DEV) % NY_DEV - lax.axis_index("gy")
     step_c = target % NZ_DEV - lax.axis_index("gz")
-    return ((step_a + 1) * 3 + step_b + 1) * 3 + step_c + 1
+    group = 1 - step_a * (1 - 2 * lax.rem(lax.axis_index("gx"), 2))
+    return (group * 3 + step_b + 1) * 3 + step_c + 1
+
+
+def is_even():
+    return lax.rem(lax.axis_index("gx"), 2) == 0
 
 
 def pack_y(rows_ref, forward_ref, backward_ref):
@@ -53,13 +59,14 @@
             ]
 
 
-def pack_x(rows_ref, forward_ref, backward_ref):
+def pack_x(rows_ref, first_ref, second_ref):
+    even = is_even()
     for c in range(3):
-        first = c * CI * CJ
-        forward_ref[c * 2 * CJ : (c + 1) * 2 * CJ, :] = rows_ref[
-            first + (CI - 2) * CJ : first + CI * CJ, :
-        ]
-        backward_ref[c * 2 * CJ : (c + 1) * 2 * CJ, :] = rows_ref[first : first + 2 * CJ, :]
+        base = c * CI * CJ
+        upper = rows_ref[base + (CI - 2) * CJ : base + CI * CJ, :]
+        lower = rows_ref[base : base + 2 * CJ, :]
+        first_ref[c * 2 * CJ : (c + 1) * 2 * CJ, :] = jnp.where(even, upper, lower)
+        second_ref[c * 2 * CJ : (c + 1) * 2 * CJ, :] = jnp.where(even, lower, upper)
 
 
 def z_masks():
@@ -71,17 +78,18 @@
     lane = z_masks()
     group = lane // 4
 
-    def step(u, blocks):
-        shift = lax.rem(2 + 4 * u, CK)
-        fresh = []
-        for b in range(6):
-            first = pl.multiple_of((b * 32 + u) * CJ, CJ)
-            turned = pltpu.roll(rows_ref[pl.ds(first, CJ), :], shift, 1)
-            fresh.append(jnp.where(group == u, turned, blocks[b]))
-        return tuple(fresh)
+    def step(t, blocks):
+        blocks = list(blocks)
+        for r in range(UNROLL):
+            u = t * UNROLL + r
+            for b in range(6):
+                first = pl.multiple_of((b * 32 + u) * CJ, CJ)
+                turned = pltpu.roll(rows_ref[pl.ds(first, CJ), :], 2 + 4 * u, 1)
+                blocks[b] = jnp.where(group == u, turned, blocks[b])
+        return tuple(blocks)
 
     zero = jnp.zeros((CJ, CK), F32)
-    blocks = lax.fori_loop(0, 32, step, (zero,) * 6)
+    blocks = lax.fori_loop(0, 32 // UNROLL, step, (zero,) * 6)
     for b in range(6):
         out_ref[b * CJ : (b + 1) * CJ, :] = blocks[b]
 
@@ -185,13 +193,16 @@
 
 
 def stage(alpha, beta, rows_ref, base_ref, visc_ref, forcing_ref, halos, padded, zsc, out_ref):
-    xlo, xhi, ylo, yhi, zlo, zhi = halos
+    xa, xb, ylo, yhi, zlo, zhi = halos
+    even = is_even()
     (x0, x1), (y0, y1), (z0, z1) = edge_flags()
     step_rows = (CI + 4) * PAD_ROWS
     for c in range(3):
-        for n, (ref, ok) in enumerate(((xlo, x0), (xhi, x1))):
-            for r in range(2):
-                value = ref[(c * 2 + r) * CJ : (c * 2 + r + 1) * CJ, :]
+        for r in range(2):
+            part = slice((c * 2 + r) * CJ, (c * 2 + r + 1) * CJ)
+            lower = jnp.where(even, xb[part, :], xa[part, :])
+            upper = jnp.where(even, xa[part, :], xb[part, :])
+            for n, (value, ok) in enumerate(((lower, x0), (upper, x1))):
                 first = c * step_rows + (n * (CI + 2) + r) * PAD_ROWS + 8
                 padded[first : first + CJ, :] = jnp.where(ok, value, 0.0)
         for i in range(0, CI, 8):
@@ -208,50 +219,59 @@
             low_part, jnp.where(z0, zlo[part, :], 0.0), jnp.where(z1, zhi[part, :], 0.0)
         )
 
-    def fill(i, carry):
-        for c in range(3):
-            source = pl.multiple_of((c * CI + i) * CJ, CJ)
-            target = pl.multiple_of(c * step_rows + (i + 2) * PAD_ROWS + 8, 8)
-            padded[pl.ds(target, CJ), :] = rows_ref[pl.ds(source, CJ), :]
+    def fill(t, carry):
+        for r in range(UNROLL):
+            i = t * UNROLL + r
+            for c in range(3):
+                source = pl.multiple_of((c * CI + i) * CJ, CJ)
+                target = pl.multiple_of(c * step_rows + (i + 2) * PAD_ROWS + 8, 8)
+                padded[pl.ds(target, CJ), :] = rows_ref[pl.ds(source, CJ), :]
         return carry
 
-    lax.fori_loop(0, CI, fill, 0)
+    lax.fori_loop(0, CI // UNROLL, fill, 0)
 
     at0, at01 = lane == 0, lane < 2
     at127, at126 = lane == CK - 1, lane >= CK - 2
 
-    def one_plane(i, carry):
-        shift = lax.rem(2 * CK - 2 - 4 * lax.rem(i, 32), CK)
-        visc = visc_ref[pl.ds(pl.multiple_of(i * CJ, CJ), CJ), :]
+    def one_plane(half, u):
+        i = half * 32 + u
+        visc = (beta * DT) * visc_ref[pl.ds(pl.multiple_of(i * CJ, CJ), CJ), :]
+        keep = beta - 6.0 * visc
 
         def at(c, di, dj):
             first = c * step_rows + (i + 2 + di) * PAD_ROWS + 8 + dj
             return padded[pl.ds(first, CJ), :]
 
         centre = [at(c, 0, 0) for c in range(3)]
+        along = [(beta * DT / 12.0) * value for value in centre]
         for c in range(3):
             here = centre[c]
-            block = pl.multiple_of((2 * c + i // 32) * CJ, CJ)
-            side = pltpu.roll(zsc[pl.ds(block, CJ), :], shift, 1)
+            block = (2 * c + half) * CJ
+            side = pltpu.roll(zsc[block : block + CJ, :], 126 - 4 * u, 1)
             za1 = pltpu.roll(jnp.where(at0, side, here), CK - 1, 1)
             za2 = pltpu.roll(jnp.where(at01, side, here), CK - 2, 1)
             zb1 = pltpu.roll(jnp.where(at127, side, here), 1, 1)
             zb2 = pltpu.roll(jnp.where(at126, side, here), 2, 1)
             xa1, xb1, xa2, xb2 = at(c, 1, 0), at(c, -1, 0), at(c, 2, 0), at(c, -2, 0)
             ya1, yb1, ya2, yb2 = at(c, 0, 1), at(c, 0, -1), at(c, 0, 2), at(c, 0, -2)
-            advect = centre[0] * (8.0 * (xa1 - xb1) - (xa2 - xb2))
-            advect = advect + centre[1] * (8.0 * (ya1 - yb1) - (ya2 - yb2))
-            advect = advect + centre[2] * (8.0 * (za1 - zb1) - (za2 - zb2))
-            diffuse = ((xa1 + xb1) + (ya1 + yb1)) + ((za1 + zb1) - 6.0 * here)
+            advect = along[0] * (8.0 * (xa1 - xb1) - (xa2 - xb2))
+            advect = advect + along[1] * (8.0 * (ya1 - yb1) - (ya2 - yb2))
+            advect = advect + along[2] * (8.0 * (za1 - zb1) - (za2 - zb2))
+            around = ((xa1 + xb1) + (ya1 + yb1)) + (za1 + zb1)
             where = pl.ds(pl.multiple_of((c * CI + i) * CJ, CJ), CJ)
-            rate = visc * diffuse - advect * (1.0 / 12.0) + forcing_ref[where, :]
-            fresh = beta * (here + DT * rate)
+            fresh = (keep * here + visc * around) - advect + (beta * DT) * forcing_ref[where, :]
             if alpha:
                 fresh = fresh + alpha * base_ref[where, :]
             out_ref[where, :] = fresh
-        return carry
-
-    lax.fori_loop(0, CI, one_plane, 0)
+
+    for half in range(2):
+
+        def planes(t, carry, half=half):
+            for r in range(UNROLL):
+                one_plane(half, t * UNROLL + r)
+            return carry
+
+        lax.fori_loop(0, 32 // UNROLL, planes, 0)
 
 
 def first_kernel(
@@ -352,9 +372,18 @@
     return lax.ppermute(forward, axis, up), lax.ppermute(backward, axis, down)
 
 
+def swapped(first, second, axis):
+    count = lax.axis_size(axis)
+    pairs = [[], []]
+    for start in range(2):
+        for i in range(start, count, 2):
+            pairs[start] += [(i, (i + 1) % count), ((i + 1) % count, i)]
+    return lax.ppermute(first, axis, pairs[0]), lax.ppermute(second, axis, pairs[1])
+
+
 def halos_of(xf, xb, yf, yb, zp):
     ylo, yhi = exchanged(yf, yb, "gy")
-    xlo, xhi = exchanged(xf, xb, "gx")
+    xlo, xhi = swapped(xf, xb, "gx")
     zlo, zhi = exchanged(zp, zp, "gz")
     return xlo, xhi, ylo, yhi, zlo, zhi
 
@@ -392,8 +421,8 @@
     )
 
     halos = halos_of(*faces)
-    from_low, from_high = exchanged(points[18:], points[:9], "gx")
-    held = jnp.stack([from_low, points[9:18], from_high]).reshape(3, 3, 3, 8, CAP)
+    from_first, from_second = swapped(points[:9], points[18:], "gx")
+    held = jnp.stack([from_first, points[9:18], from_second]).reshape(3, 3, 3, 8, CAP)
     from_low, from_high = exchanged(held[:, 2], held[:, 0], "gy")
     held = jnp.stack([from_low, held[:, 1], from_high])
     mine = held[:, :, 1].reshape(9, 8, CAP)
@@ -423,12 +452,12 @@
     from_low, from_high = exchanged(held[:, 2], held[:, 0], "gy")
     held = jnp.stack([from_low, held[:, 1], from_high])
     mine = held[:, :, 1].reshape(9, 8, CAP)
-    from_low, from_high = exchanged(
-        held[:, :, 2].reshape(9, 8, CAP), held[:, :, 0].reshape(9, 8, CAP), "gx"
+    from_first, from_second = swapped(
+        held[:, :, 0].reshape(9, 8, CAP), held[:, :, 2].reshape(9, 8, CAP), "gx"
     )
     point_velocity = call(
         pick_kernel, shape(3, RUNS * CAP), [pltpu.VMEM((27, 8, CAP), F32)],
-        tiles, from_low, mine, from_high, scalars=1,
+        tiles, from_first, mine, from_second, scalars=1,
     )
     return fresh.reshape(velocity.shape), point_velocity
 

time: 131 us -> 98.5 us (0.75); the launches traced: 129 us -> 99.2 us
  Pallas kernels: 53.3 us -> 27.6 us
  starting transfers between devices: 49.7 us -> 43.6 us
  waiting for transfers between devices: 20.9 us -> 23 us
    pallas_call x5, Pallas kernels: 53.3 us -> 27.6 us  [call(): pl.pallas_call(kernel, out_shape=outs, in_specs=[smem()] * scalars + [vme...]
    ppermute x30 -> x20, starting transfers between devices: 49.7 us -> 31.9 us  [exchanged(): return (lax.ppermute(forward, axis, up), lax.ppermute(backward, axis, down))]
    ppermute x0 -> x10, starting transfers between devices: none -> 11.8 us  [the longest x5 10.1 us: swapped(): lax.ppermute(second, axis, pairs[1])]
    ppermute x0 -> x10, waiting for transfers between devices: none -> 6.26 us  [the longest x5 6.2 us: swapped(): lax.ppermute(second, axis, pairs[1])]
    ppermute x30 -> x20, waiting for transfers between devices: 20.9 us -> 16.7 us  [exchanged(): return (lax.ppermute(forward, axis, up), lax.ppermute(backward, axis, down))]
  transfers between devices with their start and end apart: 30 -> 30, of which waited for: 15 -> 13; matrix products, arithmetic and copies ran while one was open for 0% -> 0% of each run, Pallas kernels for 0% -> 0%
where the time goes in v1:
time: 98.5 us; the launch traced here: 99.2 us
  starting transfers between devices  43.6 us (44%)
  Pallas kernels  27.6 us (28%)
  waiting for transfers between devices  23 us (23%)
  local copies, waits for them, and re-layouts  4.28 us (4%)
    ppermute x20, starting transfers between devices, exchanged(): return (lax.ppermute(forward, axis, up), lax.ppermute(backward, axis, down))  31.9 us
    pallas_call x5, Pallas kernels, call(): pl.pallas_call(kernel, out_shape=outs, in_specs=[smem()] * scalars + [vme...  27.6 us
    ppermute x20, waiting for transfers between devices, exchanged(): return (lax.ppermute(forward, axis, up), lax.ppermute(backward, axis, down))  16.7 us
    ppermute x5, starting transfers between devices, swapped(): lax.ppermute(second, axis, pairs[1])  10.1 us
    ppermute x5, waiting for transfers between devices, swapped(): lax.ppermute(second, axis, pairs[1])  6.2 us
    unnamed x16, local copies, waits for them, and re-layouts  4.22 us
  transfers between devices with their start and end apart: 30, of which 13 were waited for; matrix products, arithmetic and copies ran while one was open for 0% of the time, Pallas kernels for 0%

profile of v1, /device:TPU:30, one launch (start us, length us, event | category | flops | bytes accessed | tf_op | source)
XLA Modules:
  0.0 99.2 jit_solution(16747908577151347498)
XLA Ops:
  0.6 1.4 %copy-done = f32[3,64,16,128]{3,2,1,0:T(8,128)S(1)} copy-done((f32[3,64,16,128]{3,2,1,0:T(8,128)S(1)}, f32[3,64,16,128]{3,2,1,0:T(8,128)}, u32[]{:S(2)}) %copy-start) | copy-done | bytes 1572888
  4.9 1.7 %shard_map.77 = (f32[27,8,128]{2,1,0:T(8,128)S(1)}, f32[96,128]{1,0:T(8,128)S(1)}, f32[96,128]{1,0:T(8,128)S(1)}, f32[384,128]{1,0:T(8,128)S(1)}, f32[384,128]{1,0:T(8,128)S(1)}, /*index=5*/f32[96,128]{1,0:T(8,128)S(1)}) custom-call(s32[1024]{0:T(1024)S(1)} %bitcast.63, f32[3,1024]{1,0:T(4,128)S(1)} %copy-done.3, f32[3,1024]{1,0:T(4,128)S(1)} %copy-done.4, ...), custom_call_target="tpu_custom_call" | custom-call | tf_op jit(solution)/shard_map/pallas_call | solution.py:402
  6.7 6.0 %collective-permute-start.1 = (f32[9,8,128]{2,1,0:T(8,128)S(1)}, f32[9,8,128]{2,1,0:T(8,128)S(1)}, u32[]{:S(2)}, u32[]{:S(2)}) collective-permute-start(f32[9,8,128]{2,1,0:T(8,128)S(1)} %get-tuple-element.60), channel_id=1, source_target_pairs={{16,32},{32,16},{48,64},{64,48},{80,96},{96,80},{112,128},{128,112... | collective-permute-start | bytes 110600 | tf_op jit(solution)/shard_map/ppermute | solution.py:381
  12.7 1.6 %collective-permute-done.1 = f32[9,8,128]{2,1,0:T(8,128)S(1)} collective-permute-done((f32[9,8,128]{2,1,0:T(8,128)S(1)}, f32[9,8,128]{2,1,0:T(8,128)S(1)}, u32[]{:S(2)}, u32[]{:S(2)}) %collective-permute-start.1) | collective-permute-done | bytes 36896 | tf_op jit(solution)/shard_map/ppermute | solution.py:381
  14.9 1.5 %collective-permute-start.3 = (f32[3,3,8,128]{3,2,0,1:T(8,128)S(1)}, f32[3,3,8,128]{3,2,0,1:T(8,128)S(1)}, u32[]{:S(2)}, u32[]{:S(2)}) collective-permute-start(f32[3,3,8,128]{3,2,0,1:T(8,128)S(1)} %get-tuple-element.57), channel_id=1, source_target_pairs={{4,0},{8,4},{12,8},{0,12},{5,1},{9,5},{13,9},{1,13},{6,2},{10,6},{... | collective-permute-start | bytes 110600 | tf_op jit(solution)/shard_map/ppermute | solution.py:372
  16.4 0.7 collective-permute-start.11
  17.2 2.5 %collective-permute-start.10 = (f32[96,128]{1,0:T(8,128)S(1)}, f32[96,128]{1,0:T(8,128)S(1)}, u32[]{:S(2)}, u32[]{:S(2)}) collective-permute-start(f32[96,128]{1,0:T(8,128)S(1)} %get-tuple-element.28), channel_id=1, source_target_pairs={{0,1},{1,2},{2,3},{3,0},{4,5},{5,6},{6,7},{7,4},{8,9},{9,10},{10,1... | collective-permute-start | bytes 147464 | tf_op jit(solution)/shard_map/ppermute | solution.py:372
  19.7 1.8 %collective-permute-start.7 = (f32[96,128]{1,0:T(8,128)S(1)}, f32[96,128]{1,0:T(8,128)S(1)}, u32[]{:S(2)}, u32[]{:S(2)}) collective-permute-start(f32[96,128]{1,0:T(8,128)S(1)} %get-tuple-element.25), channel_id=1, source_target_pairs={{16,32},{32,16},{48,64},{64,48},{80,96},{96,80},{112,128},{128,112... | collective-permute-start | bytes 147464 | tf_op jit(solution)/shard_map/ppermute | solution.py:381
  21.5 1.7 %collective-permute-start.8 = (f32[384,128]{1,0:T(8,128)S(1)}, f32[384,128]{1,0:T(8,128)S(1)}, u32[]{:S(2)}, u32[]{:S(2)}) collective-permute-start(f32[384,128]{1,0:T(8,128)S(1)} %get-tuple-element.26), channel_id=1, source_target_pairs={{0,4},{4,8},{8,12},{12,0},{1,5},{5,9},{9,13},{13,1},{2,6},{6,10},{... | collective-permute-start | bytes 589832 | tf_op jit(solution)/shard_map/ppermute | solution.py:372
  23.7 0.7 collective-permute-done.7.xhi
  24.4 3.2 %collective-permute-start.4 = (f32[9,8,128]{2,1,0:T(8,128)S(1)}, f32[9,8,128]{2,1,0:T(8,128)S(1)}, u32[]{:S(2)}, u32[]{:S(2)}) collective-permute-start(f32[9,8,128]{2,1,0:T(8,128)S(1)} %bitcast.70), channel_id=1, source_target_pairs={{0,1},{1,2},{2,3},{3,0},{4,5},{5,6},{6,7},{7,4},{8,9},{9,10},{10,1... | collective-permute-start | bytes 110600 | tf_op jit(solution)/shard_map/ppermute | solution.py:372
  27.6 1.9 %collective-permute-done.5.zhi_p = f32[9,8,128]{2,1,0:T(8,128)S(1)} collective-permute-done((f32[9,8,128]{2,1,0:T(8,128)S(1)}, f32[9,8,128]{2,1,0:T(8,128)S(1)}, u32[]{:S(2)}, u32[]{:S(2)}) %collective-permute-start.5) | collective-permute-done | bytes 36896 | tf_op jit(solution)/shard_map/ppermute | solution.py:372
  30.2 10.0 %shard_map.78 = (f32[3072,128]{1,0:T(8,128)S(1)}, f32[3072,128]{1,0:T(8,128)S(1)}, f32[96,128]{1,0:T(8,128)S(1)}, f32[96,128]{1,0:T(8,128)S(1)}, f32[384,128]{1,...) custom-call(f32[9,8,128]{2,1,0:T(8,128)S(1)} %collective-permute-done.4.zlo_p, f32[9,8,128]{2,1,0:T(8,128)S(1)} %bitcast.60, ...), custom_call_target="tpu_custom_call" | custom-call | tf_op jit(solution)/shard_map/pallas_call | solution.py:402
  40.6 1.7 %collective-permute-start.15 = (f32[384,128]{1,0:T(8,128)S(1)}, f32[384,128]{1,0:T(8,128)S(1)}, u32[]{:S(2)}, u32[]{:S(2)}) collective-permute-start(f32[384,128]{1,0:T(8,128)S(1)} %get-tuple-element.34), channel_id=1, source_target_pairs={{4,0},{8,4},{12,8},{0,12},{5,1},{9,5},{13,9},{1,13},{6,2},{10,6},{... | collective-permute-start | bytes 589832 | tf_op jit(solution)/shard_map/ppermute | solution.py:372
  42.8 1.6 %collective-permute-start.13 = (f32[96,128]{1,0:T(8,128)S(1)}, f32[96,128]{1,0:T(8,128)S(1)}, u32[]{:S(2)}, u32[]{:S(2)}) collective-permute-start(f32[96,128]{1,0:T(8,128)S(1)} %get-tuple-element.32), channel_id=1, source_target_pairs={{16,32},{32,16},{48,64},{64,48},{80,96},{96,80},{112,128},{128,112... | collective-permute-start | bytes 147464 | tf_op jit(solution)/shard_map/ppermute | solution.py:381
  44.4 2.5 %collective-permute-start.17 = (f32[96,128]{1,0:T(8,128)S(1)}, f32[96,128]{1,0:T(8,128)S(1)}, u32[]{:S(2)}, u32[]{:S(2)}) collective-permute-start(f32[96,128]{1,0:T(8,128)S(1)} %get-tuple-element.35), channel_id=1, source_target_pairs={{1,0},{2,1},{3,2},{0,3},{5,4},{6,5},{7,6},{4,7},{9,8},{10,9},{11,1... | collective-permute-start | bytes 147464 | tf_op jit(solution)/shard_map/ppermute | solution.py:372
  46.9 3.7 %collective-permute-start.16 = (f32[96,128]{1,0:T(8,128)S(1)}, f32[96,128]{1,0:T(8,128)S(1)}, u32[]{:S(2)}, u32[]{:S(2)}) collective-permute-start(f32[96,128]{1,0:T(8,128)S(1)} %get-tuple-element.35), channel_id=1, source_target_pairs={{0,1},{1,2},{2,3},{3,0},{4,5},{5,6},{6,7},{7,4},{8,9},{9,10},{10,1... | collective-permute-start | bytes 147464 | tf_op jit(solution)/shard_map/ppermute | solution.py:372
  50.6 2.1 %collective-permute-done.17.zhi = f32[96,128]{1,0:T(8,128)S(1)} collective-permute-done((f32[96,128]{1,0:T(8,128)S(1)}, f32[96,128]{1,0:T(8,128)S(1)}, u32[]{:S(2)}, u32[]{:S(2)}) %collective-permute-start.17) | collective-permute-done | bytes 49184 | tf_op jit(solution)/shard_map/ppermute | solution.py:372
  52.7 5.4 %shard_map.79 = (f32[3072,128]{1,0:T(8,128)S(1)}, f32[96,128]{1,0:T(8,128)S(1)}, f32[96,128]{1,0:T(8,128)S(1)}, f32[384,128]{1,0:T(8,128)S(1)}, f32[384,128]{1,0:T(8,128)S(1)}, /*index=5*/f32[96,128]{1,0:T(8,128)S(1)}) custom-call(f32[3072,128]{1,0:T(8,128)S(1)} %get-tuple-element.29.rows_ref, f32[3072,128]{1,0:T(8,128)S(1)} %bitcast.55, ...), custom_call_target="tpu_custom_call" | custom-call | tf_op jit(solution)/shard_map/pallas_call | solution.py:402
  58.1 2.4 %collective-permute-start.20 = (f32[384,128]{1,0:T(8,128)S(1)}, f32[384,128]{1,0:T(8,128)S(1)}, u32[]{:S(2)}, u32[]{:S(2)}) collective-permute-start(f32[384,128]{1,0:T(8,128)S(1)} %get-tuple-element.39), channel_id=1, source_target_pairs={{0,4},{4,8},{8,12},{12,0},{1,5},{5,9},{9,13},{13,1},{2,6},{6,10},{... | collective-permute-start | bytes 589832 | tf_op jit(solution)/shard_map/ppermute | solution.py:372
  61.8 3.2 %collective-permute-start.22 = (f32[96,128]{1,0:T(8,128)S(1)}, f32[96,128]{1,0:T(8,128)S(1)}, u32[]{:S(2)}, u32[]{:S(2)}) collective-permute-start(f32[96,128]{1,0:T(8,128)S(1)} %get-tuple-element.41), channel_id=1, source_target_pairs={{0,1},{1,2},{2,3},{3,0},{4,5},{5,6},{6,7},{7,4},{8,9},{9,10},{10,1... | collective-permute-start | bytes 147464 | tf_op jit(solution)/shard_map/ppermute | solution.py:372
  65.3 1.5 %collective-permute-done.23.zhi = f32[96,128]{1,0:T(8,128)S(1)} collective-permute-done((f32[96,128]{1,0:T(8,128)S(1)}, f32[96,128]{1,0:T(8,128)S(1)}, u32[]{:S(2)}, u32[]{:S(2)}) %collective-permute-start.23) | collective-permute-done | bytes 49184 | tf_op jit(solution)/shard_map/ppermute | solution.py:372
  67.4 9.1 %shard_map.80 = (f32[3072,128]{1,0:T(8,128)}, f32[28,8,128]{2,1,0:T(8,128)S(1)}) custom-call(f32[9,8,128]{2,1,0:T(8,128)S(1)} %collective-permute-done.4.zlo_p, f32[9,8,128]{2,1,0:T(8,128)S(1)} %bitcast.61, f32[9,8,128]{2,1,0:T(8,128)S(1)} %collective-permute-done.5.zhi_p, f32[3072,128]{1,0:T(8,128)S(1)} %get-tuple-element.36.rows_ref, ...), custom_call_target="tpu_custom_call" | custom-call | tf_op jit(solution)/shard_map/pallas_call | solution.py:402
  76.5 3.3 %collective-permute-start.24 = (f32[9,8,128]{2,1,0:T(8,128)S(1)}, f32[9,8,128]{2,1,0:T(8,128)S(1)}, u32[]{:S(2)}, u32[]{:S(2)}) collective-permute-start(f32[9,8,128]{2,1,0:T(8,128)S(1)} %get-tuple-element.44), channel_id=1, source_target_pairs={{0,1},{1,2},{2,3},{3,0},{4,5},{5,6},{6,7},{7,4},{8,9},{9,10},{10,1... | collective-permute-start | bytes 110600 | tf_op jit(solution)/shard_map/ppermute | solution.py:372
  79.8 1.6 %collective-permute-done.24 = f32[9,8,128]{2,1,0:T(8,128)S(1)} collective-permute-done((f32[9,8,128]{2,1,0:T(8,128)S(1)}, f32[9,8,128]{2,1,0:T(8,128)S(1)}, u32[]{:S(2)}, u32[]{:S(2)}) %collective-permute-start.24) | collective-permute-done | bytes 36896 | tf_op jit(solution)/shard_map/ppermute | solution.py:372
  81.5 3.5 %collective-permute-done.25 = f32[9,8,128]{2,1,0:T(8,128)S(1)} collective-permute-done((f32[9,8,128]{2,1,0:T(8,128)S(1)}, f32[9,8,128]{2,1,0:T(8,128)S(1)}, u32[]{:S(2)}, u32[]{:S(2)}) %collective-permute-start.25) | collective-permute-done | bytes 36896 | tf_op jit(solution)/shard_map/ppermute | solution.py:372
  85.0 3.0 %collective-permute-start.26 = (f32[3,3,8,128]{3,2,0,1:T(8,128)S(1)}, f32[3,3,8,128]{3,2,0,1:T(8,128)S(1)}, u32[]{:S(2)}, u32[]{:S(2)}) collective-permute-start(f32[3,3,8,128]{3,2,0,1:T(8,128)S(1)} %get-tuple-element.50), channel_id=1, source_target_pairs={{0,4},{4,8},{8,12},{12,0},{1,5},{5,9},{9,13},{13,1},{2,6},{6,10},{... | collective-permute-start | bytes 110600 | tf_op jit(solution)/shard_map/ppermute | solution.py:372
  88.4 1.8 %collective-permute-done.26 = f32[3,3,8,128]{3,2,0,1:T(8,128)S(1)} collective-permute-done((f32[3,3,8,128]{3,2,0,1:T(8,128)S(1)}, f32[3,3,8,128]{3,2,0,1:T(8,128)S(1)}, u32[]{:S(2)}, u32[]{:S(2)}) %collective-permute-start.26) | collective-permute-done | bytes 36896 | tf_op jit(solution)/shard_map/ppermute | solution.py:372
  90.2 3.0 %collective-permute-done.27 = f32[3,3,8,128]{3,2,0,1:T(8,128)S(1)} collective-permute-done((f32[3,3,8,128]{3,2,0,1:T(8,128)S(1)}, f32[3,3,8,128]{3,2,0,1:T(8,128)S(1)}, u32[]{:S(2)}, u32[]{:S(2)}) %collective-permute-start.27) | collective-permute-done | bytes 36896 | tf_op jit(solution)/shard_map/ppermute | solution.py:372
  93.3 1.0 %collective-permute-start.28 = (f32[9,8,128]{2,1,0:T(8,128)S(1)}, f32[9,8,128]{2,1,0:T(8,128)S(1)}, u32[]{:S(2)}, u32[]{:S(2)}) collective-permute-start(f32[9,8,128]{2,1,0:T(8,128)S(1)} %bitcast.75), channel_id=1, source_target_pairs={{0,16},{16,0},{32,48},{48,32},{64,80},{80,64},{96,112},{112,96},{1... | collective-permute-start | bytes 110600 | tf_op jit(solution)/shard_map/ppermute | solution.py:381
  94.4 3.5 %collective-permute-done.29.high_ref = f32[9,8,128]{2,1,0:T(8,128)S(1)} collective-permute-done((f32[9,8,128]{2,1,0:T(8,128)S(1)}, f32[9,8,128]{2,1,0:T(8,128)S(1)}, u32[]{:S(2)}, u32[]{:S(2)}) %collective-permute-start.29) | collective-permute-done | bytes 36896 | tf_op jit(solution)/shard_map/ppermute | solution.py:381
  97.9 1.3 %shard_map.81 = f32[3,1024]{1,0:T(4,128)} custom-call(s32[1024]{0:T(1024)S(1)} %bitcast.64, f32[9,8,128]{2,1,0:T(8,128)S(1)} %collective-permute-done.28.low_ref, f32[9,8,128]{2,1,0:T(8,128)S(1)} %bitcast.62, f32[9,8,128]{2,1,0:T(8,128)S(1)} %collective-permute-done.29.high_ref), custom_call_target="tpu_custom_call" | custom-call | tf_op jit(solution)/shard_map/pallas_call | solution.py:402
  (59 shorter events, 8.2 us)
Async XLA Ops:
  4.9 25.3 %copy-start.2 = (f32[64,16,128]{2,1,0:T(8,128)S(1)}, f32[64,16,128]{2,1,0:T(8,128)}, u32[]{:S(2)}) copy-start(f32[64,16,128]{2,1,0:T(8,128)} %param.7) | copy-start | bytes 1572868
  6.6 6.1 %collective-permute-start = (f32[9,8,128]{2,1,0:T(8,128)S(1)}, f32[9,8,128]{2,1,0:T(8,128)S(1)}, u32[]{:S(2)}, u32[]{:S(2)}) collective-permute-start(f32[9,8,128]{2,1,0:T(8,128)S(1)} %get-tuple-element.59), channel_id=1, source_target_pairs={{0,16},{16,0},{32,48},{48,32},{64,80},{80,64},{96,112},{112,96},{1... | collective-permute-start | bytes 110600 | tf_op jit(solution)/shard_map/ppermute | solution.py:381
  6.7 7.6 %collective-permute-start.1 = (f32[9,8,128]{2,1,0:T(8,128)S(1)}, f32[9,8,128]{2,1,0:T(8,128)S(1)}, u32[]{:S(2)}, u32[]{:S(2)}) collective-permute-start(f32[9,8,128]{2,1,0:T(8,128)S(1)} %get-tuple-element.60), channel_id=1, source_target_pairs={{16,32},{32,16},{48,64},{64,48},{80,96},{96,80},{112,128},{128,112... | collective-permute-start | bytes 110600 | tf_op jit(solution)/shard_map/ppermute | solution.py:381
  14.3 5.3 %collective-permute-start.2 = (f32[3,3,8,128]{3,2,0,1:T(8,128)S(1)}, f32[3,3,8,128]{3,2,0,1:T(8,128)S(1)}, u32[]{:S(2)}, u32[]{:S(2)}) collective-permute-start(f32[3,3,8,128]{3,2,0,1:T(8,128)S(1)} %get-tuple-element.56), channel_id=1, source_target_pairs={{0,4},{4,8},{8,12},{12,0},{1,5},{5,9},{9,13},{13,1},{2,6},{6,10},{... | collective-permute-start | bytes 110600 | tf_op jit(solution)/shard_map/ppermute | solution.py:372
  14.9 6.6 %collective-permute-start.3 = (f32[3,3,8,128]{3,2,0,1:T(8,128)S(1)}, f32[3,3,8,128]{3,2,0,1:T(8,128)S(1)}, u32[]{:S(2)}, u32[]{:S(2)}) collective-permute-start(f32[3,3,8,128]{3,2,0,1:T(8,128)S(1)} %get-tuple-element.57), channel_id=1, source_target_pairs={{4,0},{8,4},{12,8},{0,12},{5,1},{9,5},{13,9},{1,13},{6,2},{10,6},{... | collective-permute-start | bytes 110600 | tf_op jit(solution)/shard_map/ppermute | solution.py:372
  16.4 8.0 %collective-permute-start.11 = (f32[96,128]{1,0:T(8,128)S(1)}, f32[96,128]{1,0:T(8,128)S(1)}, u32[]{:S(2)}, u32[]{:S(2)}) collective-permute-start(f32[96,128]{1,0:T(8,128)S(1)} %get-tuple-element.28), channel_id=1, source_target_pairs={{1,0},{2,1},{3,2},{0,3},{5,4},{6,5},{7,6},{4,7},{9,8},{10,9},{11,1... | collective-permute-start | bytes 147464 | tf_op jit(solution)/shard_map/ppermute | solution.py:372
  17.2 10.5 %collective-permute-start.10 = (f32[96,128]{1,0:T(8,128)S(1)}, f32[96,128]{1,0:T(8,128)S(1)}, u32[]{:S(2)}, u32[]{:S(2)}) collective-permute-start(f32[96,128]{1,0:T(8,128)S(1)} %get-tuple-element.28), channel_id=1, source_target_pairs={{0,1},{1,2},{2,3},{3,0},{4,5},{5,6},{6,7},{7,4},{8,9},{9,10},{10,1... | collective-permute-start | bytes 147464 | tf_op jit(solution)/shard_map/ppermute | solution.py:372
  19.7 3.6 %collective-permute-start.6 = (f32[96,128]{1,0:T(8,128)S(1)}, f32[96,128]{1,0:T(8,128)S(1)}, u32[]{:S(2)}, u32[]{:S(2)}) collective-permute-start(f32[96,128]{1,0:T(8,128)S(1)} %get-tuple-element.24), channel_id=1, source_target_pairs={{0,16},{16,0},{32,48},{48,32},{64,80},{80,64},{96,112},{112,96},{1... | collective-permute-start | bytes 147464 | tf_op jit(solution)/shard_map/ppermute | solution.py:381
  19.7 4.7 %collective-permute-start.7 = (f32[96,128]{1,0:T(8,128)S(1)}, f32[96,128]{1,0:T(8,128)S(1)}, u32[]{:S(2)}, u32[]{:S(2)}) collective-permute-start(f32[96,128]{1,0:T(8,128)S(1)} %get-tuple-element.25), channel_id=1, source_target_pairs={{16,32},{32,16},{48,64},{64,48},{80,96},{96,80},{112,128},{128,112... | collective-permute-start | bytes 147464 | tf_op jit(solution)/shard_map/ppermute | solution.py:381
  21.5 8.1 %collective-permute-start.8 = (f32[384,128]{1,0:T(8,128)S(1)}, f32[384,128]{1,0:T(8,128)S(1)}, u32[]{:S(2)}, u32[]{:S(2)}) collective-permute-start(f32[384,128]{1,0:T(8,128)S(1)} %get-tuple-element.26), channel_id=1, source_target_pairs={{0,4},{4,8},{8,12},{12,0},{1,5},{5,9},{9,13},{13,1},{2,6},{6,10},{... | collective-permute-start | bytes 589832 | tf_op jit(solution)/shard_map/ppermute | solution.py:372
  23.2 7.0 %collective-permute-start.9 = (f32[384,128]{1,0:T(8,128)S(1)}, f32[384,128]{1,0:T(8,128)S(1)}, u32[]{:S(2)}, u32[]{:S(2)}) collective-permute-start(f32[384,128]{1,0:T(8,128)S(1)} %get-tuple-element.27), channel_id=1, source_target_pairs={{4,0},{8,4},{12,8},{0,12},{5,1},{9,5},{13,9},{1,13},{6,2},{10,6},{... | collective-permute-start | bytes 589832 | tf_op jit(solution)/shard_map/ppermute | solution.py:372
  24.4 5.2 %collective-permute-start.5 = (f32[9,8,128]{2,1,0:T(8,128)S(1)}, f32[9,8,128]{2,1,0:T(8,128)S(1)}, u32[]{:S(2)}, u32[]{:S(2)}) collective-permute-start(f32[9,8,128]{2,1,0:T(8,128)S(1)} %bitcast.71), channel_id=1, source_target_pairs={{1,0},{2,1},{3,2},{0,3},{5,4},{6,5},{7,6},{4,7},{9,8},{10,9},{11,1... | collective-permute-start | bytes 110600 | tf_op jit(solution)/shard_map/ppermute | solution.py:372
  24.4 5.2 %collective-permute-start.4 = (f32[9,8,128]{2,1,0:T(8,128)S(1)}, f32[9,8,128]{2,1,0:T(8,128)S(1)}, u32[]{:S(2)}, u32[]{:S(2)}) collective-permute-start(f32[9,8,128]{2,1,0:T(8,128)S(1)} %bitcast.70), channel_id=1, source_target_pairs={{0,1},{1,2},{2,3},{3,0},{4,5},{5,6},{6,7},{7,4},{8,9},{9,10},{10,1... | collective-permute-start | bytes 110600 | tf_op jit(solution)/shard_map/ppermute | solution.py:372
  40.2 12.5 %collective-permute-start.14 = (f32[384,128]{1,0:T(8,128)S(1)}, f32[384,128]{1,0:T(8,128)S(1)}, u32[]{:S(2)}, u32[]{:S(2)}) collective-permute-start(f32[384,128]{1,0:T(8,128)S(1)} %get-tuple-element.33), channel_id=1, source_target_pairs={{0,4},{4,8},{8,12},{12,0},{1,5},{5,9},{9,13},{13,1},{2,6},{6,10},{... | collective-permute-start | bytes 589832 | tf_op jit(solution)/shard_map/ppermute | solution.py:372
  40.6 12.1 %collective-permute-start.15 = (f32[384,128]{1,0:T(8,128)S(1)}, f32[384,128]{1,0:T(8,128)S(1)}, u32[]{:S(2)}, u32[]{:S(2)}) collective-permute-start(f32[384,128]{1,0:T(8,128)S(1)} %get-tuple-element.34), channel_id=1, source_target_pairs={{4,0},{8,4},{12,8},{0,12},{5,1},{9,5},{13,9},{1,13},{6,2},{10,6},{... | collective-permute-start | bytes 589832 | tf_op jit(solution)/shard_map/ppermute | solution.py:372
  42.3 4.7 %collective-permute-start.12 = (f32[96,128]{1,0:T(8,128)S(1)}, f32[96,128]{1,0:T(8,128)S(1)}, u32[]{:S(2)}, u32[]{:S(2)}) collective-permute-start(f32[96,128]{1,0:T(8,128)S(1)} %get-tuple-element.31), channel_id=1, source_target_pairs={{0,16},{16,0},{32,48},{48,32},{64,80},{80,64},{96,112},{112,96},{1... | collective-permute-start | bytes 147464 | tf_op jit(solution)/shard_map/ppermute | solution.py:381
  42.8 7.9 %collective-permute-start.13 = (f32[96,128]{1,0:T(8,128)S(1)}, f32[96,128]{1,0:T(8,128)S(1)}, u32[]{:S(2)}, u32[]{:S(2)}) collective-permute-start(f32[96,128]{1,0:T(8,128)S(1)} %get-tuple-element.32), channel_id=1, source_target_pairs={{16,32},{32,16},{48,64},{64,48},{80,96},{96,80},{112,128},{128,112... | collective-permute-start | bytes 147464 | tf_op jit(solution)/shard_map/ppermute | solution.py:381
  44.4 8.3 %collective-permute-start.17 = (f32[96,128]{1,0:T(8,128)S(1)}, f32[96,128]{1,0:T(8,128)S(1)}, u32[]{:S(2)}, u32[]{:S(2)}) collective-permute-start(f32[96,128]{1,0:T(8,128)S(1)} %get-tuple-element.35), channel_id=1, source_target_pairs={{1,0},{2,1},{3,2},{0,3},{5,4},{6,5},{7,6},{4,7},{9,8},{10,9},{11,1... | collective-permute-start | bytes 147464 | tf_op jit(solution)/shard_map/ppermute | solution.py:372
  46.9 5.7 %collective-permute-start.16 = (f32[96,128]{1,0:T(8,128)S(1)}, f32[96,128]{1,0:T(8,128)S(1)}, u32[]{:S(2)}, u32[]{:S(2)}) collective-permute-start(f32[96,128]{1,0:T(8,128)S(1)} %get-tuple-element.35), channel_id=1, source_target_pairs={{0,1},{1,2},{2,3},{3,0},{4,5},{5,6},{6,7},{7,4},{8,9},{9,10},{10,1... | collective-permute-start | bytes 147464 | tf_op jit(solution)/shard_map/ppermute | solution.py:372
  58.1 8.6 %collective-permute-start.20 = (f32[384,128]{1,0:T(8,128)S(1)}, f32[384,128]{1,0:T(8,128)S(1)}, u32[]{:S(2)}, u32[]{:S(2)}) collective-permute-start(f32[384,128]{1,0:T(8,128)S(1)} %get-tuple-element.39), channel_id=1, source_target_pairs={{0,4},{4,8},{8,12},{12,0},{1,5},{5,9},{9,13},{13,1},{2,6},{6,10},{... | collective-permute-start | bytes 589832 | tf_op jit(solution)/shard_map/ppermute | solution.py:372
  60.5 6.9 %collective-permute-start.21 = (f32[384,128]{1,0:T(8,128)S(1)}, f32[384,128]{1,0:T(8,128)S(1)}, u32[]{:S(2)}, u32[]{:S(2)}) collective-permute-start(f32[384,128]{1,0:T(8,128)S(1)} %get-tuple-element.40), channel_id=1, source_target_pairs={{4,0},{8,4},{12,8},{0,12},{5,1},{9,5},{13,9},{1,13},{6,2},{10,6},{... | collective-permute-start | bytes 589832 | tf_op jit(solution)/shard_map/ppermute | solution.py:372
  60.5 1.2 %collective-permute-start.18 = (f32[96,128]{1,0:T(8,128)S(1)}, f32[96,128]{1,0:T(8,128)S(1)}, u32[]{:S(2)}, u32[]{:S(2)}) collective-permute-start(f32[96,128]{1,0:T(8,128)S(1)} %get-tuple-element.37), channel_id=1, source_target_pairs={{0,16},{16,0},{32,48},{48,32},{64,80},{80,64},{96,112},{112,96},{1... | collective-permute-start | bytes 147464 | tf_op jit(solution)/shard_map/ppermute | solution.py:381
  60.5 4.7 %collective-permute-start.19 = (f32[96,128]{1,0:T(8,128)S(1)}, f32[96,128]{1,0:T(8,128)S(1)}, u32[]{:S(2)}, u32[]{:S(2)}) collective-permute-start(f32[96,128]{1,0:T(8,128)S(1)} %get-tuple-element.38), channel_id=1, source_target_pairs={{16,32},{32,16},{48,64},{64,48},{80,96},{96,80},{112,128},{128,112... | collective-permute-start | bytes 147464 | tf_op jit(solution)/shard_map/ppermute | solution.py:381
  61.1 5.6 %collective-permute-start.23 = (f32[96,128]{1,0:T(8,128)S(1)}, f32[96,128]{1,0:T(8,128)S(1)}, u32[]{:S(2)}, u32[]{:S(2)}) collective-permute-start(f32[96,128]{1,0:T(8,128)S(1)} %get-tuple-element.41), channel_id=1, source_target_pairs={{1,0},{2,1},{3,2},{0,3},{5,4},{6,5},{7,6},{4,7},{9,8},{10,9},{11,1... | collective-permute-start | bytes 147464 | tf_op jit(solution)/shard_map/ppermute | solution.py:372
  61.8 5.0 %collective-permute-start.22 = (f32[96,128]{1,0:T(8,128)S(1)}, f32[96,128]{1,0:T(8,128)S(1)}, u32[]{:S(2)}, u32[]{:S(2)}) collective-permute-start(f32[96,128]{1,0:T(8,128)S(1)} %get-tuple-element.41), channel_id=1, source_target_pairs={{0,1},{1,2},{2,3},{3,0},{4,5},{5,6},{6,7},{7,4},{8,9},{9,10},{10,1... | collective-permute-start | bytes 147464 | tf_op jit(solution)/shard_map/ppermute | solution.py:372
  67.4 30.5 %copy-start.6 = (s32[1024,1]{0,1:T(1,128)S(1)}, s32[1024,1]{0,1:T(1,128)}, u32[]{:S(2)}) copy-start(s32[1024,1]{0,1:T(1,128)} %param.11) | copy-start | bytes 12292
  76.5 4.9 %collective-permute-start.24 = (f32[9,8,128]{2,1,0:T(8,128)S(1)}, f32[9,8,128]{2,1,0:T(8,128)S(1)}, u32[]{:S(2)}, u32[]{:S(2)}) collective-permute-start(f32[9,8,128]{2,1,0:T(8,128)S(1)} %get-tuple-element.44), channel_id=1, source_target_pairs={{0,1},{1,2},{2,3},{3,0},{4,5},{5,6},{6,7},{7,4},{8,9},{9,10},{10,1... | collective-permute-start | bytes 110600 | tf_op jit(solution)/shard_map/ppermute | solution.py:372
  79.8 5.2 %collective-permute-start.25 = (f32[9,8,128]{2,1,0:T(8,128)S(1)}, f32[9,8,128]{2,1,0:T(8,128)S(1)}, u32[]{:S(2)}, u32[]{:S(2)}) collective-permute-start(f32[9,8,128]{2,1,0:T(8,128)S(1)} %get-tuple-element.45), channel_id=1, source_target_pairs={{1,0},{2,1},{3,2},{0,3},{5,4},{6,5},{7,6},{4,7},{9,8},{10,9},{11,1... | collective-permute-start | bytes 110600 | tf_op jit(solution)/shard_map/ppermute | solution.py:372
  85.0 5.2 %collective-permute-start.26 = (f32[3,3,8,128]{3,2,0,1:T(8,128)S(1)}, f32[3,3,8,128]{3,2,0,1:T(8,128)S(1)}, u32[]{:S(2)}, u32[]{:S(2)}) collective-permute-start(f32[3,3,8,128]{3,2,0,1:T(8,128)S(1)} %get-tuple-element.50), channel_id=1, source_target_pairs={{0,4},{4,8},{8,12},{12,0},{1,5},{5,9},{9,13},{13,1},{2,6},{6,10},{... | collective-permute-start | bytes 110600 | tf_op jit(solution)/shard_map/ppermute | solution.py:372
  88.0 5.2 %collective-permute-start.27 = (f32[3,3,8,128]{3,2,0,1:T(8,128)S(1)}, f32[3,3,8,128]{3,2,0,1:T(8,128)S(1)}, u32[]{:S(2)}, u32[]{:S(2)}) collective-permute-start(f32[3,3,8,128]{3,2,0,1:T(8,128)S(1)} %get-tuple-element.51), channel_id=1, source_target_pairs={{4,0},{8,4},{12,8},{0,12},{5,1},{9,5},{13,9},{1,13},{6,2},{10,6},{... | collective-permute-start | bytes 110600 | tf_op jit(solution)/shard_map/ppermute | solution.py:372
  93.2 4.7 %collective-permute-start.29 = (f32[9,8,128]{2,1,0:T(8,128)S(1)}, f32[9,8,128]{2,1,0:T(8,128)S(1)}, u32[]{:S(2)}, u32[]{:S(2)}) collective-permute-start(f32[9,8,128]{2,1,0:T(8,128)S(1)} %bitcast.79), channel_id=1, source_target_pairs={{16,32},{32,16},{48,64},{64,48},{80,96},{96,80},{112,128},{128,112... | collective-permute-start | bytes 110600 | tf_op jit(solution)/shard_map/ppermute | solution.py:381
  93.3 4.6 %collective-permute-start.28 = (f32[9,8,128]{2,1,0:T(8,128)S(1)}, f32[9,8,128]{2,1,0:T(8,128)S(1)}, u32[]{:S(2)}, u32[]{:S(2)}) collective-permute-start(f32[9,8,128]{2,1,0:T(8,128)S(1)} %bitcast.75), channel_id=1, source_target_pairs={{0,16},{16,0},{32,48},{48,32},{64,80},{80,64},{96,112},{112,96},{1... | collective-permute-start | bytes 110600 | tf_op jit(solution)/shard_map/ppermute | solution.py:381
  (6 other events, 29.6 us)

commit v2 on v1

--- a/solution.py
+++ b/solution.py
@@ -14,6 +14,9 @@
 RUNS = 8
 NY_DEV, NZ_DEV = 4, 4
 UNROLL = 4
+SLOT_ROWS = 9 * 8
+SPREAD_PARTS = 2
+SAMPLE_PARTS = 2
 PAD_ROWS = 32
 F32 = jnp.float32
 BF16 = jnp.bfloat16
@@ -21,10 +24,6 @@
 
 def vmem():
     return pl.BlockSpec(memory_space=pltpu.VMEM)
-
-
-def smem():
-    return pl.BlockSpec(memory_space=pltpu.SMEM)
 
 
 def shape(*dims):
@@ -59,14 +58,15 @@
             ]
 
 
-def pack_x(rows_ref, first_ref, second_ref):
+def pack_x(rows_ref, first_ref, second_ref, skip=0):
     even = is_even()
     for c in range(3):
         base = c * CI * CJ
         upper = rows_ref[base + (CI - 2) * CJ : base + CI * CJ, :]
         lower = rows_ref[base : base + 2 * CJ, :]
-        first_ref[c * 2 * CJ : (c + 1) * 2 * CJ, :] = jnp.where(even, upper, lower)
-        second_ref[c * 2 * CJ : (c + 1) * 2 * CJ, :] = jnp.where(even, lower, upper)
+        part = slice(skip + c * 2 * CJ, skip + (c + 1) * 2 * CJ)
+        first_ref[part, :] = jnp.where(even, upper, lower)
+        second_ref[part, :] = jnp.where(even, lower, upper)
 
 
 def z_masks():
@@ -95,10 +95,24 @@
 
 
 def pack_kernel(
-    tile_ref, force_ref, offset_ref, cell_ref, rows_ref,
-    points_ref, xf_ref, xb_ref, yf_ref, yb_ref, zp_ref,
+    tile_any, force_any, offset_any, cell_any, rows_any,
+    mid_ref, code_ref, xa_ref, xb_ref, yf_ref, yb_ref, zp_ref,
+    points_ref, tile_ref, force_ref, offset_ref, cell_ref, rows_ref, sems,
 ):
+    moves = [
+        pltpu.make_async_copy(source, target, sems.at[n])
+        for n, (source, target) in enumerate(
+            (
+                (tile_any, tile_ref), (force_any, force_ref), (offset_any, offset_ref),
+                (cell_any, cell_ref), (rows_any, rows_ref),
+            )
+        )
+    ]
+    for move in moves:
+        move.start()
     points_ref[...] = jnp.zeros_like(points_ref)
+    for move in moves[:4]:
+        move.wait()
     for run in range(RUNS):
         code = run_code(tile_ref, run)
         lanes = slice(run * CAP, (run + 1) * CAP)
@@ -112,8 +126,13 @@
             axis=0,
         )
         points_ref[code] = block
+        code_ref[run : run + 1, :] = jnp.full((1, CAP), code, jnp.int32)
+    for group, ref in enumerate((xa_ref, mid_ref, xb_ref)):
+        for t in range(9):
+            ref[t * 8 : (t + 1) * 8, :] = points_ref[group * 9 + t]
+    moves[4].wait()
     pack_y(rows_ref, yf_ref, yb_ref)
-    pack_x(rows_ref, xf_ref, xb_ref)
+    pack_x(rows_ref, xa_ref, xb_ref, SLOT_ROWS)
     pack_z(rows_ref, zp_ref)
 
 
@@ -142,7 +161,7 @@
     for group, ref in enumerate((zlo_ref, zmid_ref, zhi_ref)):
         for t in range(9):
             s = group * 9 + t
-            value = ref[t]
+            value = ref[t * 8 : (t + 1) * 8, :]
             slots[s] = value
             filled = filled + jnp.where(value[7:8, :] > 0.5, 1 << s, 0)
     slots[27] = jnp.zeros((8, CAP), F32)
@@ -163,20 +182,62 @@
 NN = (((1,), (0,)), ((), ()))
 
 
-def spread(slots, order, count, acc):
-    acc[...] = jnp.zeros_like(acc)
+def spread(slots, order, count, plane, forcing_ref):
+    forcing_ref[...] = jnp.zeros_like(forcing_ref)
+    width = 2 * CAP
 
     def one_pair(pair, carry):
         block = pair_block(slots, order, pair)
         wx, wy, wz = point_weights(block)
-        ah, al = halves(jnp.concatenate([block[c : c + 1, :] * wx for c in range(3)], axis=0))
-        for j in range(0, CJ, 2):
-            plane = jnp.concatenate([wz * wy[j : j + 1, :], wz * wy[j + 1 : j + 2, :]], axis=0)
-            bh, bl = halves(plane)
-            total = lax.dot_general(ah, bh, NT, preferred_element_type=F32)
-            total = total + lax.dot_general(ah, bl, NT, preferred_element_type=F32)
-            total = total + lax.dot_general(al, bh, NT, preferred_element_type=F32)
-            acc[:, j * CK : (j + 2) * CK] += total
+        for i in range(CI):
+            high, low = halves(wx[i : i + 1, :] * wy)
+            plane[i * CJ : (i + 1) * CJ, :width] = high
+            plane[i * CJ : (i + 1) * CJ, width:] = low
+        parts = [halves(block[c : c + 1, :] * wz) for c in range(3)]
+        both_high = jnp.concatenate([parts[0][0], parts[1][0]], axis=0)
+        both_low = jnp.concatenate([parts[0][1], parts[1][1]], axis=0)
+        third = jnp.concatenate(parts[2], axis=0)
+
+        def dot(a, b):
+            return lax.dot_general(a, b, NT, preferred_element_type=F32)
+
+        step = CI * CJ // SPREAD_PARTS
+        for m in range(0, CI * CJ, step):
+            high, low = plane[m : m + step, :width], plane[m : m + step, width:]
+            pairs = dot(high, both_high) + dot(low, both_high) + dot(high, both_low)
+            last = dot(high, third) + dot(low, third)
+            for c in range(2):
+                first = c * CI * CJ + m
+                forcing_ref[first : first + step, :] += pairs[:, c * CK : (c + 1) * CK]
+            first = 2 * CI * CJ + m
+            forcing_ref[first : first + step, :] += last[:, :CK] + last[:, CK:]
+        return carry
+
+    lax.fori_loop(0, (count + 1) // 2, one_pair, 0)
+
+
+def sample(slots, order, count, field, sampled_ref):
+    def one_pair(pair, carry):
+        block = pair_block(slots, order, pair)
+        wx, wy, wz = point_weights(block)
+        high, low = halves(wz)
+        high = jnp.concatenate([high, high], axis=0)
+        step = CI * CJ // SAMPLE_PARTS
+        sums = [jnp.zeros((CJ, 2 * CAP), F32)] * 3
+        for m in range(0, CI * CJ, step):
+            for c in range(3):
+                part = slice(c * CI * CJ + m, c * CI * CJ + m + step)
+                along = lax.dot_general(field[part, :], high, NN, preferred_element_type=F32)
+                along = along + lax.dot_general(
+                    field[part, :CK], low, NN, preferred_element_type=F32
+                )
+                for t in range(step // CJ):
+                    i = m // CJ + t
+                    sums[c] = sums[c] + along[t * CJ : (t + 1) * CJ, :] * wx[i : i + 1, :]
+        rows = [jnp.sum(sums[c] * wy, axis=0, keepdims=True) for c in range(3)]
+        result = jnp.concatenate(rows + [jnp.zeros((5, 2 * CAP), F32)], axis=0)
+        sampled_ref[order[2 * pair]] = result[:, :CAP]
+        sampled_ref[order[2 * pair + 1]] = result[:, CAP:]
         return carry
 
     lax.fori_loop(0, (count + 1) // 2, one_pair, 0)
@@ -192,14 +253,16 @@
     )
 
 
-def stage(alpha, beta, rows_ref, base_ref, visc_ref, forcing_ref, halos, padded, zsc, out_ref):
+def stage(
+    alpha, beta, rows_ref, base_ref, visc_ref, forcing_ref, halos, padded, zsc, out_ref, skip=0
+):
     xa, xb, ylo, yhi, zlo, zhi = halos
     even = is_even()
     (x0, x1), (y0, y1), (z0, z1) = edge_flags()
     step_rows = (CI + 4) * PAD_ROWS
     for c in range(3):
         for r in range(2):
-            part = slice((c * 2 + r) * CJ, (c * 2 + r + 1) * CJ)
+            part = slice(skip + (c * 2 + r) * CJ, skip + (c * 2 + r + 1) * CJ)
             lower = jnp.where(even, xb[part, :], xa[part, :])
             upper = jnp.where(even, xa[part, :], xb[part, :])
             for n, (value, ok) in enumerate(((lower, x0), (upper, x1))):
@@ -214,8 +277,8 @@
     lane = z_masks()
     low_part = lane % 4 < 2
     for b in range(6):
-        part = slice(b * CJ, (b + 1) * CJ)
-        zsc[part, :] = jnp.where(
+        part = slice(skip + b * CJ, skip + (b + 1) * CJ)
+        zsc[b * CJ : (b + 1) * CJ, :] = jnp.where(
             low_part, jnp.where(z0, zlo[part, :], 0.0), jnp.where(z1, zhi[part, :], 0.0)
         )
 
@@ -275,18 +338,15 @@
 
 
 def first_kernel(
-    zlo_p, zmid_p, zhi_p, rows_ref, visc_ref, xlo, xhi, ylo, yhi, zlo, zhi,
+    zlo, zmid, zhi, rows_ref, visc_ref, xlo, xhi, ylo, yhi,
     out_ref, forcing_ref, xf_ref, xb_ref, yf_ref, yb_ref, zp_ref,
-    slots, order, acc, padded, zsc,
+    slots, order, plane, padded, zsc,
 ):
-    count = gather_slots(zlo_p, zmid_p, zhi_p, slots, order)
-    spread(slots, order, count, acc)
-    for s in range(0, NS, 8):
-        for j in range(CJ):
-            forcing_ref[pl.ds(s * CJ + j, 8, stride=CJ), :] = acc[s : s + 8, j * CK : (j + 1) * CK]
+    count = gather_slots(zlo, zmid, zhi, slots, order)
+    spread(slots, order, count, plane, forcing_ref)
     stage(
         0.0, 1.0, rows_ref, rows_ref, visc_ref, forcing_ref,
-        (xlo, xhi, ylo, yhi, zlo, zhi), padded, zsc, out_ref,
+        (xlo, xhi, ylo, yhi, zlo, zhi), padded, zsc, out_ref, SLOT_ROWS,
     )
     pack_y(out_ref, yf_ref, yb_ref)
     pack_x(out_ref, xf_ref, xb_ref)
@@ -308,61 +368,35 @@
 
 def third_kernel(
     zlo_p, zmid_p, zhi_p, rows_ref, base_ref, visc_ref, forcing_ref, xlo, xhi, ylo, yhi, zlo, zhi,
-    out_ref, sampled_ref, slots, order, padded, zsc, field_high, field_low,
+    out_ref, sampled_ref, slots, order, padded, zsc, field,
 ):
     stage(
         1.0 / 3.0, 2.0 / 3.0, rows_ref, base_ref, visc_ref, forcing_ref,
         (xlo, xhi, ylo, yhi, zlo, zhi), padded, zsc, out_ref,
     )
-    for j in range(CJ):
-        for s in range(0, NS, 16):
-            value = jnp.concatenate(
-                [
-                    out_ref[pl.ds(s * CJ + j, 8, stride=CJ), :],
-                    out_ref[pl.ds((s + 8) * CJ + j, 8, stride=CJ), :],
-                ],
-                axis=0,
-            )
-            high, low = halves(value)
-            field_high[s : s + 16, j * CK : (j + 1) * CK] = high
-            field_low[s : s + 16, j * CK : (j + 1) * CK] = low
+    def split(t, carry):
+        first = pl.multiple_of(t * 256, 256)
+        high, low = halves(out_ref[pl.ds(first, 256), :])
+        field[pl.ds(first, 256), :CK] = high
+        field[pl.ds(first, 256), CK:] = low
+        return carry
+
+    lax.fori_loop(0, NS * CJ // 256, split, 0)
     count = gather_slots(zlo_p, zmid_p, zhi_p, slots, order)
     sampled_ref[...] = jnp.zeros_like(sampled_ref)
-
-    def one_pair(pair, carry):
-        block = pair_block(slots, order, pair)
-        wx, wy, wz = point_weights(block)
-        total = jnp.zeros((NS, 2 * CAP), F32)
-        for j in range(0, CJ, 2):
-            plane = jnp.concatenate([wz * wy[j : j + 1, :], wz * wy[j + 1 : j + 2, :]], axis=0)
-            bh, bl = halves(plane)
-            vh = field_high[:, j * CK : (j + 2) * CK]
-            vl = field_low[:, j * CK : (j + 2) * CK]
-            total = total + lax.dot_general(vh, bh, NN, preferred_element_type=F32)
-            total = total + lax.dot_general(vh, bl, NN, preferred_element_type=F32)
-            total = total + lax.dot_general(vl, bh, NN, preferred_element_type=F32)
-        result = jnp.concatenate(
-            [
-                jnp.sum(total[c * CI : (c + 1) * CI, :] * wx, axis=0, keepdims=True)
-                for c in range(3)
-            ]
-            + [jnp.zeros((5, 2 * CAP), F32)],
-            axis=0,
-        )
-        sampled_ref[order[2 * pair]] = result[:, :CAP]
-        sampled_ref[order[2 * pair + 1]] = result[:, CAP:]
-        return carry
-
-    lax.fori_loop(0, (count + 1) // 2, one_pair, 0)
-
-
-def pick_kernel(tile_ref, low_ref, mid_ref, high_ref, out_ref, slots):
-    slots[0:9] = low_ref[...]
-    slots[9:18] = mid_ref[...]
-    slots[18:27] = high_ref[...]
+    sample(slots, order, count, field, sampled_ref)
+
+
+def pick_kernel(code_ref, low_ref, mid_ref, high_ref, out_ref):
+    picked = [jnp.zeros((3, CAP), F32)] * RUNS
+    for group, ref in enumerate((low_ref, mid_ref, high_ref)):
+        for t in range(9):
+            value = ref[t][:3, :]
+            for run in range(RUNS):
+                mine = code_ref[run : run + 1, :] == group * 9 + t
+                picked[run] = jnp.where(mine, value, picked[run])
     for run in range(RUNS):
-        code = run_code(tile_ref, run)
-        out_ref[:, run * CAP : (run + 1) * CAP] = slots[code, 0:3, :]
+        out_ref[:, run * CAP : (run + 1) * CAP] = picked[run]
 
 
 def exchanged(forward, backward, axis):
@@ -398,11 +432,13 @@
 SLOT_SCRATCH = [pltpu.VMEM((28, 8, CAP), F32), pltpu.SMEM((32,), jnp.int32)]
 
 
-def call(kernel, outs, scratch, *args, scalars=0):
+def call(kernel, outs, scratch, *args, in_place=False):
+    if in_place:
+        args = [pltpu.with_memory_space_constraint(a, pltpu.HBM) for a in args]
     return pl.pallas_call(
         kernel,
         out_shape=outs,
-        in_specs=[smem()] * scalars + [vmem()] * (len(args) - scalars),
+        in_specs=[pl.BlockSpec(memory_space=pltpu.HBM) if in_place else vmem()] * len(args),
         out_specs=jax.tree.map(lambda _: vmem(), outs),
         scratch_shapes=scratch,
         compiler_params=params(),
@@ -415,26 +451,43 @@
     visc = viscosity.reshape(CI * CJ, CK)
     cells = point_cell.reshape(RUNS, CAP)
 
-    points, *faces = call(
-        pack_kernel, (shape(27, 8, CAP),) + FACES, [],
-        tiles, point_force, point_offset, cells, rows, scalars=1,
-    )
-
-    halos = halos_of(*faces)
-    from_first, from_second = swapped(points[:9], points[18:], "gx")
-    held = jnp.stack([from_first, points[9:18], from_second]).reshape(3, 3, 3, 8, CAP)
+    message = shape(SLOT_ROWS + 6 * CJ, CK)
+    mid, codes, xa, xb, yf, yb, zp = call(
+        pack_kernel,
+        (shape(SLOT_ROWS, CAP), jax.ShapeDtypeStruct((RUNS, CAP), jnp.int32), message, message)
+        + FACES[2:],
+        [
+            pltpu.VMEM((27, 8, CAP), F32),
+            pltpu.SMEM((RUNS * CAP,), jnp.int32),
+            pltpu.VMEM((3, RUNS * CAP), F32),
+            pltpu.VMEM((3, RUNS * CAP), F32),
+            pltpu.VMEM((RUNS, CAP), jnp.int32),
+            pltpu.VMEM((NS * CJ, CK), F32),
+            pltpu.SemaphoreType.DMA((5,)),
+        ],
+        tiles, point_force, point_offset, cells, rows, in_place=True,
+    )
+
+    def slots_of(received):
+        return received[:SLOT_ROWS]
+
+    xa, xb = swapped(xa, xb, "gx")
+    ylo, yhi = exchanged(yf, yb, "gy")
+    held = jnp.stack([slots_of(xa), mid, slots_of(xb)]).reshape(3, 3, 3, 8, CAP)
     from_low, from_high = exchanged(held[:, 2], held[:, 0], "gy")
     held = jnp.stack([from_low, held[:, 1], from_high])
-    mine = held[:, :, 1].reshape(9, 8, CAP)
-    from_low, from_high = exchanged(
-        held[:, :, 2].reshape(9, 8, CAP), held[:, :, 0].reshape(9, 8, CAP), "gz"
-    )
-    arrived = (from_low, mine, from_high)
+    mine = held[:, :, 1].reshape(SLOT_ROWS, CAP)
+    zlo, zhi = exchanged(
+        jnp.concatenate([held[:, :, 2].reshape(SLOT_ROWS, CAP), zp]),
+        jnp.concatenate([held[:, :, 0].reshape(SLOT_ROWS, CAP), zp]),
+        "gz",
+    )
+    arrived = (zlo, mine, zhi)
 
     section_one, forcing, *faces = call(
         first_kernel, (shape(NS * CJ, CK), shape(NS * CJ, CK)) + FACES,
-        SLOT_SCRATCH + [pltpu.VMEM((NS, CJ * CK), F32)] + STENCIL_SCRATCH,
-        *arrived, rows, visc, *halos,
+        SLOT_SCRATCH + [pltpu.VMEM((CI * CJ, 4 * CAP), BF16)] + STENCIL_SCRATCH,
+        *arrived, rows, visc, xa, xb, ylo, yhi,
     )
     section_two, *faces = call(
         second_kernel, (shape(NS * CJ, CK),) + FACES, STENCIL_SCRATCH,
@@ -442,7 +495,7 @@
     )
     fresh, sampled = call(
         third_kernel, (shape(NS * CJ, CK), shape(28, 8, CAP)),
-        SLOT_SCRATCH + STENCIL_SCRATCH + [pltpu.VMEM((NS, CJ * CK), BF16)] * 2,
+        SLOT_SCRATCH + STENCIL_SCRATCH + [pltpu.VMEM((NS * CJ, 2 * CK), BF16)],
         *arrived, section_two, rows, visc, forcing, *halos_of(*faces),
     )
 
@@ -456,8 +509,8 @@
         held[:, :, 0].reshape(9, 8, CAP), held[:, :, 2].reshape(9, 8, CAP), "gx"
     )
     point_velocity = call(
-        pick_kernel, shape(3, RUNS * CAP), [pltpu.VMEM((27, 8, CAP), F32)],
-        tiles, from_first, mine, from_second, scalars=1,
+        pick_kernel, shape(3, RUNS * CAP), [],
+        codes, from_first, mine, from_second,
     )
     return fresh.reshape(velocity.shape), point_velocity
 

time: 98.5 us -> 89.1 us (0.905)
  local copies, waits for them, and re-layouts: 4.28 us -> 0.06 us
  starting transfers between devices: 43.6 us -> 39.6 us
  Pallas kernels: 27.6 us -> 24.8 us
    unnamed x16 -> x4, local copies, waits for them, and re-layouts: 4.22 us -> 0.01 us
    ppermute x20 -> x18, starting transfers between devices: 31.9 us -> 28 us  [exchanged(): return (lax.ppermute(forward, axis, up), lax.ppermute(backward, axis, down))]
    pallas_call x5, Pallas kernels: 27.6 us -> 24.8 us  [call(): pl.pallas_call(kernel, out_shape=outs, in_specs=[pl.BlockSpec(memory_spac...]
    ppermute x5 -> x4, starting transfers between devices: 10.1 us -> 10.6 us  [swapped(): lax.ppermute(second, axis, pairs[1])]
    ppermute x20 -> x18, waiting for transfers between devices: 16.7 us -> 17.1 us  [exchanged(): return (lax.ppermute(forward, axis, up), lax.ppermute(backward, axis, down))]
    ppermute x5 -> x4, waiting for transfers between devices: 6.2 us -> 6.51 us  [swapped(): lax.ppermute(second, axis, pairs[1])]
  transfers between devices with their start and end apart: 30 -> 26, of which waited for: 13 -> 15; matrix products, arithmetic and copies ran while one was open for 0% -> 0% of each run, Pallas kernels for 0% -> 0%
where the time goes in v2:
time: 89.1 us; the launch traced here: 88.9 us
  starting transfers between devices  39.6 us (44%)
  Pallas kernels  24.8 us (28%)
  waiting for transfers between devices  23.6 us (26%)
    ppermute x18, starting transfers between devices, exchanged(): return (lax.ppermute(forward, axis, up), lax.ppermute(backward, axis, down))  28 us
    pallas_call x5, Pallas kernels, call(): pl.pallas_call(kernel, out_shape=outs, in_specs=[pl.BlockSpec(memory_spac...  24.8 us
    ppermute x18, waiting for transfers between devices, exchanged(): return (lax.ppermute(forward, axis, up), lax.ppermute(backward, axis, down))  17.1 us
    ppermute x4, starting transfers between devices, swapped(): lax.ppermute(second, axis, pairs[1])  10.6 us
    ppermute x4, waiting for transfers between devices, swapped(): lax.ppermute(second, axis, pairs[1])  6.51 us
  transfers between devices with their start and end apart: 26, of which 15 were waited for; matrix products, arithmetic and copies ran while one was open for 0% of the time, Pallas kernels for 0%

profile of v2, /device:TPU:30, one launch (start us, length us, event | category | flops | bytes accessed | tf_op | source)
XLA Modules:
  0.0 88.9 jit_solution(7151095913355518473)
XLA Ops:
  0.7 2.7 %shard_map.77 = (f32[72,128]{1,0:T(8,128)S(1)}, s32[8,128]{1,0:T(8,128)S(1)}, f32[168,128]{1,0:T(8,128)S(1)}, f32[168,128]{1,0:T(8,128)S(1)}, f32[384,128]{1,0:T...) custom-call(s32[1024]{0:T(1024)} %bitcast.77, f32[3,1024]{1,0:T(4,128)} %force_any.1, f32[3,1024]{1,0:T(4,128)} %offset_any.1, ...), custom_call_target="tpu_custom_call" | custom-call | tf_op jit(solution)/shard_map/pallas_call | solution.py:438
  3.5 6.0 %collective-permute-start.1 = (f32[168,128]{1,0:T(8,128)S(1)}, f32[168,128]{1,0:T(8,128)S(1)}, u32[]{:S(2)}, u32[]{:S(2)}) collective-permute-start(f32[168,128]{1,0:T(8,128)S(1)} %get-tuple-element.26), channel_id=1, source_target_pairs={{16,32},{32,16},{48,64},{64,48},{80,96},{96,80},{112,128},{128,112... | collective-permute-start | bytes 258056 | tf_op jit(solution)/shard_map/ppermute | solution.py:415
  9.5 2.2 %collective-permute-done.1.xhi = f32[168,128]{1,0:T(8,128)S(1)} collective-permute-done((f32[168,128]{1,0:T(8,128)S(1)}, f32[168,128]{1,0:T(8,128)S(1)}, u32[]{:S(2)}, u32[]{:S(2)}) %collective-permute-start.1) | collective-permute-done | bytes 86048 | tf_op jit(solution)/shard_map/ppermute | solution.py:415
  12.2 1.5 %collective-permute-start.3 = (f32[3,3,8,128]{3,2,0,1:T(8,128)S(1)}, f32[3,3,8,128]{3,2,0,1:T(8,128)S(1)}, u32[]{:S(2)}, u32[]{:S(2)}) collective-permute-start(f32[3,3,8,128]{3,2,0,1:T(8,128)S(1)} %get-tuple-element.59), channel_id=1, source_target_pairs={{4,0},{8,4},{12,8},{0,12},{5,1},{9,5},{13,9},{1,13},{6,2},{10,6},{... | collective-permute-start | bytes 110600 | tf_op jit(solution)/shard_map/ppermute | solution.py:406
  13.8 1.7 %collective-permute-start.6 = (f32[384,128]{1,0:T(8,128)S(1)}, f32[384,128]{1,0:T(8,128)S(1)}, u32[]{:S(2)}, u32[]{:S(2)}) collective-permute-start(f32[384,128]{1,0:T(8,128)S(1)} %get-tuple-element.28), channel_id=1, source_target_pairs={{0,4},{4,8},{8,12},{12,0},{1,5},{5,9},{9,13},{13,1},{2,6},{6,10},{... | collective-permute-start | bytes 589832 | tf_op jit(solution)/shard_map/ppermute | solution.py:406
  15.8 1.6 %collective-permute-done.3 = f32[3,3,8,128]{3,2,0,1:T(8,128)S(1)} collective-permute-done((f32[3,3,8,128]{3,2,0,1:T(8,128)S(1)}, f32[3,3,8,128]{3,2,0,1:T(8,128)S(1)}, u32[]{:S(2)}, u32[]{:S(2)}) %collective-permute-start.3) | collective-permute-done | bytes 36896 | tf_op jit(solution)/shard_map/ppermute | solution.py:406
  17.4 0.8 collective-permute-start.5
  18.2 2.5 %collective-permute-start.4 = (f32[168,128]{1,0:T(8,128)S(1)}, f32[168,128]{1,0:T(8,128)S(1)}, u32[]{:S(2)}, u32[]{:S(2)}) collective-permute-start(f32[168,128]{1,0:T(8,128)S(1)} %get-tuple-element.62), channel_id=1, source_target_pairs={{0,1},{1,2},{2,3},{3,0},{4,5},{5,6},{6,7},{7,4},{8,9},{9,10},{10,1... | collective-permute-start | bytes 258056 | tf_op jit(solution)/shard_map/ppermute | solution.py:406
  20.7 1.6 %collective-permute-done.7.yhi = f32[384,128]{1,0:T(8,128)S(1)} collective-permute-done((f32[384,128]{1,0:T(8,128)S(1)}, f32[384,128]{1,0:T(8,128)S(1)}, u32[]{:S(2)}, u32[]{:S(2)}) %collective-permute-start.7) | collective-permute-done | bytes 196640 | tf_op jit(solution)/shard_map/ppermute | solution.py:406
  22.3 0.9 collective-permute-done.5.zhi.zhi_p
  23.2 7.7 %shard_map.78 = (f32[3072,128]{1,0:T(8,128)S(1)}, f32[3072,128]{1,0:T(8,128)S(1)}, f32[96,128]{1,0:T(8,128)S(1)}, f32[96,128]{1,0:T(8,128)S(1)}, f32[384,128]{1,...) custom-call(f32[168,128]{1,0:T(8,128)S(1)} %collective-permute-done.4.zlo.zlo_p, f32[72,128]{1,0:T(8,128)S(1)} %bitcast.60, ...), custom_call_target="tpu_custom_call" | custom-call | tf_op jit(solution)/shard_map/pallas_call | solution.py:438
  30.9 2.4 %collective-permute-start.10 = (f32[384,128]{1,0:T(8,128)S(1)}, f32[384,128]{1,0:T(8,128)S(1)}, u32[]{:S(2)}, u32[]{:S(2)}) collective-permute-start(f32[384,128]{1,0:T(8,128)S(1)} %get-tuple-element.34), channel_id=1, source_target_pairs={{0,4},{4,8},{8,12},{12,0},{1,5},{5,9},{9,13},{13,1},{2,6},{6,10},{... | collective-permute-start | bytes 589832 | tf_op jit(solution)/shard_map/ppermute | solution.py:406
  33.4 4.5 %collective-permute-start.9 = (f32[96,128]{1,0:T(8,128)S(1)}, f32[96,128]{1,0:T(8,128)S(1)}, u32[]{:S(2)}, u32[]{:S(2)}) collective-permute-start(f32[96,128]{1,0:T(8,128)S(1)} %get-tuple-element.33), channel_id=1, source_target_pairs={{16,32},{32,16},{48,64},{64,48},{80,96},{96,80},{112,128},{128,112... | collective-permute-start | bytes 147464 | tf_op jit(solution)/shard_map/ppermute | solution.py:415
  37.9 1.7 %collective-permute-start.13 = (f32[96,128]{1,0:T(8,128)S(1)}, f32[96,128]{1,0:T(8,128)S(1)}, u32[]{:S(2)}, u32[]{:S(2)}) collective-permute-start(f32[96,128]{1,0:T(8,128)S(1)} %get-tuple-element.36), channel_id=1, source_target_pairs={{1,0},{2,1},{3,2},{0,3},{5,4},{6,5},{7,6},{4,7},{9,8},{10,9},{11,1... | collective-permute-start | bytes 147464 | tf_op jit(solution)/shard_map/ppermute | solution.py:406
  39.6 1.5 %collective-permute-start.12 = (f32[96,128]{1,0:T(8,128)S(1)}, f32[96,128]{1,0:T(8,128)S(1)}, u32[]{:S(2)}, u32[]{:S(2)}) collective-permute-start(f32[96,128]{1,0:T(8,128)S(1)} %get-tuple-element.36), channel_id=1, source_target_pairs={{0,1},{1,2},{2,3},{3,0},{4,5},{5,6},{6,7},{7,4},{8,9},{9,10},{10,1... | collective-permute-start | bytes 147464 | tf_op jit(solution)/shard_map/ppermute | solution.py:406
  41.1 2.1 %collective-permute-done.13.zhi = f32[96,128]{1,0:T(8,128)S(1)} collective-permute-done((f32[96,128]{1,0:T(8,128)S(1)}, f32[96,128]{1,0:T(8,128)S(1)}, u32[]{:S(2)}, u32[]{:S(2)}) %collective-permute-start.13) | collective-permute-done | bytes 49184 | tf_op jit(solution)/shard_map/ppermute | solution.py:406
  43.7 5.4 %shard_map.79 = (f32[3072,128]{1,0:T(8,128)S(1)}, f32[96,128]{1,0:T(8,128)S(1)}, f32[96,128]{1,0:T(8,128)S(1)}, f32[384,128]{1,0:T(8,128)S(1)}, f32[384,128]{1,0:T(8,128)S(1)}, /*index=5*/f32[96,128]{1,0:T(8,128)S(1)}) custom-call(f32[3072,128]{1,0:T(8,128)S(1)} %get-tuple-element.30.rows_ref, f32[3072,128]{1,0:T(8,128)S(1)} %bitcast.55, ...), custom_call_target="tpu_custom_call" | custom-call | tf_op jit(solution)/shard_map/pallas_call | solution.py:438
  49.2 1.5 %collective-permute-start.16 = (f32[384,128]{1,0:T(8,128)S(1)}, f32[384,128]{1,0:T(8,128)S(1)}, u32[]{:S(2)}, u32[]{:S(2)}) collective-permute-start(f32[384,128]{1,0:T(8,128)S(1)} %get-tuple-element.40), channel_id=1, source_target_pairs={{0,4},{4,8},{8,12},{12,0},{1,5},{5,9},{9,13},{13,1},{2,6},{6,10},{... | collective-permute-start | bytes 589832 | tf_op jit(solution)/shard_map/ppermute | solution.py:406
  51.3 1.7 %collective-permute-start.19 = (f32[96,128]{1,0:T(8,128)S(1)}, f32[96,128]{1,0:T(8,128)S(1)}, u32[]{:S(2)}, u32[]{:S(2)}) collective-permute-start(f32[96,128]{1,0:T(8,128)S(1)} %get-tuple-element.42), channel_id=1, source_target_pairs={{1,0},{2,1},{3,2},{0,3},{5,4},{6,5},{7,6},{4,7},{9,8},{10,9},{11,1... | collective-permute-start | bytes 147464 | tf_op jit(solution)/shard_map/ppermute | solution.py:406
  53.0 2.2 %collective-permute-start.18 = (f32[96,128]{1,0:T(8,128)S(1)}, f32[96,128]{1,0:T(8,128)S(1)}, u32[]{:S(2)}, u32[]{:S(2)}) collective-permute-start(f32[96,128]{1,0:T(8,128)S(1)} %get-tuple-element.42), channel_id=1, source_target_pairs={{0,1},{1,2},{2,3},{3,0},{4,5},{5,6},{6,7},{7,4},{8,9},{9,10},{10,1... | collective-permute-start | bytes 147464 | tf_op jit(solution)/shard_map/ppermute | solution.py:406
  55.2 0.8 collective-permute-done.15.xhi
  57.5 8.2 %shard_map.80 = (f32[3072,128]{1,0:T(8,128)}, f32[28,8,128]{2,1,0:T(8,128)S(1)}) custom-call(f32[168,128]{1,0:T(8,128)S(1)} %collective-permute-done.4.zlo.zlo_p, f32[72,128]{1,0:T(8,128)S(1)} %bitcast.61, f32[168,128]{1,0:T(8,128)S(1)} %collective-permute-done.5.zhi.zhi_p, f32[3072,128]{1,0:T(8,128)S(1)} %get-tuple-element.37.rows_ref, ...), custom_call_target="tpu_custom_call" | custom-call | tf_op jit(solution)/shard_map/pallas_call | solution.py:438
  65.7 3.3 %collective-permute-start.20 = (f32[9,8,128]{2,1,0:T(8,128)S(1)}, f32[9,8,128]{2,1,0:T(8,128)S(1)}, u32[]{:S(2)}, u32[]{:S(2)}) collective-permute-start(f32[9,8,128]{2,1,0:T(8,128)S(1)} %get-tuple-element.46), channel_id=1, source_target_pairs={{0,1},{1,2},{2,3},{3,0},{4,5},{5,6},{6,7},{7,4},{8,9},{9,10},{10,1... | collective-permute-start | bytes 110600 | tf_op jit(solution)/shard_map/ppermute | solution.py:406
  69.0 1.4 %collective-permute-start.21 = (f32[9,8,128]{2,1,0:T(8,128)S(1)}, f32[9,8,128]{2,1,0:T(8,128)S(1)}, u32[]{:S(2)}, u32[]{:S(2)}) collective-permute-start(f32[9,8,128]{2,1,0:T(8,128)S(1)} %get-tuple-element.47), channel_id=1, source_target_pairs={{1,0},{2,1},{3,2},{0,3},{5,4},{6,5},{7,6},{4,7},{9,8},{10,9},{11,1... | collective-permute-start | bytes 110600 | tf_op jit(solution)/shard_map/ppermute | solution.py:406
  70.5 1.8 %collective-permute-done.20 = f32[9,8,128]{2,1,0:T(8,128)S(1)} collective-permute-done((f32[9,8,128]{2,1,0:T(8,128)S(1)}, f32[9,8,128]{2,1,0:T(8,128)S(1)}, u32[]{:S(2)}, u32[]{:S(2)}) %collective-permute-start.20) | collective-permute-done | bytes 36896 | tf_op jit(solution)/shard_map/ppermute | solution.py:406
  72.3 1.9 %collective-permute-done.21 = f32[9,8,128]{2,1,0:T(8,128)S(1)} collective-permute-done((f32[9,8,128]{2,1,0:T(8,128)S(1)}, f32[9,8,128]{2,1,0:T(8,128)S(1)}, u32[]{:S(2)}, u32[]{:S(2)}) %collective-permute-start.21) | collective-permute-done | bytes 36896 | tf_op jit(solution)/shard_map/ppermute | solution.py:406
  74.2 4.0 %collective-permute-start.22 = (f32[3,3,8,128]{3,2,0,1:T(8,128)S(1)}, f32[3,3,8,128]{3,2,0,1:T(8,128)S(1)}, u32[]{:S(2)}, u32[]{:S(2)}) collective-permute-start(f32[3,3,8,128]{3,2,0,1:T(8,128)S(1)} %get-tuple-element.52), channel_id=1, source_target_pairs={{0,4},{4,8},{8,12},{12,0},{1,5},{5,9},{9,13},{13,1},{2,6},{6,10},{... | collective-permute-start | bytes 110600 | tf_op jit(solution)/shard_map/ppermute | solution.py:406
  78.2 1.6 %collective-permute-done.22 = f32[3,3,8,128]{3,2,0,1:T(8,128)S(1)} collective-permute-done((f32[3,3,8,128]{3,2,0,1:T(8,128)S(1)}, f32[3,3,8,128]{3,2,0,1:T(8,128)S(1)}, u32[]{:S(2)}, u32[]{:S(2)}) %collective-permute-start.22) | collective-permute-done | bytes 36896 | tf_op jit(solution)/shard_map/ppermute | solution.py:406
  79.9 3.5 %collective-permute-done.23 = f32[3,3,8,128]{3,2,0,1:T(8,128)S(1)} collective-permute-done((f32[3,3,8,128]{3,2,0,1:T(8,128)S(1)}, f32[3,3,8,128]{3,2,0,1:T(8,128)S(1)}, u32[]{:S(2)}, u32[]{:S(2)}) %collective-permute-start.23) | collective-permute-done | bytes 36896 | tf_op jit(solution)/shard_map/ppermute | solution.py:406
  83.5 1.0 %collective-permute-start.24 = (f32[9,8,128]{2,1,0:T(8,128)S(1)}, f32[9,8,128]{2,1,0:T(8,128)S(1)}, u32[]{:S(2)}, u32[]{:S(2)}) collective-permute-start(f32[9,8,128]{2,1,0:T(8,128)S(1)} %bitcast.73), channel_id=1, source_target_pairs={{0,16},{16,0},{32,48},{48,32},{64,80},{80,64},{96,112},{112,96},{1... | collective-permute-start | bytes 110600 | tf_op jit(solution)/shard_map/ppermute | solution.py:415
  84.6 3.6 %collective-permute-done.25.high_ref = f32[9,8,128]{2,1,0:T(8,128)S(1)} collective-permute-done((f32[9,8,128]{2,1,0:T(8,128)S(1)}, f32[9,8,128]{2,1,0:T(8,128)S(1)}, u32[]{:S(2)}, u32[]{:S(2)}) %collective-permute-start.25) | collective-permute-done | bytes 36896 | tf_op jit(solution)/shard_map/ppermute | solution.py:415
  88.1 0.8 shard_map.81
  (41 shorter events, 4.0 us)
Async XLA Ops:
  0.6 22.6 %copy-start = (f32[3,64,16,128]{3,2,1,0:T(8,128)S(1)}, f32[3,64,16,128]{3,2,1,0:T(8,128)}, u32[]{:S(2)}) copy-start(f32[3,64,16,128]{3,2,1,0:T(8,128)} %param.6) | copy-start | bytes 4718596
  0.6 22.6 %copy-start.1 = (f32[64,16,128]{2,1,0:T(8,128)S(1)}, f32[64,16,128]{2,1,0:T(8,128)}, u32[]{:S(2)}) copy-start(f32[64,16,128]{2,1,0:T(8,128)} %param.7) | copy-start | bytes 1572868
  3.4 6.1 %collective-permute-start = (f32[168,128]{1,0:T(8,128)S(1)}, f32[168,128]{1,0:T(8,128)S(1)}, u32[]{:S(2)}, u32[]{:S(2)}) collective-permute-start(f32[168,128]{1,0:T(8,128)S(1)} %get-tuple-element.24), channel_id=1, source_target_pairs={{0,16},{16,0},{32,48},{48,32},{64,80},{80,64},{96,112},{112,96},{1... | collective-permute-start | bytes 258056 | tf_op jit(solution)/shard_map/ppermute | solution.py:415
  3.5 8.1 %collective-permute-start.1 = (f32[168,128]{1,0:T(8,128)S(1)}, f32[168,128]{1,0:T(8,128)S(1)}, u32[]{:S(2)}, u32[]{:S(2)}) collective-permute-start(f32[168,128]{1,0:T(8,128)S(1)} %get-tuple-element.26), channel_id=1, source_target_pairs={{16,32},{32,16},{48,64},{64,48},{80,96},{96,80},{112,128},{128,112... | collective-permute-start | bytes 258056 | tf_op jit(solution)/shard_map/ppermute | solution.py:415
  11.6 4.1 %collective-permute-start.2 = (f32[3,3,8,128]{3,2,0,1:T(8,128)S(1)}, f32[3,3,8,128]{3,2,0,1:T(8,128)S(1)}, u32[]{:S(2)}, u32[]{:S(2)}) collective-permute-start(f32[3,3,8,128]{3,2,0,1:T(8,128)S(1)} %get-tuple-element.58), channel_id=1, source_target_pairs={{0,4},{4,8},{8,12},{12,0},{1,5},{5,9},{9,13},{13,1},{2,6},{6,10},{... | collective-permute-start | bytes 110600 | tf_op jit(solution)/shard_map/ppermute | solution.py:406
  12.2 5.2 %collective-permute-start.3 = (f32[3,3,8,128]{3,2,0,1:T(8,128)S(1)}, f32[3,3,8,128]{3,2,0,1:T(8,128)S(1)}, u32[]{:S(2)}, u32[]{:S(2)}) collective-permute-start(f32[3,3,8,128]{3,2,0,1:T(8,128)S(1)} %get-tuple-element.59), channel_id=1, source_target_pairs={{4,0},{8,4},{12,8},{0,12},{5,1},{9,5},{13,9},{1,13},{6,2},{10,6},{... | collective-permute-start | bytes 110600 | tf_op jit(solution)/shard_map/ppermute | solution.py:406
  13.8 7.0 %collective-permute-start.6 = (f32[384,128]{1,0:T(8,128)S(1)}, f32[384,128]{1,0:T(8,128)S(1)}, u32[]{:S(2)}, u32[]{:S(2)}) collective-permute-start(f32[384,128]{1,0:T(8,128)S(1)} %get-tuple-element.28), channel_id=1, source_target_pairs={{0,4},{4,8},{8,12},{12,0},{1,5},{5,9},{9,13},{13,1},{2,6},{6,10},{... | collective-permute-start | bytes 589832 | tf_op jit(solution)/shard_map/ppermute | solution.py:406
  15.4 6.9 %collective-permute-start.7 = (f32[384,128]{1,0:T(8,128)S(1)}, f32[384,128]{1,0:T(8,128)S(1)}, u32[]{:S(2)}, u32[]{:S(2)}) collective-permute-start(f32[384,128]{1,0:T(8,128)S(1)} %get-tuple-element.29), channel_id=1, source_target_pairs={{4,0},{8,4},{12,8},{0,12},{5,1},{9,5},{13,9},{1,13},{6,2},{10,6},{... | collective-permute-start | bytes 589832 | tf_op jit(solution)/shard_map/ppermute | solution.py:406
  17.4 5.8 %collective-permute-start.5 = (f32[168,128]{1,0:T(8,128)S(1)}, f32[168,128]{1,0:T(8,128)S(1)}, u32[]{:S(2)}, u32[]{:S(2)}) collective-permute-start(f32[168,128]{1,0:T(8,128)S(1)} %get-tuple-element.61), channel_id=1, source_target_pairs={{1,0},{2,1},{3,2},{0,3},{5,4},{6,5},{7,6},{4,7},{9,8},{10,9},{11,1... | collective-permute-start | bytes 258056 | tf_op jit(solution)/shard_map/ppermute | solution.py:406
  18.2 5.0 %collective-permute-start.4 = (f32[168,128]{1,0:T(8,128)S(1)}, f32[168,128]{1,0:T(8,128)S(1)}, u32[]{:S(2)}, u32[]{:S(2)}) collective-permute-start(f32[168,128]{1,0:T(8,128)S(1)} %get-tuple-element.62), channel_id=1, source_target_pairs={{0,1},{1,2},{2,3},{3,0},{4,5},{5,6},{6,7},{7,4},{8,9},{9,10},{10,1... | collective-permute-start | bytes 258056 | tf_op jit(solution)/shard_map/ppermute | solution.py:406
  30.9 12.8 %collective-permute-start.10 = (f32[384,128]{1,0:T(8,128)S(1)}, f32[384,128]{1,0:T(8,128)S(1)}, u32[]{:S(2)}, u32[]{:S(2)}) collective-permute-start(f32[384,128]{1,0:T(8,128)S(1)} %get-tuple-element.34), channel_id=1, source_target_pairs={{0,4},{4,8},{8,12},{12,0},{1,5},{5,9},{9,13},{13,1},{2,6},{6,10},{... | collective-permute-start | bytes 589832 | tf_op jit(solution)/shard_map/ppermute | solution.py:406
  33.3 10.4 %collective-permute-start.11 = (f32[384,128]{1,0:T(8,128)S(1)}, f32[384,128]{1,0:T(8,128)S(1)}, u32[]{:S(2)}, u32[]{:S(2)}) collective-permute-start(f32[384,128]{1,0:T(8,128)S(1)} %get-tuple-element.35), channel_id=1, source_target_pairs={{4,0},{8,4},{12,8},{0,12},{5,1},{9,5},{13,9},{1,13},{6,2},{10,6},{... | collective-permute-start | bytes 589832 | tf_op jit(solution)/shard_map/ppermute | solution.py:406
  33.4 6.2 %collective-permute-start.8 = (f32[96,128]{1,0:T(8,128)S(1)}, f32[96,128]{1,0:T(8,128)S(1)}, u32[]{:S(2)}, u32[]{:S(2)}) collective-permute-start(f32[96,128]{1,0:T(8,128)S(1)} %get-tuple-element.32), channel_id=1, source_target_pairs={{0,16},{16,0},{32,48},{48,32},{64,80},{80,64},{96,112},{112,96},{1... | collective-permute-start | bytes 147464 | tf_op jit(solution)/shard_map/ppermute | solution.py:415
  33.4 7.7 %collective-permute-start.9 = (f32[96,128]{1,0:T(8,128)S(1)}, f32[96,128]{1,0:T(8,128)S(1)}, u32[]{:S(2)}, u32[]{:S(2)}) collective-permute-start(f32[96,128]{1,0:T(8,128)S(1)} %get-tuple-element.33), channel_id=1, source_target_pairs={{16,32},{32,16},{48,64},{64,48},{80,96},{96,80},{112,128},{128,112... | collective-permute-start | bytes 147464 | tf_op jit(solution)/shard_map/ppermute | solution.py:415
  37.9 5.3 %collective-permute-start.13 = (f32[96,128]{1,0:T(8,128)S(1)}, f32[96,128]{1,0:T(8,128)S(1)}, u32[]{:S(2)}, u32[]{:S(2)}) collective-permute-start(f32[96,128]{1,0:T(8,128)S(1)} %get-tuple-element.36), channel_id=1, source_target_pairs={{1,0},{2,1},{3,2},{0,3},{5,4},{6,5},{7,6},{4,7},{9,8},{10,9},{11,1... | collective-permute-start | bytes 147464 | tf_op jit(solution)/shard_map/ppermute | solution.py:406
  39.6 4.1 %collective-permute-start.12 = (f32[96,128]{1,0:T(8,128)S(1)}, f32[96,128]{1,0:T(8,128)S(1)}, u32[]{:S(2)}, u32[]{:S(2)}) collective-permute-start(f32[96,128]{1,0:T(8,128)S(1)} %get-tuple-element.36), channel_id=1, source_target_pairs={{0,1},{1,2},{2,3},{3,0},{4,5},{5,6},{6,7},{7,4},{8,9},{9,10},{10,1... | collective-permute-start | bytes 147464 | tf_op jit(solution)/shard_map/ppermute | solution.py:406
  49.2 7.9 %collective-permute-start.16 = (f32[384,128]{1,0:T(8,128)S(1)}, f32[384,128]{1,0:T(8,128)S(1)}, u32[]{:S(2)}, u32[]{:S(2)}) collective-permute-start(f32[384,128]{1,0:T(8,128)S(1)} %get-tuple-element.40), channel_id=1, source_target_pairs={{0,4},{4,8},{8,12},{12,0},{1,5},{5,9},{9,13},{13,1},{2,6},{6,10},{... | collective-permute-start | bytes 589832 | tf_op jit(solution)/shard_map/ppermute | solution.py:406
  50.6 6.9 %collective-permute-start.17 = (f32[384,128]{1,0:T(8,128)S(1)}, f32[384,128]{1,0:T(8,128)S(1)}, u32[]{:S(2)}, u32[]{:S(2)}) collective-permute-start(f32[384,128]{1,0:T(8,128)S(1)} %get-tuple-element.41), channel_id=1, source_target_pairs={{4,0},{8,4},{12,8},{0,12},{5,1},{9,5},{13,9},{1,13},{6,2},{10,6},{... | collective-permute-start | bytes 589832 | tf_op jit(solution)/shard_map/ppermute | solution.py:406
  51.3 1.7 %collective-permute-start.14 = (f32[96,128]{1,0:T(8,128)S(1)}, f32[96,128]{1,0:T(8,128)S(1)}, u32[]{:S(2)}, u32[]{:S(2)}) collective-permute-start(f32[96,128]{1,0:T(8,128)S(1)} %get-tuple-element.38), channel_id=1, source_target_pairs={{0,16},{16,0},{32,48},{48,32},{64,80},{80,64},{96,112},{112,96},{1... | collective-permute-start | bytes 147464 | tf_op jit(solution)/shard_map/ppermute | solution.py:415
  51.3 4.7 %collective-permute-start.15 = (f32[96,128]{1,0:T(8,128)S(1)}, f32[96,128]{1,0:T(8,128)S(1)}, u32[]{:S(2)}, u32[]{:S(2)}) collective-permute-start(f32[96,128]{1,0:T(8,128)S(1)} %get-tuple-element.39), channel_id=1, source_target_pairs={{16,32},{32,16},{48,64},{64,48},{80,96},{96,80},{112,128},{128,112... | collective-permute-start | bytes 147464 | tf_op jit(solution)/shard_map/ppermute | solution.py:415
  51.3 5.4 %collective-permute-start.19 = (f32[96,128]{1,0:T(8,128)S(1)}, f32[96,128]{1,0:T(8,128)S(1)}, u32[]{:S(2)}, u32[]{:S(2)}) collective-permute-start(f32[96,128]{1,0:T(8,128)S(1)} %get-tuple-element.42), channel_id=1, source_target_pairs={{1,0},{2,1},{3,2},{0,3},{5,4},{6,5},{7,6},{4,7},{9,8},{10,9},{11,1... | collective-permute-start | bytes 147464 | tf_op jit(solution)/shard_map/ppermute | solution.py:406
  53.0 4.1 %collective-permute-start.18 = (f32[96,128]{1,0:T(8,128)S(1)}, f32[96,128]{1,0:T(8,128)S(1)}, u32[]{:S(2)}, u32[]{:S(2)}) collective-permute-start(f32[96,128]{1,0:T(8,128)S(1)} %get-tuple-element.42), channel_id=1, source_target_pairs={{0,1},{1,2},{2,3},{3,0},{4,5},{5,6},{6,7},{7,4},{8,9},{9,10},{10,1... | collective-permute-start | bytes 147464 | tf_op jit(solution)/shard_map/ppermute | solution.py:406
  65.7 6.6 %collective-permute-start.20 = (f32[9,8,128]{2,1,0:T(8,128)S(1)}, f32[9,8,128]{2,1,0:T(8,128)S(1)}, u32[]{:S(2)}, u32[]{:S(2)}) collective-permute-start(f32[9,8,128]{2,1,0:T(8,128)S(1)} %get-tuple-element.46), channel_id=1, source_target_pairs={{0,1},{1,2},{2,3},{3,0},{4,5},{5,6},{6,7},{7,4},{8,9},{9,10},{10,1... | collective-permute-start | bytes 110600 | tf_op jit(solution)/shard_map/ppermute | solution.py:406
  69.0 5.2 %collective-permute-start.21 = (f32[9,8,128]{2,1,0:T(8,128)S(1)}, f32[9,8,128]{2,1,0:T(8,128)S(1)}, u32[]{:S(2)}, u32[]{:S(2)}) collective-permute-start(f32[9,8,128]{2,1,0:T(8,128)S(1)} %get-tuple-element.47), channel_id=1, source_target_pairs={{1,0},{2,1},{3,2},{0,3},{5,4},{6,5},{7,6},{4,7},{9,8},{10,9},{11,1... | collective-permute-start | bytes 110600 | tf_op jit(solution)/shard_map/ppermute | solution.py:406
  74.2 5.7 %collective-permute-start.22 = (f32[3,3,8,128]{3,2,0,1:T(8,128)S(1)}, f32[3,3,8,128]{3,2,0,1:T(8,128)S(1)}, u32[]{:S(2)}, u32[]{:S(2)}) collective-permute-start(f32[3,3,8,128]{3,2,0,1:T(8,128)S(1)} %get-tuple-element.52), channel_id=1, source_target_pairs={{0,4},{4,8},{8,12},{12,0},{1,5},{5,9},{9,13},{13,1},{2,6},{6,10},{... | collective-permute-start | bytes 110600 | tf_op jit(solution)/shard_map/ppermute | solution.py:406
  78.2 5.2 %collective-permute-start.23 = (f32[3,3,8,128]{3,2,0,1:T(8,128)S(1)}, f32[3,3,8,128]{3,2,0,1:T(8,128)S(1)}, u32[]{:S(2)}, u32[]{:S(2)}) collective-permute-start(f32[3,3,8,128]{3,2,0,1:T(8,128)S(1)} %get-tuple-element.53), channel_id=1, source_target_pairs={{4,0},{8,4},{12,8},{0,12},{5,1},{9,5},{13,9},{1,13},{6,2},{10,6},{... | collective-permute-start | bytes 110600 | tf_op jit(solution)/shard_map/ppermute | solution.py:406
  83.4 4.7 %collective-permute-start.25 = (f32[9,8,128]{2,1,0:T(8,128)S(1)}, f32[9,8,128]{2,1,0:T(8,128)S(1)}, u32[]{:S(2)}, u32[]{:S(2)}) collective-permute-start(f32[9,8,128]{2,1,0:T(8,128)S(1)} %bitcast.76), channel_id=1, source_target_pairs={{16,32},{32,16},{48,64},{64,48},{80,96},{96,80},{112,128},{128,112... | collective-permute-start | bytes 110600 | tf_op jit(solution)/shard_map/ppermute | solution.py:415
  83.5 4.6 %collective-permute-start.24 = (f32[9,8,128]{2,1,0:T(8,128)S(1)}, f32[9,8,128]{2,1,0:T(8,128)S(1)}, u32[]{:S(2)}, u32[]{:S(2)}) collective-permute-start(f32[9,8,128]{2,1,0:T(8,128)S(1)} %bitcast.73), channel_id=1, source_target_pairs={{0,16},{16,0},{32,48},{48,32},{64,80},{80,64},{96,112},{112,96},{1... | collective-permute-start | bytes 110600 | tf_op jit(solution)/shard_map/ppermute | solution.py:415

commit v3 on v2

--- a/solution.py
+++ b/solution.py
@@ -14,6 +14,7 @@
 RUNS = 8
 NY_DEV, NZ_DEV = 4, 4
 UNROLL = 4
+PACK_UNROLL = 8
 SLOT_ROWS = 9 * 8
 SPREAD_PARTS = 2
 SAMPLE_PARTS = 2
@@ -80,8 +81,8 @@
 
     def step(t, blocks):
         blocks = list(blocks)
-        for r in range(UNROLL):
-            u = t * UNROLL + r
+        for r in range(PACK_UNROLL):
+            u = t * PACK_UNROLL + r
             for b in range(6):
                 first = pl.multiple_of((b * 32 + u) * CJ, CJ)
                 turned = pltpu.roll(rows_ref[pl.ds(first, CJ), :], 2 + 4 * u, 1)
@@ -89,7 +90,7 @@
         return tuple(blocks)
 
     zero = jnp.zeros((CJ, CK), F32)
-    blocks = lax.fori_loop(0, 32 // UNROLL, step, (zero,) * 6)
+    blocks = lax.fori_loop(0, 32 // PACK_UNROLL, step, (zero,) * 6)
     for b in range(6):
         out_ref[b * CJ : (b + 1) * CJ, :] = blocks[b]
 
@@ -156,21 +157,22 @@
     return high, (value - high.astype(F32)).astype(BF16)
 
 
-def gather_slots(zlo_ref, zmid_ref, zhi_ref, slots, order):
+def gather_slots(refs, slots, order):
     filled = jnp.zeros((1, CAP), jnp.int32)
-    for group, ref in enumerate((zlo_ref, zmid_ref, zhi_ref)):
+    for group, ref in enumerate(refs):
         for t in range(9):
             s = group * 9 + t
             value = ref[t * 8 : (t + 1) * 8, :]
             slots[s] = value
             filled = filled + jnp.where(value[7:8, :] > 0.5, 1 << s, 0)
-    slots[27] = jnp.zeros((8, CAP), F32)
+    total = 9 * len(refs)
+    slots[total] = jnp.zeros((8, CAP), F32)
     mask = jnp.max(filled)
     count = jnp.int32(0)
-    for s in range(27):
+    for s in range(total):
         order[count] = s
         count = count + ((mask >> s) & 1)
-    order[count] = 27
+    order[count] = total
     return count
 
 
@@ -183,7 +185,6 @@
 
 
 def spread(slots, order, count, plane, forcing_ref):
-    forcing_ref[...] = jnp.zeros_like(forcing_ref)
     width = 2 * CAP
 
     def one_pair(pair, carry):
@@ -337,12 +338,24 @@
         lax.fori_loop(0, 32 // UNROLL, planes, 0)
 
 
+def middle_spread_kernel(mid_ref, forcing_ref, slots, order, plane):
+    forcing_ref[...] = jnp.zeros_like(forcing_ref)
+    spread(slots, order, gather_slots((mid_ref,), slots, order), plane, forcing_ref)
+
+
+def middle_sample_kernel(mid_ref, field, sampled_ref, slots, order):
+    count = gather_slots((mid_ref,), slots, order)
+    sampled_ref[...] = jnp.zeros_like(sampled_ref)
+    sample(slots, order, count, field, sampled_ref)
+
+
 def first_kernel(
-    zlo, zmid, zhi, rows_ref, visc_ref, xlo, xhi, ylo, yhi,
+    zlo, zhi, part_ref, rows_ref, visc_ref, xlo, xhi, ylo, yhi,
     out_ref, forcing_ref, xf_ref, xb_ref, yf_ref, yb_ref, zp_ref,
     slots, order, plane, padded, zsc,
 ):
-    count = gather_slots(zlo, zmid, zhi, slots, order)
+    count = gather_slots((zlo, zhi), slots, order)
+    forcing_ref[...] = part_ref[...]
     spread(slots, order, count, plane, forcing_ref)
     stage(
         0.0, 1.0, rows_ref, rows_ref, visc_ref, forcing_ref,
@@ -367,8 +380,8 @@
 
 
 def third_kernel(
-    zlo_p, zmid_p, zhi_p, rows_ref, base_ref, visc_ref, forcing_ref, xlo, xhi, ylo, yhi, zlo, zhi,
-    out_ref, sampled_ref, slots, order, padded, zsc, field,
+    zlo_p, zhi_p, rows_ref, base_ref, visc_ref, forcing_ref, xlo, xhi, ylo, yhi, zlo, zhi,
+    out_ref, sampled_ref, field, slots, order, padded, zsc,
 ):
     stage(
         1.0 / 3.0, 2.0 / 3.0, rows_ref, base_ref, visc_ref, forcing_ref,
@@ -382,7 +395,7 @@
         return carry
 
     lax.fori_loop(0, NS * CJ // 256, split, 0)
-    count = gather_slots(zlo_p, zmid_p, zhi_p, slots, order)
+    count = gather_slots((zlo_p, zhi_p), slots, order)
     sampled_ref[...] = jnp.zeros_like(sampled_ref)
     sample(slots, order, count, field, sampled_ref)
 
@@ -429,10 +442,11 @@
     pltpu.VMEM((3 * (CI + 4) * PAD_ROWS, CK), F32),
     pltpu.VMEM((6 * CJ, CK), F32),
 ]
-SLOT_SCRATCH = [pltpu.VMEM((28, 8, CAP), F32), pltpu.SMEM((32,), jnp.int32)]
-
-
-def call(kernel, outs, scratch, *args, in_place=False):
+SLOT_SCRATCH = [pltpu.VMEM((19, 8, CAP), F32), pltpu.SMEM((32,), jnp.int32)]
+PLANE = pltpu.VMEM((CI * CJ, 4 * CAP), BF16)
+
+
+def call(kernel, outs, scratch, *args, in_place=False, cost=None):
     if in_place:
         args = [pltpu.with_memory_space_constraint(a, pltpu.HBM) for a in args]
     return pl.pallas_call(
@@ -442,6 +456,7 @@
         out_specs=jax.tree.map(lambda _: vmem(), outs),
         scratch_shapes=scratch,
         compiler_params=params(),
+        cost_estimate=cost,
     )(*args)
 
 
@@ -482,26 +497,36 @@
         jnp.concatenate([held[:, :, 0].reshape(SLOT_ROWS, CAP), zp]),
         "gz",
     )
-    arrived = (zlo, mine, zhi)
+    cost = pl.CostEstimate(flops=4_000_000_000, bytes_accessed=4_000_000, transcendentals=200_000)
+    part = call(
+        middle_spread_kernel, shape(NS * CJ, CK), SLOT_SCRATCH + [PLANE], mine, cost=cost
+    )
 
     section_one, forcing, *faces = call(
         first_kernel, (shape(NS * CJ, CK), shape(NS * CJ, CK)) + FACES,
-        SLOT_SCRATCH + [pltpu.VMEM((CI * CJ, 4 * CAP), BF16)] + STENCIL_SCRATCH,
-        *arrived, rows, visc, xa, xb, ylo, yhi,
+        SLOT_SCRATCH + [PLANE] + STENCIL_SCRATCH,
+        zlo, zhi, part, rows, visc, xa, xb, ylo, yhi,
     )
     section_two, *faces = call(
         second_kernel, (shape(NS * CJ, CK),) + FACES, STENCIL_SCRATCH,
         section_one, rows, visc, forcing, *halos_of(*faces),
     )
-    fresh, sampled = call(
-        third_kernel, (shape(NS * CJ, CK), shape(28, 8, CAP)),
-        SLOT_SCRATCH + STENCIL_SCRATCH + [pltpu.VMEM((NS * CJ, 2 * CK), BF16)],
-        *arrived, section_two, rows, visc, forcing, *halos_of(*faces),
-    )
-
-    back = sampled[:27].reshape(3, 9, 8, CAP)
-    from_low, from_high = exchanged(back[2], back[0], "gz")
-    held = jnp.stack([from_low, back[1], from_high]).reshape(3, 3, 3, 8, CAP)
+    fresh, sampled, field = call(
+        third_kernel,
+        (
+            shape(NS * CJ, CK),
+            shape(19, 8, CAP),
+            jax.ShapeDtypeStruct((NS * CJ, 2 * CK), BF16),
+        ),
+        SLOT_SCRATCH + STENCIL_SCRATCH,
+        zlo, zhi, section_two, rows, visc, forcing, *halos_of(*faces),
+    )
+
+    from_low, from_high = exchanged(sampled[9:18], sampled[:9], "gz")
+    middle = call(
+        middle_sample_kernel, shape(10, 8, CAP), SLOT_SCRATCH, mine, field, cost=cost
+    )
+    held = jnp.stack([from_low, middle[:9], from_high]).reshape(3, 3, 3, 8, CAP)
     from_low, from_high = exchanged(held[:, 2], held[:, 0], "gy")
     held = jnp.stack([from_low, held[:, 1], from_high])
     mine = held[:, :, 1].reshape(9, 8, CAP)

time: 89.1 us -> 85.7 us (0.962); the launches traced: 88.9 us -> 84.2 us
  waiting for transfers between devices: 23.6 us -> 18.5 us
  Pallas kernels: 24.8 us -> 28.5 us
  starting transfers between devices: 39.6 us -> 36.3 us
    ppermute x18, waiting for transfers between devices: 17.1 us -> 12.5 us  [exchanged(): return (lax.ppermute(forward, axis, up), lax.ppermute(backward, axis, down))]
    pallas_call x5 -> x7, Pallas kernels: 24.8 us -> 28.5 us  [call(): pl.pallas_call(kernel, out_shape=outs, in_specs=[pl.BlockSpec(memory_spac...]
    ppermute x18, starting transfers between devices: 28 us -> 25.5 us  [exchanged(): return (lax.ppermute(forward, axis, up), lax.ppermute(backward, axis, down))]
    ppermute x4, starting transfers between devices: 10.6 us -> 9.1 us  [swapped(): lax.ppermute(second, axis, pairs[1])]
  transfers between devices with their start and end apart: 26 -> 26, of which waited for: 15 -> 12; matrix products, arithmetic and copies ran while one was open for 0% -> 0% of each run, Pallas kernels for 0% -> 5%
where the time goes in v3:
time: 85.7 us; the launch traced here: 84.2 us
  starting transfers between devices  36.3 us (42%)
  Pallas kernels  28.5 us (33%)
  waiting for transfers between devices  18.5 us (22%)
    pallas_call x7, Pallas kernels, call(): pl.pallas_call(kernel, out_shape=outs, in_specs=[pl.BlockSpec(memory_spac...  28.5 us
    ppermute x18, starting transfers between devices, exchanged(): return (lax.ppermute(forward, axis, up), lax.ppermute(backward, axis, down))  25.5 us
    ppermute x18, waiting for transfers between devices, exchanged(): return (lax.ppermute(forward, axis, up), lax.ppermute(backward, axis, down))  12.5 us
    ppermute x4, starting transfers between devices, swapped(): lax.ppermute(second, axis, pairs[1])  9.1 us
    ppermute x4, waiting for transfers between devices, swapped(): lax.ppermute(second, axis, pairs[1])  5.99 us
  transfers between devices with their start and end apart: 26, of which 12 were waited for; matrix products, arithmetic and copies ran while one was open for 0% of the time, Pallas kernels for 5%

profile of v3, /device:TPU:30, one launch (start us, length us, event | category | flops | bytes accessed | tf_op | source)
XLA Modules:
  0.0 84.2 jit_solution(12911225700906478443)
XLA Ops:
  0.6 2.3 %shard_map.77 = (f32[72,128]{1,0:T(8,128)S(1)}, s32[8,128]{1,0:T(8,128)S(1)}, f32[168,128]{1,0:T(8,128)S(1)}, f32[168,128]{1,0:T(8,128)S(1)}, f32[384,128]{1,0:T...) custom-call(s32[1024]{0:T(1024)} %bitcast.77, f32[3,1024]{1,0:T(4,128)} %force_any.1, f32[3,1024]{1,0:T(4,128)} %offset_any.1, ...), custom_call_target="tpu_custom_call" | custom-call | tf_op jit(solution)/shard_map/pallas_call | solution.py:452
  3.1 6.0 %collective-permute-start.1 = (f32[168,128]{1,0:T(8,128)S(1)}, f32[168,128]{1,0:T(8,128)S(1)}, u32[]{:S(2)}, u32[]{:S(2)}) collective-permute-start(f32[168,128]{1,0:T(8,128)S(1)} %get-tuple-element.27), channel_id=1, source_target_pairs={{16,32},{32,16},{48,64},{64,48},{80,96},{96,80},{112,128},{128,112... | collective-permute-start | bytes 258056 | tf_op jit(solution)/shard_map/ppermute | solution.py:428
  9.0 2.2 %collective-permute-done.1.xhi = f32[168,128]{1,0:T(8,128)S(1)} collective-permute-done((f32[168,128]{1,0:T(8,128)S(1)}, f32[168,128]{1,0:T(8,128)S(1)}, u32[]{:S(2)}, u32[]{:S(2)}) %collective-permute-start.1) | collective-permute-done | bytes 86048 | tf_op jit(solution)/shard_map/ppermute | solution.py:428
  11.8 1.5 %collective-permute-start.3 = (f32[3,3,8,128]{3,2,0,1:T(8,128)S(1)}, f32[3,3,8,128]{3,2,0,1:T(8,128)S(1)}, u32[]{:S(2)}, u32[]{:S(2)}) collective-permute-start(f32[3,3,8,128]{3,2,0,1:T(8,128)S(1)} %get-tuple-element.58), channel_id=1, source_target_pairs={{4,0},{8,4},{12,8},{0,12},{5,1},{9,5},{13,9},{1,13},{6,2},{10,6},{... | collective-permute-start | bytes 110600 | tf_op jit(solution)/shard_map/ppermute | solution.py:419
  13.3 1.7 %collective-permute-start.6 = (f32[384,128]{1,0:T(8,128)S(1)}, f32[384,128]{1,0:T(8,128)S(1)}, u32[]{:S(2)}, u32[]{:S(2)}) collective-permute-start(f32[384,128]{1,0:T(8,128)S(1)} %get-tuple-element.29), channel_id=1, source_target_pairs={{0,4},{4,8},{8,12},{12,0},{1,5},{5,9},{9,13},{13,1},{2,6},{6,10},{... | collective-permute-start | bytes 589832 | tf_op jit(solution)/shard_map/ppermute | solution.py:419
  15.3 1.6 %collective-permute-done.3 = f32[3,3,8,128]{3,2,0,1:T(8,128)S(1)} collective-permute-done((f32[3,3,8,128]{3,2,0,1:T(8,128)S(1)}, f32[3,3,8,128]{3,2,0,1:T(8,128)S(1)}, u32[]{:S(2)}, u32[]{:S(2)}) %collective-permute-start.3) | collective-permute-done | bytes 36896 | tf_op jit(solution)/shard_map/ppermute | solution.py:419
  17.0 0.8 collective-permute-start.5
  17.8 2.5 %collective-permute-start.4 = (f32[168,128]{1,0:T(8,128)S(1)}, f32[168,128]{1,0:T(8,128)S(1)}, u32[]{:S(2)}, u32[]{:S(2)}) collective-permute-start(f32[168,128]{1,0:T(8,128)S(1)} %get-tuple-element.63), channel_id=1, source_target_pairs={{0,1},{1,2},{2,3},{3,0},{4,5},{5,6},{6,7},{7,4},{8,9},{9,10},{10,1... | collective-permute-start | bytes 258056 | tf_op jit(solution)/shard_map/ppermute | solution.py:419
  20.3 2.2 %shard_map.78.part_ref = f32[3072,128]{1,0:T(8,128)S(1)} custom-call(f32[72,128]{1,0:T(8,128)S(1)} %bitcast.61), custom_call_target="tpu_custom_call" | custom-call | flops 4000000000 | bytes 4000000 | tf_op jit(solution)/shard_map/pallas_call | solution.py:452
  22.8 7.4 %shard_map.79 = (f32[3072,128]{1,0:T(8,128)S(1)}, f32[3072,128]{1,0:T(8,128)S(1)}, f32[96,128]{1,0:T(8,128)S(1)}, f32[96,128]{1,0:T(8,128)S(1)}, f32[384,128]{1,...) custom-call(f32[168,128]{1,0:T(8,128)S(1)} %collective-permute-done.4.zlo.zlo_p, ...), custom_call_target="tpu_custom_call" | custom-call | tf_op jit(solution)/shard_map/pallas_call | solution.py:452
  30.6 1.7 %collective-permute-start.11 = (f32[384,128]{1,0:T(8,128)S(1)}, f32[384,128]{1,0:T(8,128)S(1)}, u32[]{:S(2)}, u32[]{:S(2)}) collective-permute-start(f32[384,128]{1,0:T(8,128)S(1)} %get-tuple-element.36), channel_id=1, source_target_pairs={{4,0},{8,4},{12,8},{0,12},{5,1},{9,5},{13,9},{1,13},{6,2},{10,6},{... | collective-permute-start | bytes 589832 | tf_op jit(solution)/shard_map/ppermute | solution.py:419
  32.3 3.0 %collective-permute-start.9 = (f32[96,128]{1,0:T(8,128)S(1)}, f32[96,128]{1,0:T(8,128)S(1)}, u32[]{:S(2)}, u32[]{:S(2)}) collective-permute-start(f32[96,128]{1,0:T(8,128)S(1)} %get-tuple-element.34), channel_id=1, source_target_pairs={{16,32},{32,16},{48,64},{64,48},{80,96},{96,80},{112,128},{128,112... | collective-permute-start | bytes 147464 | tf_op jit(solution)/shard_map/ppermute | solution.py:428
  35.4 0.7 collective-permute-start.13
  36.0 2.6 %collective-permute-start.12 = (f32[96,128]{1,0:T(8,128)S(1)}, f32[96,128]{1,0:T(8,128)S(1)}, u32[]{:S(2)}, u32[]{:S(2)}) collective-permute-start(f32[96,128]{1,0:T(8,128)S(1)} %get-tuple-element.37), channel_id=1, source_target_pairs={{0,1},{1,2},{2,3},{3,0},{4,5},{5,6},{6,7},{7,4},{8,9},{9,10},{10,1... | collective-permute-start | bytes 147464 | tf_op jit(solution)/shard_map/ppermute | solution.py:419
  38.6 2.1 %collective-permute-done.13.zhi = f32[96,128]{1,0:T(8,128)S(1)} collective-permute-done((f32[96,128]{1,0:T(8,128)S(1)}, f32[96,128]{1,0:T(8,128)S(1)}, u32[]{:S(2)}, u32[]{:S(2)}) %collective-permute-start.13) | collective-permute-done | bytes 49184 | tf_op jit(solution)/shard_map/ppermute | solution.py:419
  40.7 5.2 %shard_map.80 = (f32[3072,128]{1,0:T(8,128)S(1)}, f32[96,128]{1,0:T(8,128)S(1)}, f32[96,128]{1,0:T(8,128)S(1)}, f32[384,128]{1,0:T(8,128)S(1)}, f32[384,128]{1,0:T(8,128)S(1)}, /*index=5*/f32[96,128]{1,0:T(8,128)S(1)}) custom-call(f32[3072,128]{1,0:T(8,128)S(1)} %get-tuple-element.31.rows_ref, f32[3072,128]{1,0:T(8,128)S(1)} %bitcast.55, ...), custom_call_target="tpu_custom_call" | custom-call | tf_op jit(solution)/shard_map/pallas_call | solution.py:452
  45.9 2.7 %collective-permute-start.16 = (f32[384,128]{1,0:T(8,128)S(1)}, f32[384,128]{1,0:T(8,128)S(1)}, u32[]{:S(2)}, u32[]{:S(2)}) collective-permute-start(f32[384,128]{1,0:T(8,128)S(1)} %get-tuple-element.41), channel_id=1, source_target_pairs={{0,4},{4,8},{8,12},{12,0},{1,5},{5,9},{9,13},{13,1},{2,6},{6,10},{... | collective-permute-start | bytes 589832 | tf_op jit(solution)/shard_map/ppermute | solution.py:419
  48.6 2.5 %collective-permute-start.19 = (f32[96,128]{1,0:T(8,128)S(1)}, f32[96,128]{1,0:T(8,128)S(1)}, u32[]{:S(2)}, u32[]{:S(2)}) collective-permute-start(f32[96,128]{1,0:T(8,128)S(1)} %get-tuple-element.43), channel_id=1, source_target_pairs={{1,0},{2,1},{3,2},{0,3},{5,4},{6,5},{7,6},{4,7},{9,8},{10,9},{11,1... | collective-permute-start | bytes 147464 | tf_op jit(solution)/shard_map/ppermute | solution.py:419
  51.2 1.4 %collective-permute-start.18 = (f32[96,128]{1,0:T(8,128)S(1)}, f32[96,128]{1,0:T(8,128)S(1)}, u32[]{:S(2)}, u32[]{:S(2)}) collective-permute-start(f32[96,128]{1,0:T(8,128)S(1)} %get-tuple-element.43), channel_id=1, source_target_pairs={{0,1},{1,2},{2,3},{3,0},{4,5},{5,6},{6,7},{7,4},{8,9},{9,10},{10,1... | collective-permute-start | bytes 147464 | tf_op jit(solution)/shard_map/ppermute | solution.py:419
  52.5 0.8 collective-permute-done.15.xhi
  53.4 0.7 collective-permute-done.19.zhi
  54.0 1.2 %collective-permute-done.18.zlo = f32[96,128]{1,0:T(8,128)S(1)} collective-permute-done((f32[96,128]{1,0:T(8,128)S(1)}, f32[96,128]{1,0:T(8,128)S(1)}, u32[]{:S(2)}, u32[]{:S(2)}) %collective-permute-start.18) | collective-permute-done | bytes 49184 | tf_op jit(solution)/shard_map/ppermute | solution.py:419
  55.5 8.3 %shard_map.81 = (f32[3072,128]{1,0:T(8,128)}, f32[19,8,128]{2,1,0:T(8,128)S(1)}, bf16[3072,256]{1,0:T(8,128)(2,1)S(1)}) custom-call(f32[168,128]{1,0:T(8,128)S(1)} %collective-permute-done.4.zlo.zlo_p, f32[168,128]{1,0:T(8,128)S(1)} %collective-permute-done.5.zhi.zhi_p, f32[3072,128]{1,0:T(8,128)S(1)} %get-tuple-element.38.rows_ref, ...), custom_call_target="tpu_custom_call" | custom-call | tf_op jit(solution)/shard_map/pallas_call | solution.py:452
  64.3 1.5 %collective-permute-start.21 = (f32[9,8,128]{2,1,0:T(8,128)S(1)}, f32[9,8,128]{2,1,0:T(8,128)S(1)}, u32[]{:S(2)}, u32[]{:S(2)}) collective-permute-start(f32[9,8,128]{2,1,0:T(8,128)S(1)} %get-tuple-element.61), channel_id=1, source_target_pairs={{1,0},{2,1},{3,2},{0,3},{5,4},{6,5},{7,6},{4,7},{9,8},{10,9},{11,1... | collective-permute-start | bytes 110600 | tf_op jit(solution)/shard_map/ppermute | solution.py:419
  65.8 2.3 %shard_map.82 = f32[10,8,128]{2,1,0:T(8,128)S(1)} custom-call(f32[72,128]{1,0:T(8,128)S(1)} %bitcast.62, bf16[3072,256]{1,0:T(8,128)(2,1)S(1)} %get-tuple-element.47.field), custom_call_target="tpu_custom_call" | custom-call | flops 4000000000 | bytes 4000000 | tf_op jit(solution)/shard_map/pallas_call | solution.py:452
  68.2 1.3 %collective-permute-done.21 = f32[9,8,128]{2,1,0:T(8,128)S(1)} collective-permute-done((f32[9,8,128]{2,1,0:T(8,128)S(1)}, f32[9,8,128]{2,1,0:T(8,128)S(1)}, u32[]{:S(2)}, u32[]{:S(2)}) %collective-permute-start.21) | collective-permute-done | bytes 36896 | tf_op jit(solution)/shard_map/ppermute | solution.py:419
  69.5 4.0 %collective-permute-start.22 = (f32[3,3,8,128]{3,2,0,1:T(8,128)S(1)}, f32[3,3,8,128]{3,2,0,1:T(8,128)S(1)}, u32[]{:S(2)}, u32[]{:S(2)}) collective-permute-start(f32[3,3,8,128]{3,2,0,1:T(8,128)S(1)} %get-tuple-element.51), channel_id=1, source_target_pairs={{0,4},{4,8},{8,12},{12,0},{1,5},{5,9},{9,13},{13,1},{2,6},{6,10},{... | collective-permute-start | bytes 110600 | tf_op jit(solution)/shard_map/ppermute | solution.py:419
  73.6 1.6 %collective-permute-done.22 = f32[3,3,8,128]{3,2,0,1:T(8,128)S(1)} collective-permute-done((f32[3,3,8,128]{3,2,0,1:T(8,128)S(1)}, f32[3,3,8,128]{3,2,0,1:T(8,128)S(1)}, u32[]{:S(2)}, u32[]{:S(2)}) %collective-permute-start.22) | collective-permute-done | bytes 36896 | tf_op jit(solution)/shard_map/ppermute | solution.py:419
  75.2 3.5 %collective-permute-done.23 = f32[3,3,8,128]{3,2,0,1:T(8,128)S(1)} collective-permute-done((f32[3,3,8,128]{3,2,0,1:T(8,128)S(1)}, f32[3,3,8,128]{3,2,0,1:T(8,128)S(1)}, u32[]{:S(2)}, u32[]{:S(2)}) %collective-permute-start.23) | collective-permute-done | bytes 36896 | tf_op jit(solution)/shard_map/ppermute | solution.py:419
  78.9 1.6 %collective-permute-start.24 = (f32[9,8,128]{2,1,0:T(8,128)S(1)}, f32[9,8,128]{2,1,0:T(8,128)S(1)}, u32[]{:S(2)}, u32[]{:S(2)}) collective-permute-start(f32[9,8,128]{2,1,0:T(8,128)S(1)} %bitcast.74), channel_id=1, source_target_pairs={{0,16},{16,0},{32,48},{48,32},{64,80},{80,64},{96,112},{112,96},{1... | collective-permute-start | bytes 110600 | tf_op jit(solution)/shard_map/ppermute | solution.py:428
  80.5 3.0 %collective-permute-done.25.high_ref = f32[9,8,128]{2,1,0:T(8,128)S(1)} collective-permute-done((f32[9,8,128]{2,1,0:T(8,128)S(1)}, f32[9,8,128]{2,1,0:T(8,128)S(1)}, u32[]{:S(2)}, u32[]{:S(2)}) %collective-permute-start.25) | collective-permute-done | bytes 36896 | tf_op jit(solution)/shard_map/ppermute | solution.py:428
  83.5 0.8 shard_map.83
  (44 shorter events, 2.7 us)
Async XLA Ops:
  3.0 6.1 %collective-permute-start = (f32[168,128]{1,0:T(8,128)S(1)}, f32[168,128]{1,0:T(8,128)S(1)}, u32[]{:S(2)}, u32[]{:S(2)}) collective-permute-start(f32[168,128]{1,0:T(8,128)S(1)} %get-tuple-element.25), channel_id=1, source_target_pairs={{0,16},{16,0},{32,48},{48,32},{64,80},{80,64},{96,112},{112,96},{1... | collective-permute-start | bytes 258056 | tf_op jit(solution)/shard_map/ppermute | solution.py:428
  3.1 8.1 %collective-permute-start.1 = (f32[168,128]{1,0:T(8,128)S(1)}, f32[168,128]{1,0:T(8,128)S(1)}, u32[]{:S(2)}, u32[]{:S(2)}) collective-permute-start(f32[168,128]{1,0:T(8,128)S(1)} %get-tuple-element.27), channel_id=1, source_target_pairs={{16,32},{32,16},{48,64},{64,48},{80,96},{96,80},{112,128},{128,112... | collective-permute-start | bytes 258056 | tf_op jit(solution)/shard_map/ppermute | solution.py:428
  11.2 4.1 %collective-permute-start.2 = (f32[3,3,8,128]{3,2,0,1:T(8,128)S(1)}, f32[3,3,8,128]{3,2,0,1:T(8,128)S(1)}, u32[]{:S(2)}, u32[]{:S(2)}) collective-permute-start(f32[3,3,8,128]{3,2,0,1:T(8,128)S(1)} %get-tuple-element.57), channel_id=1, source_target_pairs={{0,4},{4,8},{8,12},{12,0},{1,5},{5,9},{9,13},{13,1},{2,6},{6,10},{... | collective-permute-start | bytes 110600 | tf_op jit(solution)/shard_map/ppermute | solution.py:419
  11.8 5.2 %collective-permute-start.3 = (f32[3,3,8,128]{3,2,0,1:T(8,128)S(1)}, f32[3,3,8,128]{3,2,0,1:T(8,128)S(1)}, u32[]{:S(2)}, u32[]{:S(2)}) collective-permute-start(f32[3,3,8,128]{3,2,0,1:T(8,128)S(1)} %get-tuple-element.58), channel_id=1, source_target_pairs={{4,0},{8,4},{12,8},{0,12},{5,1},{9,5},{13,9},{1,13},{6,2},{10,6},{... | collective-permute-start | bytes 110600 | tf_op jit(solution)/shard_map/ppermute | solution.py:419
  13.3 9.2 %collective-permute-start.6 = (f32[384,128]{1,0:T(8,128)S(1)}, f32[384,128]{1,0:T(8,128)S(1)}, u32[]{:S(2)}, u32[]{:S(2)}) collective-permute-start(f32[384,128]{1,0:T(8,128)S(1)} %get-tuple-element.29), channel_id=1, source_target_pairs={{0,4},{4,8},{8,12},{12,0},{1,5},{5,9},{9,13},{13,1},{2,6},{6,10},{... | collective-permute-start | bytes 589832 | tf_op jit(solution)/shard_map/ppermute | solution.py:419
  15.0 7.5 %collective-permute-start.7 = (f32[384,128]{1,0:T(8,128)S(1)}, f32[384,128]{1,0:T(8,128)S(1)}, u32[]{:S(2)}, u32[]{:S(2)}) collective-permute-start(f32[384,128]{1,0:T(8,128)S(1)} %get-tuple-element.30), channel_id=1, source_target_pairs={{4,0},{8,4},{12,8},{0,12},{5,1},{9,5},{13,9},{1,13},{6,2},{10,6},{... | collective-permute-start | bytes 589832 | tf_op jit(solution)/shard_map/ppermute | solution.py:419
  17.0 5.8 %collective-permute-start.5 = (f32[168,128]{1,0:T(8,128)S(1)}, f32[168,128]{1,0:T(8,128)S(1)}, u32[]{:S(2)}, u32[]{:S(2)}) collective-permute-start(f32[168,128]{1,0:T(8,128)S(1)} %get-tuple-element.62), channel_id=1, source_target_pairs={{1,0},{2,1},{3,2},{0,3},{5,4},{6,5},{7,6},{4,7},{9,8},{10,9},{11,1... | collective-permute-start | bytes 258056 | tf_op jit(solution)/shard_map/ppermute | solution.py:419
  17.8 5.0 %collective-permute-start.4 = (f32[168,128]{1,0:T(8,128)S(1)}, f32[168,128]{1,0:T(8,128)S(1)}, u32[]{:S(2)}, u32[]{:S(2)}) collective-permute-start(f32[168,128]{1,0:T(8,128)S(1)} %get-tuple-element.63), channel_id=1, source_target_pairs={{0,1},{1,2},{2,3},{3,0},{4,5},{5,6},{6,7},{7,4},{8,9},{9,10},{10,1... | collective-permute-start | bytes 258056 | tf_op jit(solution)/shard_map/ppermute | solution.py:419
  20.3 2.5 %copy-start = (f32[3,64,16,128]{3,2,1,0:T(8,128)S(1)}, f32[3,64,16,128]{3,2,1,0:T(8,128)}, u32[]{:S(2)}) copy-start(f32[3,64,16,128]{3,2,1,0:T(8,128)} %param.6) | copy-start | bytes 4718596
  20.3 2.5 %copy-start.1 = (f32[64,16,128]{2,1,0:T(8,128)S(1)}, f32[64,16,128]{2,1,0:T(8,128)}, u32[]{:S(2)}) copy-start(f32[64,16,128]{2,1,0:T(8,128)} %param.7) | copy-start | bytes 1572868
  30.2 10.5 %collective-permute-start.10 = (f32[384,128]{1,0:T(8,128)S(1)}, f32[384,128]{1,0:T(8,128)S(1)}, u32[]{:S(2)}, u32[]{:S(2)}) collective-permute-start(f32[384,128]{1,0:T(8,128)S(1)} %get-tuple-element.35), channel_id=1, source_target_pairs={{0,4},{4,8},{8,12},{12,0},{1,5},{5,9},{9,13},{13,1},{2,6},{6,10},{... | collective-permute-start | bytes 589832 | tf_op jit(solution)/shard_map/ppermute | solution.py:419
  30.6 10.1 %collective-permute-start.11 = (f32[384,128]{1,0:T(8,128)S(1)}, f32[384,128]{1,0:T(8,128)S(1)}, u32[]{:S(2)}, u32[]{:S(2)}) collective-permute-start(f32[384,128]{1,0:T(8,128)S(1)} %get-tuple-element.36), channel_id=1, source_target_pairs={{4,0},{8,4},{12,8},{0,12},{5,1},{9,5},{13,9},{1,13},{6,2},{10,6},{... | collective-permute-start | bytes 589832 | tf_op jit(solution)/shard_map/ppermute | solution.py:419
  32.3 3.7 %collective-permute-start.8 = (f32[96,128]{1,0:T(8,128)S(1)}, f32[96,128]{1,0:T(8,128)S(1)}, u32[]{:S(2)}, u32[]{:S(2)}) collective-permute-start(f32[96,128]{1,0:T(8,128)S(1)} %get-tuple-element.33), channel_id=1, source_target_pairs={{0,16},{16,0},{32,48},{48,32},{64,80},{80,64},{96,112},{112,96},{1... | collective-permute-start | bytes 147464 | tf_op jit(solution)/shard_map/ppermute | solution.py:428
  32.3 6.3 %collective-permute-start.9 = (f32[96,128]{1,0:T(8,128)S(1)}, f32[96,128]{1,0:T(8,128)S(1)}, u32[]{:S(2)}, u32[]{:S(2)}) collective-permute-start(f32[96,128]{1,0:T(8,128)S(1)} %get-tuple-element.34), channel_id=1, source_target_pairs={{16,32},{32,16},{48,64},{64,48},{80,96},{96,80},{112,128},{128,112... | collective-permute-start | bytes 147464 | tf_op jit(solution)/shard_map/ppermute | solution.py:428
  35.4 5.3 %collective-permute-start.13 = (f32[96,128]{1,0:T(8,128)S(1)}, f32[96,128]{1,0:T(8,128)S(1)}, u32[]{:S(2)}, u32[]{:S(2)}) collective-permute-start(f32[96,128]{1,0:T(8,128)S(1)} %get-tuple-element.37), channel_id=1, source_target_pairs={{1,0},{2,1},{3,2},{0,3},{5,4},{6,5},{7,6},{4,7},{9,8},{10,9},{11,1... | collective-permute-start | bytes 147464 | tf_op jit(solution)/shard_map/ppermute | solution.py:419
  36.0 4.6 %collective-permute-start.12 = (f32[96,128]{1,0:T(8,128)S(1)}, f32[96,128]{1,0:T(8,128)S(1)}, u32[]{:S(2)}, u32[]{:S(2)}) collective-permute-start(f32[96,128]{1,0:T(8,128)S(1)} %get-tuple-element.37), channel_id=1, source_target_pairs={{0,1},{1,2},{2,3},{3,0},{4,5},{5,6},{6,7},{7,4},{8,9},{9,10},{10,1... | collective-permute-start | bytes 147464 | tf_op jit(solution)/shard_map/ppermute | solution.py:419
  45.9 9.4 %collective-permute-start.16 = (f32[384,128]{1,0:T(8,128)S(1)}, f32[384,128]{1,0:T(8,128)S(1)}, u32[]{:S(2)}, u32[]{:S(2)}) collective-permute-start(f32[384,128]{1,0:T(8,128)S(1)} %get-tuple-element.41), channel_id=1, source_target_pairs={{0,4},{4,8},{8,12},{12,0},{1,5},{5,9},{9,13},{13,1},{2,6},{6,10},{... | collective-permute-start | bytes 589832 | tf_op jit(solution)/shard_map/ppermute | solution.py:419
  48.6 6.9 %collective-permute-start.17 = (f32[384,128]{1,0:T(8,128)S(1)}, f32[384,128]{1,0:T(8,128)S(1)}, u32[]{:S(2)}, u32[]{:S(2)}) collective-permute-start(f32[384,128]{1,0:T(8,128)S(1)} %get-tuple-element.42), channel_id=1, source_target_pairs={{4,0},{8,4},{12,8},{0,12},{5,1},{9,5},{13,9},{1,13},{6,2},{10,6},{... | collective-permute-start | bytes 589832 | tf_op jit(solution)/shard_map/ppermute | solution.py:419
  48.6 2.5 %collective-permute-start.14 = (f32[96,128]{1,0:T(8,128)S(1)}, f32[96,128]{1,0:T(8,128)S(1)}, u32[]{:S(2)}, u32[]{:S(2)}) collective-permute-start(f32[96,128]{1,0:T(8,128)S(1)} %get-tuple-element.39), channel_id=1, source_target_pairs={{0,16},{16,0},{32,48},{48,32},{64,80},{80,64},{96,112},{112,96},{1... | collective-permute-start | bytes 147464 | tf_op jit(solution)/shard_map/ppermute | solution.py:428
  48.6 4.7 %collective-permute-start.15 = (f32[96,128]{1,0:T(8,128)S(1)}, f32[96,128]{1,0:T(8,128)S(1)}, u32[]{:S(2)}, u32[]{:S(2)}) collective-permute-start(f32[96,128]{1,0:T(8,128)S(1)} %get-tuple-element.40), channel_id=1, source_target_pairs={{16,32},{32,16},{48,64},{64,48},{80,96},{96,80},{112,128},{128,112... | collective-permute-start | bytes 147464 | tf_op jit(solution)/shard_map/ppermute | solution.py:428
  48.6 5.4 %collective-permute-start.19 = (f32[96,128]{1,0:T(8,128)S(1)}, f32[96,128]{1,0:T(8,128)S(1)}, u32[]{:S(2)}, u32[]{:S(2)}) collective-permute-start(f32[96,128]{1,0:T(8,128)S(1)} %get-tuple-element.43), channel_id=1, source_target_pairs={{1,0},{2,1},{3,2},{0,3},{5,4},{6,5},{7,6},{4,7},{9,8},{10,9},{11,1... | collective-permute-start | bytes 147464 | tf_op jit(solution)/shard_map/ppermute | solution.py:419
  51.2 4.1 %collective-permute-start.18 = (f32[96,128]{1,0:T(8,128)S(1)}, f32[96,128]{1,0:T(8,128)S(1)}, u32[]{:S(2)}, u32[]{:S(2)}) collective-permute-start(f32[96,128]{1,0:T(8,128)S(1)} %get-tuple-element.43), channel_id=1, source_target_pairs={{0,1},{1,2},{2,3},{3,0},{4,5},{5,6},{6,7},{7,4},{8,9},{9,10},{10,1... | collective-permute-start | bytes 147464 | tf_op jit(solution)/shard_map/ppermute | solution.py:419
  63.8 4.4 %collective-permute-start.20 = (f32[9,8,128]{2,1,0:T(8,128)S(1)}, f32[9,8,128]{2,1,0:T(8,128)S(1)}, u32[]{:S(2)}, u32[]{:S(2)}) collective-permute-start(f32[9,8,128]{2,1,0:T(8,128)S(1)} %get-tuple-element.60), channel_id=1, source_target_pairs={{0,1},{1,2},{2,3},{3,0},{4,5},{5,6},{6,7},{7,4},{8,9},{9,10},{10,1... | collective-permute-start | bytes 110600 | tf_op jit(solution)/shard_map/ppermute | solution.py:419
  64.3 5.2 %collective-permute-start.21 = (f32[9,8,128]{2,1,0:T(8,128)S(1)}, f32[9,8,128]{2,1,0:T(8,128)S(1)}, u32[]{:S(2)}, u32[]{:S(2)}) collective-permute-start(f32[9,8,128]{2,1,0:T(8,128)S(1)} %get-tuple-element.61), channel_id=1, source_target_pairs={{1,0},{2,1},{3,2},{0,3},{5,4},{6,5},{7,6},{4,7},{9,8},{10,9},{11,1... | collective-permute-start | bytes 110600 | tf_op jit(solution)/shard_map/ppermute | solution.py:419
  69.5 5.7 %collective-permute-start.22 = (f32[3,3,8,128]{3,2,0,1:T(8,128)S(1)}, f32[3,3,8,128]{3,2,0,1:T(8,128)S(1)}, u32[]{:S(2)}, u32[]{:S(2)}) collective-permute-start(f32[3,3,8,128]{3,2,0,1:T(8,128)S(1)} %get-tuple-element.51), channel_id=1, source_target_pairs={{0,4},{4,8},{8,12},{12,0},{1,5},{5,9},{9,13},{13,1},{2,6},{6,10},{... | collective-permute-start | bytes 110600 | tf_op jit(solution)/shard_map/ppermute | solution.py:419
  73.6 5.2 %collective-permute-start.23 = (f32[3,3,8,128]{3,2,0,1:T(8,128)S(1)}, f32[3,3,8,128]{3,2,0,1:T(8,128)S(1)}, u32[]{:S(2)}, u32[]{:S(2)}) collective-permute-start(f32[3,3,8,128]{3,2,0,1:T(8,128)S(1)} %get-tuple-element.52), channel_id=1, source_target_pairs={{4,0},{8,4},{12,8},{0,12},{5,1},{9,5},{13,9},{1,13},{6,2},{10,6},{... | collective-permute-start | bytes 110600 | tf_op jit(solution)/shard_map/ppermute | solution.py:419
  78.8 4.7 %collective-permute-start.25 = (f32[9,8,128]{2,1,0:T(8,128)S(1)}, f32[9,8,128]{2,1,0:T(8,128)S(1)}, u32[]{:S(2)}, u32[]{:S(2)}) collective-permute-start(f32[9,8,128]{2,1,0:T(8,128)S(1)} %bitcast.76), channel_id=1, source_target_pairs={{16,32},{32,16},{48,64},{64,48},{80,96},{96,80},{112,128},{128,112... | collective-permute-start | bytes 110600 | tf_op jit(solution)/shard_map/ppermute | solution.py:428
  78.9 4.6 %collective-permute-start.24 = (f32[9,8,128]{2,1,0:T(8,128)S(1)}, f32[9,8,128]{2,1,0:T(8,128)S(1)}, u32[]{:S(2)}, u32[]{:S(2)}) collective-permute-start(f32[9,8,128]{2,1,0:T(8,128)S(1)} %bitcast.74), channel_id=1, source_target_pairs={{0,16},{16,0},{32,48},{48,32},{64,80},{80,64},{96,112},{112,96},{1... | collective-permute-start | bytes 110600 | tf_op jit(solution)/shard_map/ppermute | solution.py:428

commit v4 on v3

--- a/solution.py
+++ b/solution.py
@@ -1,11 +1,10 @@
-import functools
-
 import jax
 import jax.numpy as jnp
 from jax import lax
 from jax.experimental import pallas as pl
 from jax.experimental.pallas import tpu as pltpu
 from jax.sharding import PartitionSpec as P
+
 
 DT = 0.1
 CI, CJ, CK = 64, 16, 128
@@ -59,15 +58,16 @@
             ]
 
 
-def pack_x(rows_ref, first_ref, second_ref, skip=0):
+def pack_x(rows_ref, message_ref, skip=0):
     even = is_even()
+    half = skip + 6 * CJ
     for c in range(3):
         base = c * CI * CJ
         upper = rows_ref[base + (CI - 2) * CJ : base + CI * CJ, :]
         lower = rows_ref[base : base + 2 * CJ, :]
-        part = slice(skip + c * 2 * CJ, skip + (c + 1) * 2 * CJ)
-        first_ref[part, :] = jnp.where(even, upper, lower)
-        second_ref[part, :] = jnp.where(even, lower, upper)
+        first = skip + c * 2 * CJ
+        message_ref[first : first + 2 * CJ, :] = jnp.where(even, upper, lower)
+        message_ref[half + first : half + first + 2 * CJ, :] = jnp.where(even, lower, upper)
 
 
 def z_masks():
@@ -97,7 +97,7 @@
 
 def pack_kernel(
     tile_any, force_any, offset_any, cell_any, rows_any,
-    mid_ref, code_ref, xa_ref, xb_ref, yf_ref, yb_ref, zp_ref,
+    mid_ref, code_ref, x_ref, yf_ref, yb_ref, zp_ref,
     points_ref, tile_ref, force_ref, offset_ref, cell_ref, rows_ref, sems,
 ):
     moves = [
@@ -128,12 +128,13 @@
         )
         points_ref[code] = block
         code_ref[run : run + 1, :] = jnp.full((1, CAP), code, jnp.int32)
-    for group, ref in enumerate((xa_ref, mid_ref, xb_ref)):
+    half = SLOT_ROWS + 6 * CJ
+    for group, (ref, first) in enumerate(((x_ref, 0), (mid_ref, 0), (x_ref, half))):
         for t in range(9):
-            ref[t * 8 : (t + 1) * 8, :] = points_ref[group * 9 + t]
+            ref[first + t * 8 : first + (t + 1) * 8, :] = points_ref[group * 9 + t]
     moves[4].wait()
     pack_y(rows_ref, yf_ref, yb_ref)
-    pack_x(rows_ref, xa_ref, xb_ref, SLOT_ROWS)
+    pack_x(rows_ref, x_ref, SLOT_ROWS)
     pack_z(rows_ref, zp_ref)
 
 
@@ -351,7 +352,7 @@
 
 def first_kernel(
     zlo, zhi, part_ref, rows_ref, visc_ref, xlo, xhi, ylo, yhi,
-    out_ref, forcing_ref, xf_ref, xb_ref, yf_ref, yb_ref, zp_ref,
+    out_ref, forcing_ref, x_ref, yf_ref, yb_ref, zp_ref,
     slots, order, plane, padded, zsc,
 ):
     count = gather_slots((zlo, zhi), slots, order)
@@ -362,20 +363,20 @@
         (xlo, xhi, ylo, yhi, zlo, zhi), padded, zsc, out_ref, SLOT_ROWS,
     )
     pack_y(out_ref, yf_ref, yb_ref)
-    pack_x(out_ref, xf_ref, xb_ref)
+    pack_x(out_ref, x_ref)
     pack_z(out_ref, zp_ref)
 
 
 def second_kernel(
     rows_ref, base_ref, visc_ref, forcing_ref, xlo, xhi, ylo, yhi, zlo, zhi,
-    out_ref, xf_ref, xb_ref, yf_ref, yb_ref, zp_ref, padded, zsc,
+    out_ref, x_ref, yf_ref, yb_ref, zp_ref, padded, zsc,
 ):
     stage(
         0.75, 0.25, rows_ref, base_ref, visc_ref, forcing_ref,
         (xlo, xhi, ylo, yhi, zlo, zhi), padded, zsc, out_ref,
     )
     pack_y(out_ref, yf_ref, yb_ref)
-    pack_x(out_ref, xf_ref, xb_ref)
+    pack_x(out_ref, x_ref)
     pack_z(out_ref, zp_ref)
 
 
@@ -387,6 +388,7 @@
         1.0 / 3.0, 2.0 / 3.0, rows_ref, base_ref, visc_ref, forcing_ref,
         (xlo, xhi, ylo, yhi, zlo, zhi), padded, zsc, out_ref,
     )
+
     def split(t, carry):
         first = pl.multiple_of(t * 256, 256)
         high, low = halves(out_ref[pl.ds(first, 256), :])
@@ -416,7 +418,9 @@
     count = lax.axis_size(axis)
     up = [(i, (i + 1) % count) for i in range(count)]
     down = [(target, source) for source, target in up]
-    return lax.ppermute(forward, axis, up), lax.ppermute(backward, axis, down)
+    low = lax.ppermute(forward, axis, up)
+    high = lax.ppermute(backward, axis, down)
+    return low, high
 
 
 def swapped(first, second, axis):
@@ -428,15 +432,23 @@
     return lax.ppermute(first, axis, pairs[0]), lax.ppermute(second, axis, pairs[1])
 
 
-def halos_of(xf, xb, yf, yb, zp):
+def passed_on(message, axis):
+    count = lax.axis_size(axis)
+    across = [(i, i + 1 - 2 * (i % 2)) for i in range(count)]
+    onward = [(i, (i + 2 - 4 * (i % 2)) % count) for i in range(count)]
+    near = lax.ppermute(message, axis, across)
+    return near, lax.ppermute(near[message.shape[0] // 2 :], axis, onward)
+
+
+def halos_of(x, yf, yb, zp):
+    xlo, xhi = passed_on(x, "gx")
     ylo, yhi = exchanged(yf, yb, "gy")
-    xlo, xhi = swapped(xf, xb, "gx")
     zlo, zhi = exchanged(zp, zp, "gz")
     return xlo, xhi, ylo, yhi, zlo, zhi
 
 
 FACES = (
-    shape(6 * CJ, CK), shape(6 * CJ, CK), shape(2 * NS, CK), shape(2 * NS, CK), shape(6 * CJ, CK),
+    shape(12 * CJ, CK), shape(2 * NS, CK), shape(2 * NS, CK), shape(6 * CJ, CK),
 )
 STENCIL_SCRATCH = [
     pltpu.VMEM((3 * (CI + 4) * PAD_ROWS, CK), F32),
@@ -466,11 +478,11 @@
     visc = viscosity.reshape(CI * CJ, CK)
     cells = point_cell.reshape(RUNS, CAP)
 
-    message = shape(SLOT_ROWS + 6 * CJ, CK)
-    mid, codes, xa, xb, yf, yb, zp = call(
+    message = shape(2 * (SLOT_ROWS + 6 * CJ), CK)
+    mid, codes, x, yf, yb, zp = call(
         pack_kernel,
-        (shape(SLOT_ROWS, CAP), jax.ShapeDtypeStruct((RUNS, CAP), jnp.int32), message, message)
-        + FACES[2:],
+        (shape(SLOT_ROWS, CAP), jax.ShapeDtypeStruct((RUNS, CAP), jnp.int32), message)
+        + FACES[1:],
         [
             pltpu.VMEM((27, 8, CAP), F32),
             pltpu.SMEM((RUNS * CAP,), jnp.int32),
@@ -486,9 +498,10 @@
     def slots_of(received):
         return received[:SLOT_ROWS]
 
-    xa, xb = swapped(xa, xb, "gx")
+    xa, xb = passed_on(x, "gx")
     ylo, yhi = exchanged(yf, yb, "gy")
-    held = jnp.stack([slots_of(xa), mid, slots_of(xb)]).reshape(3, 3, 3, 8, CAP)
+    far = slots_of(xb)
+    held = jnp.stack([slots_of(xa), mid, far]).reshape(3, 3, 3, 8, CAP)
     from_low, from_high = exchanged(held[:, 2], held[:, 0], "gy")
     held = jnp.stack([from_low, held[:, 1], from_high])
     mine = held[:, :, 1].reshape(SLOT_ROWS, CAP)
@@ -550,6 +563,5 @@
         P(("gx", "gy", "gz"), None),
     )
     out_specs = (P(None, "gx", "gy", "gz"), P(None, ("gx", "gy", "gz")))
-    return jax.shard_map(
-        per_device, mesh=mesh, in_specs=in_specs, out_specs=out_specs, check_vma=False
-    )
+
+    return jax.shard_map(per_device, mesh=mesh, in_specs=in_specs, out_specs=out_specs, check_vma=False)

time: 85.7 us -> 89.5 us (1.044)
  the two profiles are of different devices: /device:TPU:30 before, /device:TPU:99 now
where the time goes in v4:
time: 89.5 us; the launch traced here: 89.4 us
  Pallas kernels  32.7 us (37%)
  starting transfers between devices  32.6 us (36%)
  waiting for transfers between devices  23.2 us (26%)
    pallas_call x7, Pallas kernels, call(): pl.pallas_call(kernel, out_shape=outs, in_specs=[pl.BlockSpec(memory_spac...  32.7 us
    ppermute x1, starting transfers between devices, swapped(): lax.ppermute(second, axis, pairs[1])  10.3 us
    ppermute x9, starting transfers between devices, exchanged(): low = lax.ppermute(forward, axis, up)  8.37 us
    ppermute x9, starting transfers between devices, exchanged(): high = lax.ppermute(backward, axis, down)  8.17 us
    ppermute x3, waiting for transfers between devices, passed_on(): return (near, lax.ppermute(near[message.shape[0] // 2:], axis, onward))  7.72 us
    ppermute x9, waiting for transfers between devices, exchanged(): high = lax.ppermute(backward, axis, down)  6.4 us
    ppermute x9, waiting for transfers between devices, exchanged(): low = lax.ppermute(forward, axis, up)  6.39 us
    ppermute x3, starting transfers between devices, passed_on(): near = lax.ppermute(message, axis, across)  5.6 us
  transfers between devices with their start and end apart: 26, of which 13 were waited for; matrix products, arithmetic and copies ran while one was open for 0% of the time, Pallas kernels for 7%

profile of v4, /device:TPU:99, one launch (start us, length us, event | category | flops | bytes accessed | tf_op | source)
XLA Modules:
  0.0 89.4 jit_solution(315913371332361195)
XLA Ops:
  0.6 2.3 %shard_map.77 = (f32[72,128]{1,0:T(8,128)S(1)}, s32[8,128]{1,0:T(8,128)S(1)}, f32[336,128]{1,0:T(8,128)S(1)}, f32[384,128]{1,0:T(8,128)S(1)}, f32[384,128]{1,0:T(8,128)S(1)}, /*index=5*/f32[96,128]{1,0:T(8,128)S(1)}) custom-call(s32[1024]{0:T(1024)} %bitcast.77, f32[3,1024]{1,0:T(4,128)} %force_any.1, f32[3,1024]{1,0:T(4,128)} %offset_any.1, ...), custom_call_target="tpu_custom_call" | custom-call | tf_op jit(solution)/shard_map/pallas_call | solution.py:464
  3.7 1.0 %collective-permute-done.xlo = f32[336,128]{1,0:T(8,128)S(1)} collective-permute-done((f32[336,128]{1,0:T(8,128)S(1)}, f32[336,128]{1,0:T(8,128)S(1)}, u32[]{:S(2)}, u32[]{:S(2)}) %collective-permute-start) | collective-permute-done | bytes 172064 | tf_op jit(solution)/shard_map/ppermute | solution.py:439
  4.8 4.7 %collective-permute-done.1.xhi = f32[168,128]{1,0:T(8,128)S(1)} collective-permute-done((f32[168,128]{1,0:T(8,128)S(1)}, f32[168,128]{1,0:T(8,128)S(1)}, u32[]{:S(2)}, u32[]{:S(2)}) %collective-permute-start.1) | collective-permute-done | bytes 86048 | tf_op jit(solution)/shard_map/ppermute | solution.py:440
  9.5 1.3 %collective-permute-start.2 = (f32[3,3,8,128]{3,2,0,1:T(8,128)S(1)}, f32[3,3,8,128]{3,2,0,1:T(8,128)S(1)}, u32[]{:S(2)}, u32[]{:S(2)}) collective-permute-start(f32[3,3,8,128]{3,2,0,1:T(8,128)S(1)} %get-tuple-element.51), channel_id=1, source_target_pairs={{0,4},{4,8},{8,12},{12,0},{1,5},{5,9},{9,13},{13,1},{2,6},{6,10},{... | collective-permute-start | bytes 110600 | tf_op jit(solution)/shard_map/ppermute | solution.py:421
  11.1 1.2 %collective-permute-start.6 = (f32[384,128]{1,0:T(8,128)S(1)}, f32[384,128]{1,0:T(8,128)S(1)}, u32[]{:S(2)}, u32[]{:S(2)}) collective-permute-start(f32[384,128]{1,0:T(8,128)S(1)} %get-tuple-element.25), channel_id=1, source_target_pairs={{0,4},{4,8},{8,12},{12,0},{1,5},{5,9},{9,13},{13,1},{2,6},{6,10},{... | collective-permute-start | bytes 589832 | tf_op jit(solution)/shard_map/ppermute | solution.py:421
  12.5 1.4 %collective-permute-done.3 = f32[3,3,8,128]{3,2,0,1:T(8,128)S(1)} collective-permute-done((f32[3,3,8,128]{3,2,0,1:T(8,128)S(1)}, f32[3,3,8,128]{3,2,0,1:T(8,128)S(1)}, u32[]{:S(2)}, u32[]{:S(2)}) %collective-permute-start.3) | collective-permute-done | bytes 36896 | tf_op jit(solution)/shard_map/ppermute | solution.py:422
  14.0 2.8 %collective-permute-start.5 = (f32[168,128]{1,0:T(8,128)S(1)}, f32[168,128]{1,0:T(8,128)S(1)}, u32[]{:S(2)}, u32[]{:S(2)}) collective-permute-start(f32[168,128]{1,0:T(8,128)S(1)} %get-tuple-element.56), channel_id=1, source_target_pairs={{1,0},{2,1},{3,2},{0,3},{5,4},{6,5},{7,6},{4,7},{9,8},{10,9},{11,1... | collective-permute-start | bytes 258056 | tf_op jit(solution)/shard_map/ppermute | solution.py:422
  16.8 3.2 %shard_map.78.part_ref = f32[3072,128]{1,0:T(8,128)S(1)} custom-call(f32[72,128]{1,0:T(8,128)S(1)} %bitcast.61), custom_call_target="tpu_custom_call" | custom-call | flops 4000000000 | bytes 4000000 | tf_op jit(solution)/shard_map/pallas_call | solution.py:464
  20.0 1.3 %collective-permute-done.4.zlo.zlo_p = f32[168,128]{1,0:T(8,128)S(1)} collective-permute-done((f32[168,128]{1,0:T(8,128)S(1)}, f32[168,128]{1,0:T(8,128)S(1)}, u32[]{:S(2)}, u32[]{:S(2)}) %collective-permute-start.4) | collective-permute-done | bytes 86048 | tf_op jit(solution)/shard_map/ppermute | solution.py:421
  21.3 8.4 %shard_map.79 = (f32[3072,128]{1,0:T(8,128)S(1)}, f32[3072,128]{1,0:T(8,128)S(1)}, f32[192,128]{1,0:T(8,128)S(1)}, f32[384,128]{1,0:T(8,128)S(1)}, f32[384,128]{1,0:T(8,128)S(1)}, /*index=5*/f32[96,128]{1,0:T(8,128)S(1)}) custom-call(f32[168,128]{1,0:T(8,128)S(1)} %collective-permute-done.4.zlo.zlo_p, f32[168,128]{1,0:T(8,128)S(1)} %collective-permute-done.5.zhi.zhi_p, ...), custom_call_target="tpu_custom_call" | custom-call | tf_op jit(solution)/shard_map/pallas_call | solution.py:464
  29.8 1.5 %collective-permute-start.11 = (f32[384,128]{1,0:T(8,128)S(1)}, f32[384,128]{1,0:T(8,128)S(1)}, u32[]{:S(2)}, u32[]{:S(2)}) collective-permute-start(f32[384,128]{1,0:T(8,128)S(1)} %get-tuple-element.31), channel_id=1, source_target_pairs={{4,0},{8,4},{12,8},{0,12},{5,1},{9,5},{13,9},{1,13},{6,2},{10,6},{... | collective-permute-start | bytes 589832 | tf_op jit(solution)/shard_map/ppermute | solution.py:422
  31.3 3.5 %collective-permute-start.8 = (f32[192,128]{1,0:T(8,128)S(1)}, f32[192,128]{1,0:T(8,128)S(1)}, u32[]{:S(2)}, u32[]{:S(2)}) collective-permute-start(f32[192,128]{1,0:T(8,128)S(1)} %get-tuple-element.29), channel_id=1, source_target_pairs={{0,16},{16,0},{32,48},{48,32},{64,80},{80,64},{96,112},{112,96},{1... | collective-permute-start | bytes 294920 | tf_op jit(solution)/shard_map/ppermute | solution.py:439
  34.8 1.5 %collective-permute-start.13 = (f32[96,128]{1,0:T(8,128)S(1)}, f32[96,128]{1,0:T(8,128)S(1)}, u32[]{:S(2)}, u32[]{:S(2)}) collective-permute-start(f32[96,128]{1,0:T(8,128)S(1)} %get-tuple-element.32), channel_id=1, source_target_pairs={{1,0},{2,1},{3,2},{0,3},{5,4},{6,5},{7,6},{4,7},{9,8},{10,9},{11,1... | collective-permute-start | bytes 147464 | tf_op jit(solution)/shard_map/ppermute | solution.py:422
  36.4 1.7 %collective-permute-done.13.zhi = f32[96,128]{1,0:T(8,128)S(1)} collective-permute-done((f32[96,128]{1,0:T(8,128)S(1)}, f32[96,128]{1,0:T(8,128)S(1)}, u32[]{:S(2)}, u32[]{:S(2)}) %collective-permute-start.13) | collective-permute-done | bytes 49184 | tf_op jit(solution)/shard_map/ppermute | solution.py:422
  38.1 2.4 %collective-permute-done.12.zlo = f32[96,128]{1,0:T(8,128)S(1)} collective-permute-done((f32[96,128]{1,0:T(8,128)S(1)}, f32[96,128]{1,0:T(8,128)S(1)}, u32[]{:S(2)}, u32[]{:S(2)}) %collective-permute-start.12) | collective-permute-done | bytes 49184 | tf_op jit(solution)/shard_map/ppermute | solution.py:421
  40.4 1.5 %collective-permute-done.9.xhi = f32[96,128]{1,0:T(8,128)S(1)} collective-permute-done((f32[96,128]{1,0:T(8,128)S(1)}, f32[96,128]{1,0:T(8,128)S(1)}, u32[]{:S(2)}, u32[]{:S(2)}) %collective-permute-start.9) | collective-permute-done | bytes 49184 | tf_op jit(solution)/shard_map/ppermute | solution.py:440
  42.0 5.2 %shard_map.80 = (f32[3072,128]{1,0:T(8,128)S(1)}, f32[192,128]{1,0:T(8,128)S(1)}, f32[384,128]{1,0:T(8,128)S(1)}, f32[384,128]{1,0:T(8,128)S(1)}, f32[96,128]{1,0:T(8,128)S(1)}) custom-call(f32[3072,128]{1,0:T(8,128)S(1)} %get-tuple-element.27.rows_ref, f32[3072,128]{1,0:T(8,128)S(1)} %bitcast.55, f32[1024,128]{1,0:T(8,128)S(1)} %bitcast.58, ...), custom_call_target="tpu_custom_call" | custom-call | tf_op jit(solution)/shard_map/pallas_call | solution.py:464
  47.2 1.8 %collective-permute-start.16 = (f32[384,128]{1,0:T(8,128)S(1)}, f32[384,128]{1,0:T(8,128)S(1)}, u32[]{:S(2)}, u32[]{:S(2)}) collective-permute-start(f32[384,128]{1,0:T(8,128)S(1)} %get-tuple-element.35), channel_id=1, source_target_pairs={{0,4},{4,8},{8,12},{12,0},{1,5},{5,9},{9,13},{13,1},{2,6},{6,10},{... | collective-permute-start | bytes 589832 | tf_op jit(solution)/shard_map/ppermute | solution.py:421
  49.0 1.4 %collective-permute-start.14 = (f32[192,128]{1,0:T(8,128)S(1)}, f32[192,128]{1,0:T(8,128)S(1)}, u32[]{:S(2)}, u32[]{:S(2)}) collective-permute-start(f32[192,128]{1,0:T(8,128)S(1)} %get-tuple-element.34), channel_id=1, source_target_pairs={{0,16},{16,0},{32,48},{48,32},{64,80},{80,64},{96,112},{112,96},{1... | collective-permute-start | bytes 294920 | tf_op jit(solution)/shard_map/ppermute | solution.py:439
  51.0 0.8 collective-permute-start.18
  52.0 1.8 %collective-permute-done.19.zhi = f32[96,128]{1,0:T(8,128)S(1)} collective-permute-done((f32[96,128]{1,0:T(8,128)S(1)}, f32[96,128]{1,0:T(8,128)S(1)}, u32[]{:S(2)}, u32[]{:S(2)}) %collective-permute-start.19) | collective-permute-done | bytes 49184 | tf_op jit(solution)/shard_map/ppermute | solution.py:422
  53.7 1.5 %collective-permute-done.18.zlo = f32[96,128]{1,0:T(8,128)S(1)} collective-permute-done((f32[96,128]{1,0:T(8,128)S(1)}, f32[96,128]{1,0:T(8,128)S(1)}, u32[]{:S(2)}, u32[]{:S(2)}) %collective-permute-start.18) | collective-permute-done | bytes 49184 | tf_op jit(solution)/shard_map/ppermute | solution.py:421
  55.2 1.5 %collective-permute-done.15.xhi = f32[96,128]{1,0:T(8,128)S(1)} collective-permute-done((f32[96,128]{1,0:T(8,128)S(1)}, f32[96,128]{1,0:T(8,128)S(1)}, u32[]{:S(2)}, u32[]{:S(2)}) %collective-permute-start.15) | collective-permute-done | bytes 49184 | tf_op jit(solution)/shard_map/ppermute | solution.py:440
  56.7 9.4 %shard_map.81 = (f32[3072,128]{1,0:T(8,128)}, f32[19,8,128]{2,1,0:T(8,128)S(1)}, bf16[3072,256]{1,0:T(8,128)(2,1)S(1)}) custom-call(f32[168,128]{1,0:T(8,128)S(1)} %collective-permute-done.4.zlo.zlo_p, f32[168,128]{1,0:T(8,128)S(1)} %collective-permute-done.5.zhi.zhi_p, f32[3072,128]{1,0:T(8,128)S(1)} %get-tuple-element.33.rows_ref, ...), custom_call_target="tpu_custom_call" | custom-call | tf_op jit(solution)/shard_map/pallas_call | solution.py:464
  66.1 1.5 %collective-permute-start.20 = (f32[9,8,128]{2,1,0:T(8,128)S(1)}, f32[9,8,128]{2,1,0:T(8,128)S(1)}, u32[]{:S(2)}, u32[]{:S(2)}) collective-permute-start(f32[9,8,128]{2,1,0:T(8,128)S(1)} %get-tuple-element.54), channel_id=1, source_target_pairs={{0,1},{1,2},{2,3},{3,0},{4,5},{5,6},{6,7},{7,4},{8,9},{9,10},{10,1... | collective-permute-start | bytes 110600 | tf_op jit(solution)/shard_map/ppermute | solution.py:421
  67.5 1.2 %collective-permute-start.21 = (f32[9,8,128]{2,1,0:T(8,128)S(1)}, f32[9,8,128]{2,1,0:T(8,128)S(1)}, u32[]{:S(2)}, u32[]{:S(2)}) collective-permute-start(f32[9,8,128]{2,1,0:T(8,128)S(1)} %get-tuple-element.55), channel_id=1, source_target_pairs={{1,0},{2,1},{3,2},{0,3},{5,4},{6,5},{7,6},{4,7},{9,8},{10,9},{11,1... | collective-permute-start | bytes 110600 | tf_op jit(solution)/shard_map/ppermute | solution.py:422
  68.8 3.4 %shard_map.82 = f32[10,8,128]{2,1,0:T(8,128)S(1)} custom-call(f32[72,128]{1,0:T(8,128)S(1)} %bitcast.62, bf16[3072,256]{1,0:T(8,128)(2,1)S(1)} %get-tuple-element.41.field), custom_call_target="tpu_custom_call" | custom-call | flops 4000000000 | bytes 4000000 | tf_op jit(solution)/shard_map/pallas_call | solution.py:464
  72.2 1.7 %collective-permute-start.22 = (f32[3,3,8,128]{3,2,0,1:T(8,128)S(1)}, f32[3,3,8,128]{3,2,0,1:T(8,128)S(1)}, u32[]{:S(2)}, u32[]{:S(2)}) collective-permute-start(f32[3,3,8,128]{3,2,0,1:T(8,128)S(1)} %get-tuple-element.45), channel_id=1, source_target_pairs={{0,4},{4,8},{8,12},{12,0},{1,5},{5,9},{9,13},{13,1},{2,6},{6,10},{... | collective-permute-start | bytes 110600 | tf_op jit(solution)/shard_map/ppermute | solution.py:421
  73.9 1.2 %collective-permute-done.22 = f32[3,3,8,128]{3,2,0,1:T(8,128)S(1)} collective-permute-done((f32[3,3,8,128]{3,2,0,1:T(8,128)S(1)}, f32[3,3,8,128]{3,2,0,1:T(8,128)S(1)}, u32[]{:S(2)}, u32[]{:S(2)}) %collective-permute-start.22) | collective-permute-done | bytes 36896 | tf_op jit(solution)/shard_map/ppermute | solution.py:421
  75.1 1.6 %collective-permute-done.23 = f32[3,3,8,128]{3,2,0,1:T(8,128)S(1)} collective-permute-done((f32[3,3,8,128]{3,2,0,1:T(8,128)S(1)}, f32[3,3,8,128]{3,2,0,1:T(8,128)S(1)}, u32[]{:S(2)}, u32[]{:S(2)}) %collective-permute-start.23) | collective-permute-done | bytes 36896 | tf_op jit(solution)/shard_map/ppermute | solution.py:422
  76.7 10.3 %collective-permute-start.25 = (f32[9,8,128]{2,1,0:T(8,128)S(1)}, f32[9,8,128]{2,1,0:T(8,128)S(1)}, u32[]{:S(2)}, u32[]{:S(2)}) collective-permute-start(f32[9,8,128]{2,1,0:T(8,128)S(1)} %bitcast.76), channel_id=1, source_target_pairs={{16,32},{32,16},{48,64},{64,48},{80,96},{96,80},{112,128},{128,112... | collective-permute-start | bytes 110600 | tf_op jit(solution)/shard_map/ppermute | solution.py:432
  87.0 1.6 %collective-permute-done.25.high_ref = f32[9,8,128]{2,1,0:T(8,128)S(1)} collective-permute-done((f32[9,8,128]{2,1,0:T(8,128)S(1)}, f32[9,8,128]{2,1,0:T(8,128)S(1)}, u32[]{:S(2)}, u32[]{:S(2)}) %collective-permute-start.25) | collective-permute-done | bytes 36896 | tf_op jit(solution)/shard_map/ppermute | solution.py:432
  (47 shorter events, 3.1 us)
Async XLA Ops:
  3.0 1.8 %collective-permute-start = (f32[336,128]{1,0:T(8,128)S(1)}, f32[336,128]{1,0:T(8,128)S(1)}, u32[]{:S(2)}, u32[]{:S(2)}) collective-permute-start(f32[336,128]{1,0:T(8,128)S(1)} %get-tuple-element.22), channel_id=1, source_target_pairs={{0,16},{16,0},{32,48},{48,32},{64,80},{80,64},{96,112},{112,96},{1... | collective-permute-start | bytes 516104 | tf_op jit(solution)/shard_map/ppermute | solution.py:439
  4.8 4.7 %collective-permute-start.1 = (f32[168,128]{1,0:T(8,128)S(1)}, f32[168,128]{1,0:T(8,128)S(1)}, u32[]{:S(2)}, u32[]{:S(2)}) collective-permute-start(f32[168,128]{1,0:T(8,128)S(1)} %slice.81), channel_id=1, source_target_pairs={{0,32},{16,240},{32,64},{48,16},{64,96},{80,48},{96,128},{112,80},... | collective-permute-start | bytes 258056 | tf_op jit(solution)/shard_map/ppermute | solution.py:440
  9.5 3.0 %collective-permute-start.2 = (f32[3,3,8,128]{3,2,0,1:T(8,128)S(1)}, f32[3,3,8,128]{3,2,0,1:T(8,128)S(1)}, u32[]{:S(2)}, u32[]{:S(2)}) collective-permute-start(f32[3,3,8,128]{3,2,0,1:T(8,128)S(1)} %get-tuple-element.51), channel_id=1, source_target_pairs={{0,4},{4,8},{8,12},{12,0},{1,5},{5,9},{9,13},{13,1},{2,6},{6,10},{... | collective-permute-start | bytes 110600 | tf_op jit(solution)/shard_map/ppermute | solution.py:421
  10.8 3.1 %collective-permute-start.3 = (f32[3,3,8,128]{3,2,0,1:T(8,128)S(1)}, f32[3,3,8,128]{3,2,0,1:T(8,128)S(1)}, u32[]{:S(2)}, u32[]{:S(2)}) collective-permute-start(f32[3,3,8,128]{3,2,0,1:T(8,128)S(1)} %get-tuple-element.52), channel_id=1, source_target_pairs={{4,0},{8,4},{12,8},{0,12},{5,1},{9,5},{13,9},{1,13},{6,2},{10,6},{... | collective-permute-start | bytes 110600 | tf_op jit(solution)/shard_map/ppermute | solution.py:422
  11.1 8.9 %collective-permute-start.6 = (f32[384,128]{1,0:T(8,128)S(1)}, f32[384,128]{1,0:T(8,128)S(1)}, u32[]{:S(2)}, u32[]{:S(2)}) collective-permute-start(f32[384,128]{1,0:T(8,128)S(1)} %get-tuple-element.25), channel_id=1, source_target_pairs={{0,4},{4,8},{8,12},{12,0},{1,5},{5,9},{9,13},{13,1},{2,6},{6,10},{... | collective-permute-start | bytes 589832 | tf_op jit(solution)/shard_map/ppermute | solution.py:421
  12.3 7.7 %collective-permute-start.7 = (f32[384,128]{1,0:T(8,128)S(1)}, f32[384,128]{1,0:T(8,128)S(1)}, u32[]{:S(2)}, u32[]{:S(2)}) collective-permute-start(f32[384,128]{1,0:T(8,128)S(1)} %get-tuple-element.26), channel_id=1, source_target_pairs={{4,0},{8,4},{12,8},{0,12},{5,1},{9,5},{13,9},{1,13},{6,2},{10,6},{... | collective-permute-start | bytes 589832 | tf_op jit(solution)/shard_map/ppermute | solution.py:422
  14.0 6.0 %collective-permute-start.5 = (f32[168,128]{1,0:T(8,128)S(1)}, f32[168,128]{1,0:T(8,128)S(1)}, u32[]{:S(2)}, u32[]{:S(2)}) collective-permute-start(f32[168,128]{1,0:T(8,128)S(1)} %get-tuple-element.56), channel_id=1, source_target_pairs={{1,0},{2,1},{3,2},{0,3},{5,4},{6,5},{7,6},{4,7},{9,8},{10,9},{11,1... | collective-permute-start | bytes 258056 | tf_op jit(solution)/shard_map/ppermute | solution.py:422
  16.8 4.5 %collective-permute-start.4 = (f32[168,128]{1,0:T(8,128)S(1)}, f32[168,128]{1,0:T(8,128)S(1)}, u32[]{:S(2)}, u32[]{:S(2)}) collective-permute-start(f32[168,128]{1,0:T(8,128)S(1)} %get-tuple-element.57), channel_id=1, source_target_pairs={{0,1},{1,2},{2,3},{3,0},{4,5},{5,6},{6,7},{7,4},{8,9},{9,10},{10,1... | collective-permute-start | bytes 258056 | tf_op jit(solution)/shard_map/ppermute | solution.py:421
  16.8 4.5 %copy-start = (f32[3,64,16,128]{3,2,1,0:T(8,128)S(1)}, f32[3,64,16,128]{3,2,1,0:T(8,128)}, u32[]{:S(2)}) copy-start(f32[3,64,16,128]{3,2,1,0:T(8,128)} %param.6) | copy-start | bytes 4718596
  16.8 4.5 %copy-start.1 = (f32[64,16,128]{2,1,0:T(8,128)S(1)}, f32[64,16,128]{2,1,0:T(8,128)}, u32[]{:S(2)}) copy-start(f32[64,16,128]{2,1,0:T(8,128)} %param.7) | copy-start | bytes 1572868
  29.8 12.2 %collective-permute-start.10 = (f32[384,128]{1,0:T(8,128)S(1)}, f32[384,128]{1,0:T(8,128)S(1)}, u32[]{:S(2)}, u32[]{:S(2)}) collective-permute-start(f32[384,128]{1,0:T(8,128)S(1)} %get-tuple-element.30), channel_id=1, source_target_pairs={{0,4},{4,8},{8,12},{12,0},{1,5},{5,9},{9,13},{13,1},{2,6},{6,10},{... | collective-permute-start | bytes 589832 | tf_op jit(solution)/shard_map/ppermute | solution.py:421
  29.8 12.1 %collective-permute-start.11 = (f32[384,128]{1,0:T(8,128)S(1)}, f32[384,128]{1,0:T(8,128)S(1)}, u32[]{:S(2)}, u32[]{:S(2)}) collective-permute-start(f32[384,128]{1,0:T(8,128)S(1)} %get-tuple-element.31), channel_id=1, source_target_pairs={{4,0},{8,4},{12,8},{0,12},{5,1},{9,5},{13,9},{1,13},{6,2},{10,6},{... | collective-permute-start | bytes 589832 | tf_op jit(solution)/shard_map/ppermute | solution.py:422
  31.3 5.0 %collective-permute-start.8 = (f32[192,128]{1,0:T(8,128)S(1)}, f32[192,128]{1,0:T(8,128)S(1)}, u32[]{:S(2)}, u32[]{:S(2)}) collective-permute-start(f32[192,128]{1,0:T(8,128)S(1)} %get-tuple-element.29), channel_id=1, source_target_pairs={{0,16},{16,0},{32,48},{48,32},{64,80},{80,64},{96,112},{112,96},{1... | collective-permute-start | bytes 294920 | tf_op jit(solution)/shard_map/ppermute | solution.py:439
  34.8 3.3 %collective-permute-start.13 = (f32[96,128]{1,0:T(8,128)S(1)}, f32[96,128]{1,0:T(8,128)S(1)}, u32[]{:S(2)}, u32[]{:S(2)}) collective-permute-start(f32[96,128]{1,0:T(8,128)S(1)} %get-tuple-element.32), channel_id=1, source_target_pairs={{1,0},{2,1},{3,2},{0,3},{5,4},{6,5},{7,6},{4,7},{9,8},{10,9},{11,1... | collective-permute-start | bytes 147464 | tf_op jit(solution)/shard_map/ppermute | solution.py:422
  36.3 4.2 %collective-permute-start.12 = (f32[96,128]{1,0:T(8,128)S(1)}, f32[96,128]{1,0:T(8,128)S(1)}, u32[]{:S(2)}, u32[]{:S(2)}) collective-permute-start(f32[96,128]{1,0:T(8,128)S(1)} %get-tuple-element.32), channel_id=1, source_target_pairs={{0,1},{1,2},{2,3},{3,0},{4,5},{5,6},{6,7},{7,4},{8,9},{9,10},{10,1... | collective-permute-start | bytes 147464 | tf_op jit(solution)/shard_map/ppermute | solution.py:421
  36.3 5.6 %collective-permute-start.9 = (f32[96,128]{1,0:T(8,128)S(1)}, f32[96,128]{1,0:T(8,128)S(1)}, u32[]{:S(2)}, u32[]{:S(2)}) collective-permute-start(f32[96,128]{1,0:T(8,128)S(1)} %slice.89), channel_id=1, source_target_pairs={{0,32},{16,240},{32,64},{48,16},{64,96},{80,48},{96,128},{112,80},... | collective-permute-start | bytes 147464 | tf_op jit(solution)/shard_map/ppermute | solution.py:440
  47.2 9.5 %collective-permute-start.16 = (f32[384,128]{1,0:T(8,128)S(1)}, f32[384,128]{1,0:T(8,128)S(1)}, u32[]{:S(2)}, u32[]{:S(2)}) collective-permute-start(f32[384,128]{1,0:T(8,128)S(1)} %get-tuple-element.35), channel_id=1, source_target_pairs={{0,4},{4,8},{8,12},{12,0},{1,5},{5,9},{9,13},{13,1},{2,6},{6,10},{... | collective-permute-start | bytes 589832 | tf_op jit(solution)/shard_map/ppermute | solution.py:421
  49.0 7.7 %collective-permute-start.17 = (f32[384,128]{1,0:T(8,128)S(1)}, f32[384,128]{1,0:T(8,128)S(1)}, u32[]{:S(2)}, u32[]{:S(2)}) collective-permute-start(f32[384,128]{1,0:T(8,128)S(1)} %get-tuple-element.36), channel_id=1, source_target_pairs={{4,0},{8,4},{12,8},{0,12},{5,1},{9,5},{13,9},{1,13},{6,2},{10,6},{... | collective-permute-start | bytes 589832 | tf_op jit(solution)/shard_map/ppermute | solution.py:422
  49.0 2.9 %collective-permute-start.14 = (f32[192,128]{1,0:T(8,128)S(1)}, f32[192,128]{1,0:T(8,128)S(1)}, u32[]{:S(2)}, u32[]{:S(2)}) collective-permute-start(f32[192,128]{1,0:T(8,128)S(1)} %get-tuple-element.34), channel_id=1, source_target_pairs={{0,16},{16,0},{32,48},{48,32},{64,80},{80,64},{96,112},{112,96},{1... | collective-permute-start | bytes 294920 | tf_op jit(solution)/shard_map/ppermute | solution.py:439
  50.4 3.3 %collective-permute-start.19 = (f32[96,128]{1,0:T(8,128)S(1)}, f32[96,128]{1,0:T(8,128)S(1)}, u32[]{:S(2)}, u32[]{:S(2)}) collective-permute-start(f32[96,128]{1,0:T(8,128)S(1)} %get-tuple-element.37), channel_id=1, source_target_pairs={{1,0},{2,1},{3,2},{0,3},{5,4},{6,5},{7,6},{4,7},{9,8},{10,9},{11,1... | collective-permute-start | bytes 147464 | tf_op jit(solution)/shard_map/ppermute | solution.py:422
  51.0 4.2 %collective-permute-start.18 = (f32[96,128]{1,0:T(8,128)S(1)}, f32[96,128]{1,0:T(8,128)S(1)}, u32[]{:S(2)}, u32[]{:S(2)}) collective-permute-start(f32[96,128]{1,0:T(8,128)S(1)} %get-tuple-element.37), channel_id=1, source_target_pairs={{0,1},{1,2},{2,3},{3,0},{4,5},{5,6},{6,7},{7,4},{8,9},{9,10},{10,1... | collective-permute-start | bytes 147464 | tf_op jit(solution)/shard_map/ppermute | solution.py:421
  51.9 4.8 %collective-permute-start.15 = (f32[96,128]{1,0:T(8,128)S(1)}, f32[96,128]{1,0:T(8,128)S(1)}, u32[]{:S(2)}, u32[]{:S(2)}) collective-permute-start(f32[96,128]{1,0:T(8,128)S(1)} %slice.90), channel_id=1, source_target_pairs={{0,32},{16,240},{32,64},{48,16},{64,96},{80,48},{96,128},{112,80},... | collective-permute-start | bytes 147464 | tf_op jit(solution)/shard_map/ppermute | solution.py:440
  66.1 6.1 %collective-permute-start.20 = (f32[9,8,128]{2,1,0:T(8,128)S(1)}, f32[9,8,128]{2,1,0:T(8,128)S(1)}, u32[]{:S(2)}, u32[]{:S(2)}) collective-permute-start(f32[9,8,128]{2,1,0:T(8,128)S(1)} %get-tuple-element.54), channel_id=1, source_target_pairs={{0,1},{1,2},{2,3},{3,0},{4,5},{5,6},{6,7},{7,4},{8,9},{9,10},{10,1... | collective-permute-start | bytes 110600 | tf_op jit(solution)/shard_map/ppermute | solution.py:421
  67.5 4.6 %collective-permute-start.21 = (f32[9,8,128]{2,1,0:T(8,128)S(1)}, f32[9,8,128]{2,1,0:T(8,128)S(1)}, u32[]{:S(2)}, u32[]{:S(2)}) collective-permute-start(f32[9,8,128]{2,1,0:T(8,128)S(1)} %get-tuple-element.55), channel_id=1, source_target_pairs={{1,0},{2,1},{3,2},{0,3},{5,4},{6,5},{7,6},{4,7},{9,8},{10,9},{11,1... | collective-permute-start | bytes 110600 | tf_op jit(solution)/shard_map/ppermute | solution.py:422
  72.2 2.9 %collective-permute-start.22 = (f32[3,3,8,128]{3,2,0,1:T(8,128)S(1)}, f32[3,3,8,128]{3,2,0,1:T(8,128)S(1)}, u32[]{:S(2)}, u32[]{:S(2)}) collective-permute-start(f32[3,3,8,128]{3,2,0,1:T(8,128)S(1)} %get-tuple-element.45), channel_id=1, source_target_pairs={{0,4},{4,8},{8,12},{12,0},{1,5},{5,9},{9,13},{13,1},{2,6},{6,10},{... | collective-permute-start | bytes 110600 | tf_op jit(solution)/shard_map/ppermute | solution.py:421
  73.9 2.8 %collective-permute-start.23 = (f32[3,3,8,128]{3,2,0,1:T(8,128)S(1)}, f32[3,3,8,128]{3,2,0,1:T(8,128)S(1)}, u32[]{:S(2)}, u32[]{:S(2)}) collective-permute-start(f32[3,3,8,128]{3,2,0,1:T(8,128)S(1)} %get-tuple-element.46), channel_id=1, source_target_pairs={{4,0},{8,4},{12,8},{0,12},{5,1},{9,5},{13,9},{1,13},{6,2},{10,6},{... | collective-permute-start | bytes 110600 | tf_op jit(solution)/shard_map/ppermute | solution.py:422
  76.7 11.9 %collective-permute-start.25 = (f32[9,8,128]{2,1,0:T(8,128)S(1)}, f32[9,8,128]{2,1,0:T(8,128)S(1)}, u32[]{:S(2)}, u32[]{:S(2)}) collective-permute-start(f32[9,8,128]{2,1,0:T(8,128)S(1)} %bitcast.76), channel_id=1, source_target_pairs={{16,32},{32,16},{48,64},{64,48},{80,96},{96,80},{112,128},{128,112... | collective-permute-start | bytes 110600 | tf_op jit(solution)/shard_map/ppermute | solution.py:432
  87.0 1.6 %collective-permute-start.24 = (f32[9,8,128]{2,1,0:T(8,128)S(1)}, f32[9,8,128]{2,1,0:T(8,128)S(1)}, u32[]{:S(2)}, u32[]{:S(2)}) collective-permute-start(f32[9,8,128]{2,1,0:T(8,128)S(1)} %bitcast.74), channel_id=1, source_target_pairs={{0,16},{16,0},{32,48},{48,32},{64,80},{80,64},{96,112},{112,96},{1... | collective-permute-start | bytes 110600 | tf_op jit(solution)/shard_map/ppermute | solution.py:432

commit v5 on v3

--- a/solution.py
+++ b/solution.py
@@ -6,6 +6,7 @@
 from jax.experimental import pallas as pl
 from jax.experimental.pallas import tpu as pltpu
 from jax.sharding import PartitionSpec as P
+
 
 DT = 0.1
 CI, CJ, CK = 64, 16, 128
@@ -157,15 +158,15 @@
     return high, (value - high.astype(F32)).astype(BF16)
 
 
-def gather_slots(refs, slots, order):
+def gather_slots(refs, slots, order, picks=tuple(range(9))):
     filled = jnp.zeros((1, CAP), jnp.int32)
     for group, ref in enumerate(refs):
-        for t in range(9):
-            s = group * 9 + t
+        for n, t in enumerate(picks):
+            s = group * len(picks) + n
             value = ref[t * 8 : (t + 1) * 8, :]
             slots[s] = value
             filled = filled + jnp.where(value[7:8, :] > 0.5, 1 << s, 0)
-    total = 9 * len(refs)
+    total = len(picks) * len(refs)
     slots[total] = jnp.zeros((8, CAP), F32)
     mask = jnp.max(filled)
     count = jnp.int32(0)
@@ -343,8 +344,8 @@
     spread(slots, order, gather_slots((mid_ref,), slots, order), plane, forcing_ref)
 
 
-def middle_sample_kernel(mid_ref, field, sampled_ref, slots, order):
-    count = gather_slots((mid_ref,), slots, order)
+def middle_sample_kernel(picks, mid_ref, field, sampled_ref, slots, order):
+    count = gather_slots((mid_ref,), slots, order, picks)
     sampled_ref[...] = jnp.zeros_like(sampled_ref)
     sample(slots, order, count, field, sampled_ref)
 
@@ -387,6 +388,7 @@
         1.0 / 3.0, 2.0 / 3.0, rows_ref, base_ref, visc_ref, forcing_ref,
         (xlo, xhi, ylo, yhi, zlo, zhi), padded, zsc, out_ref,
     )
+
     def split(t, carry):
         first = pl.multiple_of(t * 256, 256)
         high, low = halves(out_ref[pl.ds(first, 256), :])
@@ -416,7 +418,9 @@
     count = lax.axis_size(axis)
     up = [(i, (i + 1) % count) for i in range(count)]
     down = [(target, source) for source, target in up]
-    return lax.ppermute(forward, axis, up), lax.ppermute(backward, axis, down)
+    low = lax.ppermute(forward, axis, up)
+    high = lax.ppermute(backward, axis, down)
+    return low, high
 
 
 def swapped(first, second, axis):
@@ -493,13 +497,13 @@
     held = jnp.stack([from_low, held[:, 1], from_high])
     mine = held[:, :, 1].reshape(SLOT_ROWS, CAP)
     zlo, zhi = exchanged(
-        jnp.concatenate([held[:, :, 2].reshape(SLOT_ROWS, CAP), zp]),
-        jnp.concatenate([held[:, :, 0].reshape(SLOT_ROWS, CAP), zp]),
-        "gz",
+      jnp.concatenate([held[:, :, 2].reshape(SLOT_ROWS, CAP), zp]),
+      jnp.concatenate([held[:, :, 0].reshape(SLOT_ROWS, CAP), zp]),
+      "gz",
     )
     cost = pl.CostEstimate(flops=4_000_000_000, bytes_accessed=4_000_000, transcendentals=200_000)
     part = call(
-        middle_spread_kernel, shape(NS * CJ, CK), SLOT_SCRATCH + [PLANE], mine, cost=cost
+      middle_spread_kernel, shape(NS * CJ, CK), SLOT_SCRATCH + [PLANE], mine, cost=cost
     )
 
     section_one, forcing, *faces = call(
@@ -522,13 +526,20 @@
         zlo, zhi, section_two, rows, visc, forcing, *halos_of(*faces),
     )
 
-    from_low, from_high = exchanged(sampled[9:18], sampled[:9], "gz")
-    middle = call(
-        middle_sample_kernel, shape(10, 8, CAP), SLOT_SCRATCH, mine, field, cost=cost
-    )
-    held = jnp.stack([from_low, middle[:9], from_high]).reshape(3, 3, 3, 8, CAP)
-    from_low, from_high = exchanged(held[:, 2], held[:, 0], "gy")
-    held = jnp.stack([from_low, held[:, 1], from_high])
+    def middle(picks, blocks):
+        return call(
+            functools.partial(middle_sample_kernel, picks),
+            shape(len(picks) + 1, 8, CAP), SLOT_SCRATCH, blocks, field, cost=cost,
+        )
+
+    outer = middle((0, 1, 2, 6, 7, 8), mine)
+    low, high = exchanged(sampled[9:18], sampled[:9], "gz")
+    low, high, after = lax.optimization_barrier((low, high, mine))
+    up, down = (jnp.stack([low[t : t + 3], outer[n : n + 3], high[t : t + 3]]) for t, n in ((6, 3), (0, 0)))
+    from_low, from_high = exchanged(up, down, "gy")
+    inner = middle((3, 4, 5), after)
+    centre = jnp.stack([low[3:6], inner[:3], high[3:6]])
+    held = jnp.stack([from_low, centre, from_high])
     mine = held[:, :, 1].reshape(9, 8, CAP)
     from_first, from_second = swapped(
         held[:, :, 0].reshape(9, 8, CAP), held[:, :, 2].reshape(9, 8, CAP), "gx"
@@ -550,6 +561,5 @@
         P(("gx", "gy", "gz"), None),
     )
     out_specs = (P(None, "gx", "gy", "gz"), P(None, ("gx", "gy", "gz")))
-    return jax.shard_map(
-        per_device, mesh=mesh, in_specs=in_specs, out_specs=out_specs, check_vma=False
-    )
+
+    return jax.shard_map(per_device, mesh=mesh, in_specs=in_specs, out_specs=out_specs, check_vma=False)

time: 85.7 us -> 86.9 us (1.014)
  the two profiles are of different devices: /device:TPU:30 before, /device:TPU:1 now
where the time goes in v5:
time: 86.9 us; the launch traced here: 86.8 us
  starting transfers between devices  36.3 us (42%)
  Pallas kernels  30.7 us (35%)
  waiting for transfers between devices  18.8 us (22%)
    pallas_call x8, Pallas kernels, call(): pl.pallas_call(kernel, out_shape=outs, in_specs=[pl.BlockSpec(memory_spac...  30.7 us
    ppermute x4, starting transfers between devices, swapped(): lax.ppermute(first, axis, pairs[0])  13.5 us
    ppermute x9, starting transfers between devices, exchanged(): high = lax.ppermute(backward, axis, down)  12 us
    ppermute x4, waiting for transfers between devices, swapped(): lax.ppermute(second, axis, pairs[1])  7.4 us
    ppermute x9, starting transfers between devices, exchanged(): low = lax.ppermute(forward, axis, up)  7.31 us
    ppermute x9, waiting for transfers between devices, exchanged(): low = lax.ppermute(forward, axis, up)  6.34 us
    ppermute x4, starting transfers between devices, swapped(): lax.ppermute(second, axis, pairs[1])  3.41 us
    ppermute x9, waiting for transfers between devices, exchanged(): high = lax.ppermute(backward, axis, down)  3.14 us
  transfers between devices with their start and end apart: 26, of which 15 were waited for; matrix products, arithmetic and copies ran while one was open for 0% of the time, Pallas kernels for 4%

profile of v5, /device:TPU:1, one launch (start us, length us, event | category | flops | bytes accessed | tf_op | source)
XLA Modules:
  0.0 86.8 jit_solution(13237802931852219953)
XLA Ops:
  0.6 2.3 %shard_map.77 = (f32[72,128]{1,0:T(8,128)S(1)}, s32[8,128]{1,0:T(8,128)S(1)}, f32[168,128]{1,0:T(8,128)S(1)}, f32[168,128]{1,0:T(8,128)S(1)}, f32[384,128]{1,0:T...) custom-call(s32[1024]{0:T(1024)} %bitcast.76, f32[3,1024]{1,0:T(4,128)} %force_any.1, f32[3,1024]{1,0:T(4,128)} %offset_any.1, ...), custom_call_target="tpu_custom_call" | custom-call | tf_op jit(solution)/shard_map/pallas_call | solution.py:456
  3.0 3.3 %collective-permute-start = (f32[168,128]{1,0:T(8,128)S(1)}, f32[168,128]{1,0:T(8,128)S(1)}, u32[]{:S(2)}, u32[]{:S(2)}) collective-permute-start(f32[168,128]{1,0:T(8,128)S(1)} %get-tuple-element.28), channel_id=1, source_target_pairs={{0,16},{16,0},{32,48},{48,32},{64,80},{80,64},{96,112},{112,96},{1... | collective-permute-start | bytes 258056 | tf_op jit(solution)/shard_map/ppermute | solution.py:432
  6.2 0.9 %collective-permute-done.xlo = f32[168,128]{1,0:T(8,128)S(1)} collective-permute-done((f32[168,128]{1,0:T(8,128)S(1)}, f32[168,128]{1,0:T(8,128)S(1)}, u32[]{:S(2)}, u32[]{:S(2)}) %collective-permute-start) | collective-permute-done | bytes 86048 | tf_op jit(solution)/shard_map/ppermute | solution.py:432
  7.2 3.0 %collective-permute-done.1.xhi = f32[168,128]{1,0:T(8,128)S(1)} collective-permute-done((f32[168,128]{1,0:T(8,128)S(1)}, f32[168,128]{1,0:T(8,128)S(1)}, u32[]{:S(2)}, u32[]{:S(2)}) %collective-permute-start.1) | collective-permute-done | bytes 86048 | tf_op jit(solution)/shard_map/ppermute | solution.py:432
  10.3 2.7 %collective-permute-start.3 = (f32[3,3,8,128]{3,2,0,1:T(8,128)S(1)}, f32[3,3,8,128]{3,2,0,1:T(8,128)S(1)}, u32[]{:S(2)}, u32[]{:S(2)}) collective-permute-start(f32[3,3,8,128]{3,2,0,1:T(8,128)S(1)} %get-tuple-element.61), channel_id=1, source_target_pairs={{4,0},{8,4},{12,8},{0,12},{5,1},{9,5},{13,9},{1,13},{6,2},{10,6},{... | collective-permute-start | bytes 110600 | tf_op jit(solution)/shard_map/ppermute | solution.py:422
  12.9 2.7 %collective-permute-start.7 = (f32[384,128]{1,0:T(8,128)S(1)}, f32[384,128]{1,0:T(8,128)S(1)}, u32[]{:S(2)}, u32[]{:S(2)}) collective-permute-start(f32[384,128]{1,0:T(8,128)S(1)} %get-tuple-element.33), channel_id=1, source_target_pairs={{4,0},{8,4},{12,8},{0,12},{5,1},{9,5},{13,9},{1,13},{6,2},{10,6},{... | collective-permute-start | bytes 589832 | tf_op jit(solution)/shard_map/ppermute | solution.py:422
  15.7 1.1 %collective-permute-start.5 = (f32[168,128]{1,0:T(8,128)S(1)}, f32[168,128]{1,0:T(8,128)S(1)}, u32[]{:S(2)}, u32[]{:S(2)}) collective-permute-start(f32[168,128]{1,0:T(8,128)S(1)} %get-tuple-element.65), channel_id=1, source_target_pairs={{1,0},{2,1},{3,2},{0,3},{5,4},{6,5},{7,6},{4,7},{9,8},{10,9},{11,1... | collective-permute-start | bytes 258056 | tf_op jit(solution)/shard_map/ppermute | solution.py:422
  17.2 3.2 %shard_map.78.part_ref = f32[3072,128]{1,0:T(8,128)S(1)} custom-call(f32[72,128]{1,0:T(8,128)S(1)} %bitcast.62), custom_call_target="tpu_custom_call" | custom-call | flops 4000000000 | bytes 4000000 | tf_op jit(solution)/shard_map/pallas_call | solution.py:456
  20.5 1.2 %collective-permute-done.4.zlo.zlo_p = f32[168,128]{1,0:T(8,128)S(1)} collective-permute-done((f32[168,128]{1,0:T(8,128)S(1)}, f32[168,128]{1,0:T(8,128)S(1)}, u32[]{:S(2)}, u32[]{:S(2)}) %collective-permute-start.4) | collective-permute-done | bytes 86048 | tf_op jit(solution)/shard_map/ppermute | solution.py:421
  21.6 7.4 %shard_map.79 = (f32[3072,128]{1,0:T(8,128)S(1)}, f32[3072,128]{1,0:T(8,128)S(1)}, f32[96,128]{1,0:T(8,128)S(1)}, f32[96,128]{1,0:T(8,128)S(1)}, f32[384,128]{1,...) custom-call(f32[168,128]{1,0:T(8,128)S(1)} %collective-permute-done.4.zlo.zlo_p, ...), custom_call_target="tpu_custom_call" | custom-call | tf_op jit(solution)/shard_map/pallas_call | solution.py:456
  29.2 2.7 %collective-permute-start.11 = (f32[384,128]{1,0:T(8,128)S(1)}, f32[384,128]{1,0:T(8,128)S(1)}, u32[]{:S(2)}, u32[]{:S(2)}) collective-permute-start(f32[384,128]{1,0:T(8,128)S(1)} %get-tuple-element.39), channel_id=1, source_target_pairs={{4,0},{8,4},{12,8},{0,12},{5,1},{9,5},{13,9},{1,13},{6,2},{10,6},{... | collective-permute-start | bytes 589832 | tf_op jit(solution)/shard_map/ppermute | solution.py:422
  31.8 5.1 %collective-permute-start.8 = (f32[96,128]{1,0:T(8,128)S(1)}, f32[96,128]{1,0:T(8,128)S(1)}, u32[]{:S(2)}, u32[]{:S(2)}) collective-permute-start(f32[96,128]{1,0:T(8,128)S(1)} %get-tuple-element.36), channel_id=1, source_target_pairs={{0,16},{16,0},{32,48},{48,32},{64,80},{80,64},{96,112},{112,96},{1... | collective-permute-start | bytes 147464 | tf_op jit(solution)/shard_map/ppermute | solution.py:432
  37.8 2.5 %collective-permute-start.12 = (f32[96,128]{1,0:T(8,128)S(1)}, f32[96,128]{1,0:T(8,128)S(1)}, u32[]{:S(2)}, u32[]{:S(2)}) collective-permute-start(f32[96,128]{1,0:T(8,128)S(1)} %get-tuple-element.40), channel_id=1, source_target_pairs={{0,1},{1,2},{2,3},{3,0},{4,5},{5,6},{6,7},{7,4},{8,9},{9,10},{10,1... | collective-permute-start | bytes 147464 | tf_op jit(solution)/shard_map/ppermute | solution.py:421
  41.1 1.1 %collective-permute-done.12.zlo = f32[96,128]{1,0:T(8,128)S(1)} collective-permute-done((f32[96,128]{1,0:T(8,128)S(1)}, f32[96,128]{1,0:T(8,128)S(1)}, u32[]{:S(2)}, u32[]{:S(2)}) %collective-permute-start.12) | collective-permute-done | bytes 49184 | tf_op jit(solution)/shard_map/ppermute | solution.py:421
  42.2 5.2 %shard_map.80 = (f32[3072,128]{1,0:T(8,128)S(1)}, f32[96,128]{1,0:T(8,128)S(1)}, f32[96,128]{1,0:T(8,128)S(1)}, f32[384,128]{1,0:T(8,128)S(1)}, f32[384,128]{1,0:T(8,128)S(1)}, /*index=5*/f32[96,128]{1,0:T(8,128)S(1)}) custom-call(f32[3072,128]{1,0:T(8,128)S(1)} %get-tuple-element.34.rows_ref, f32[3072,128]{1,0:T(8,128)S(1)} %bitcast.56, ...), custom_call_target="tpu_custom_call" | custom-call | tf_op jit(solution)/shard_map/pallas_call | solution.py:456
  48.1 2.0 %collective-permute-start.17 = (f32[384,128]{1,0:T(8,128)S(1)}, f32[384,128]{1,0:T(8,128)S(1)}, u32[]{:S(2)}, u32[]{:S(2)}) collective-permute-start(f32[384,128]{1,0:T(8,128)S(1)} %get-tuple-element.45), channel_id=1, source_target_pairs={{4,0},{8,4},{12,8},{0,12},{5,1},{9,5},{13,9},{1,13},{6,2},{10,6},{... | collective-permute-start | bytes 589832 | tf_op jit(solution)/shard_map/ppermute | solution.py:422
  50.2 5.2 %collective-permute-start.14 = (f32[96,128]{1,0:T(8,128)S(1)}, f32[96,128]{1,0:T(8,128)S(1)}, u32[]{:S(2)}, u32[]{:S(2)}) collective-permute-start(f32[96,128]{1,0:T(8,128)S(1)} %get-tuple-element.42), channel_id=1, source_target_pairs={{0,16},{16,0},{32,48},{48,32},{64,80},{80,64},{96,112},{112,96},{1... | collective-permute-start | bytes 147464 | tf_op jit(solution)/shard_map/ppermute | solution.py:432
  55.4 0.9 %collective-permute-done.14.xlo = f32[96,128]{1,0:T(8,128)S(1)} collective-permute-done((f32[96,128]{1,0:T(8,128)S(1)}, f32[96,128]{1,0:T(8,128)S(1)}, u32[]{:S(2)}, u32[]{:S(2)}) %collective-permute-start.14) | collective-permute-done | bytes 49184 | tf_op jit(solution)/shard_map/ppermute | solution.py:432
  56.8 2.3 %collective-permute-done.15.xhi = f32[96,128]{1,0:T(8,128)S(1)} collective-permute-done((f32[96,128]{1,0:T(8,128)S(1)}, f32[96,128]{1,0:T(8,128)S(1)}, u32[]{:S(2)}, u32[]{:S(2)}) %collective-permute-start.15) | collective-permute-done | bytes 49184 | tf_op jit(solution)/shard_map/ppermute | solution.py:432
  59.2 1.2 %collective-permute-done.18.zlo = f32[96,128]{1,0:T(8,128)S(1)} collective-permute-done((f32[96,128]{1,0:T(8,128)S(1)}, f32[96,128]{1,0:T(8,128)S(1)}, u32[]{:S(2)}, u32[]{:S(2)}) %collective-permute-start.18) | collective-permute-done | bytes 49184 | tf_op jit(solution)/shard_map/ppermute | solution.py:421
  60.4 8.3 %shard_map.81 = (f32[3072,128]{1,0:T(8,128)}, f32[19,8,128]{2,1,0:T(8,128)S(1)}, bf16[3072,256]{1,0:T(8,128)(2,1)S(1)}) custom-call(f32[168,128]{1,0:T(8,128)S(1)} %collective-permute-done.4.zlo.zlo_p, f32[168,128]{1,0:T(8,128)S(1)} %collective-permute-done.5.zhi.zhi_p, f32[3072,128]{1,0:T(8,128)S(1)} %get-tuple-element.41.rows_ref, ...), custom_call_target="tpu_custom_call" | custom-call | tf_op jit(solution)/shard_map/pallas_call | solution.py:456
  68.6 1.3 %shard_map.82 = f32[7,8,128]{2,1,0:T(8,128)S(1)} custom-call(f32[72,128]{1,0:T(8,128)S(1)} %bitcast.63, bf16[3072,256]{1,0:T(8,128)(2,1)S(1)} %get-tuple-element.51.field), custom_call_target="tpu_custom_call" | custom-call | flops 4000000000 | bytes 4000000 | tf_op jit(solution)/shard_map/pallas_call | solution.py:456
  70.0 1.5 %collective-permute-start.20 = (f32[9,8,128]{2,1,0:T(8,128)S(1)}, f32[9,8,128]{2,1,0:T(8,128)S(1)}, u32[]{:S(2)}, u32[]{:S(2)}) collective-permute-start(f32[9,8,128]{2,1,0:T(8,128)S(1)} %get-tuple-element.64), channel_id=1, source_target_pairs={{0,1},{1,2},{2,3},{3,0},{4,5},{5,6},{6,7},{7,4},{8,9},{9,10},{10,1... | collective-permute-start | bytes 110600 | tf_op jit(solution)/shard_map/ppermute | solution.py:421
  71.5 1.3 %collective-permute-done.21 = f32[9,8,128]{2,1,0:T(8,128)S(1)} collective-permute-done((f32[9,8,128]{2,1,0:T(8,128)S(1)}, f32[9,8,128]{2,1,0:T(8,128)S(1)}, u32[]{:S(2)}, u32[]{:S(2)}) %collective-permute-start.21) | collective-permute-done | bytes 36896 | tf_op jit(solution)/shard_map/ppermute | solution.py:422
  72.8 1.3 %collective-permute-done.20 = f32[9,8,128]{2,1,0:T(8,128)S(1)} collective-permute-done((f32[9,8,128]{2,1,0:T(8,128)S(1)}, f32[9,8,128]{2,1,0:T(8,128)S(1)}, u32[]{:S(2)}, u32[]{:S(2)}) %collective-permute-start.20) | collective-permute-done | bytes 36896 | tf_op jit(solution)/shard_map/ppermute | solution.py:421
  74.1 2.3 %shard_map.83 = f32[4,8,128]{2,1,0:T(8,128)S(1)} custom-call(f32[72,128]{1,0:T(8,128)S(1)} %bitcast.64, bf16[3072,256]{1,0:T(8,128)(2,1)S(1)} %get-tuple-element.51.field), custom_call_target="tpu_custom_call" | custom-call | flops 4000000000 | bytes 4000000 | tf_op jit(solution)/shard_map/pallas_call | solution.py:456
  76.6 1.4 %collective-permute-start.22 = (f32[3,3,8,128]{3,2,1,0:T(8,128)S(1)}, f32[3,3,8,128]{3,2,1,0:T(8,128)S(1)}, u32[]{:S(2)}, u32[]{:S(2)}) collective-permute-start(f32[3,3,8,128]{3,2,1,0:T(8,128)S(1)} %pad_maximum_fusion.5), channel_id=1, source_target_pairs={{0,4},{4,8},{8,12},{12,0},{1,5},{5,9},{9,13},{13,1},{2,6},{6,10},{... | collective-permute-start | bytes 110600 | tf_op jit(solution)/shard_map/ppermute | solution.py:421
  78.1 1.3 %collective-permute-done.23 = f32[3,3,8,128]{3,2,1,0:T(8,128)S(1)} collective-permute-done((f32[3,3,8,128]{3,2,1,0:T(8,128)S(1)}, f32[3,3,8,128]{3,2,1,0:T(8,128)S(1)}, u32[]{:S(2)}, u32[]{:S(2)}) %collective-permute-start.23) | collective-permute-done | bytes 36896 | tf_op jit(solution)/shard_map/ppermute | solution.py:422
  79.4 1.6 %collective-permute-done.22 = f32[3,3,8,128]{3,2,1,0:T(8,128)S(1)} collective-permute-done((f32[3,3,8,128]{3,2,1,0:T(8,128)S(1)}, f32[3,3,8,128]{3,2,1,0:T(8,128)S(1)}, u32[]{:S(2)}, u32[]{:S(2)}) %collective-permute-start.22) | collective-permute-done | bytes 36896 | tf_op jit(solution)/shard_map/ppermute | solution.py:421
  81.0 3.4 %collective-permute-start.25 = (f32[9,8,128]{2,1,0:T(8,128)S(1)}, f32[9,8,128]{2,1,0:T(8,128)S(1)}, u32[]{:S(2)}, u32[]{:S(2)}) collective-permute-start(f32[9,8,128]{2,1,0:T(8,128)S(1)} %bitcast.75), channel_id=1, source_target_pairs={{16,32},{32,16},{48,64},{64,48},{80,96},{96,80},{112,128},{128,112... | collective-permute-start | bytes 110600 | tf_op jit(solution)/shard_map/ppermute | solution.py:432
  84.4 1.6 %collective-permute-done.25.high_ref = f32[9,8,128]{2,1,0:T(8,128)S(1)} collective-permute-done((f32[9,8,128]{2,1,0:T(8,128)S(1)}, f32[9,8,128]{2,1,0:T(8,128)S(1)}, u32[]{:S(2)}, u32[]{:S(2)}) %collective-permute-start.25) | collective-permute-done | bytes 36896 | tf_op jit(solution)/shard_map/ppermute | solution.py:432
  86.0 0.8 shard_map.84
  (48 shorter events, 4.1 us)
Async XLA Ops:
  3.0 4.2 %collective-permute-start = (f32[168,128]{1,0:T(8,128)S(1)}, f32[168,128]{1,0:T(8,128)S(1)}, u32[]{:S(2)}, u32[]{:S(2)}) collective-permute-start(f32[168,128]{1,0:T(8,128)S(1)} %get-tuple-element.28), channel_id=1, source_target_pairs={{0,16},{16,0},{32,48},{48,32},{64,80},{80,64},{96,112},{112,96},{1... | collective-permute-start | bytes 258056 | tf_op jit(solution)/shard_map/ppermute | solution.py:432
  6.2 3.9 %collective-permute-start.1 = (f32[168,128]{1,0:T(8,128)S(1)}, f32[168,128]{1,0:T(8,128)S(1)}, u32[]{:S(2)}, u32[]{:S(2)}) collective-permute-start(f32[168,128]{1,0:T(8,128)S(1)} %get-tuple-element.30), channel_id=1, source_target_pairs={{16,32},{32,16},{48,64},{64,48},{80,96},{96,80},{112,128},{128,112... | collective-permute-start | bytes 258056 | tf_op jit(solution)/shard_map/ppermute | solution.py:432
  10.2 5.4 %collective-permute-start.2 = (f32[3,3,8,128]{3,2,0,1:T(8,128)S(1)}, f32[3,3,8,128]{3,2,0,1:T(8,128)S(1)}, u32[]{:S(2)}, u32[]{:S(2)}) collective-permute-start(f32[3,3,8,128]{3,2,0,1:T(8,128)S(1)} %get-tuple-element.60), channel_id=1, source_target_pairs={{0,4},{4,8},{8,12},{12,0},{1,5},{5,9},{9,13},{13,1},{2,6},{6,10},{... | collective-permute-start | bytes 110600 | tf_op jit(solution)/shard_map/ppermute | solution.py:421
  10.3 5.3 %collective-permute-start.3 = (f32[3,3,8,128]{3,2,0,1:T(8,128)S(1)}, f32[3,3,8,128]{3,2,0,1:T(8,128)S(1)}, u32[]{:S(2)}, u32[]{:S(2)}) collective-permute-start(f32[3,3,8,128]{3,2,0,1:T(8,128)S(1)} %get-tuple-element.61), channel_id=1, source_target_pairs={{4,0},{8,4},{12,8},{0,12},{5,1},{9,5},{13,9},{1,13},{6,2},{10,6},{... | collective-permute-start | bytes 110600 | tf_op jit(solution)/shard_map/ppermute | solution.py:422
  12.9 7.5 %collective-permute-start.6 = (f32[384,128]{1,0:T(8,128)S(1)}, f32[384,128]{1,0:T(8,128)S(1)}, u32[]{:S(2)}, u32[]{:S(2)}) collective-permute-start(f32[384,128]{1,0:T(8,128)S(1)} %get-tuple-element.32), channel_id=1, source_target_pairs={{0,4},{4,8},{8,12},{12,0},{1,5},{5,9},{9,13},{13,1},{2,6},{6,10},{... | collective-permute-start | bytes 589832 | tf_op jit(solution)/shard_map/ppermute | solution.py:421
  12.9 7.5 %collective-permute-start.7 = (f32[384,128]{1,0:T(8,128)S(1)}, f32[384,128]{1,0:T(8,128)S(1)}, u32[]{:S(2)}, u32[]{:S(2)}) collective-permute-start(f32[384,128]{1,0:T(8,128)S(1)} %get-tuple-element.33), channel_id=1, source_target_pairs={{4,0},{8,4},{12,8},{0,12},{5,1},{9,5},{13,9},{1,13},{6,2},{10,6},{... | collective-permute-start | bytes 589832 | tf_op jit(solution)/shard_map/ppermute | solution.py:422
  15.7 4.8 %collective-permute-start.5 = (f32[168,128]{1,0:T(8,128)S(1)}, f32[168,128]{1,0:T(8,128)S(1)}, u32[]{:S(2)}, u32[]{:S(2)}) collective-permute-start(f32[168,128]{1,0:T(8,128)S(1)} %get-tuple-element.65), channel_id=1, source_target_pairs={{1,0},{2,1},{3,2},{0,3},{5,4},{6,5},{7,6},{4,7},{9,8},{10,9},{11,1... | collective-permute-start | bytes 258056 | tf_op jit(solution)/shard_map/ppermute | solution.py:422
  16.8 4.8 %collective-permute-start.4 = (f32[168,128]{1,0:T(8,128)S(1)}, f32[168,128]{1,0:T(8,128)S(1)}, u32[]{:S(2)}, u32[]{:S(2)}) collective-permute-start(f32[168,128]{1,0:T(8,128)S(1)} %get-tuple-element.66), channel_id=1, source_target_pairs={{0,1},{1,2},{2,3},{3,0},{4,5},{5,6},{6,7},{7,4},{8,9},{9,10},{10,1... | collective-permute-start | bytes 258056 | tf_op jit(solution)/shard_map/ppermute | solution.py:421
  17.2 4.4 %copy-start = (f32[3,64,16,128]{3,2,1,0:T(8,128)S(1)}, f32[3,64,16,128]{3,2,1,0:T(8,128)}, u32[]{:S(2)}) copy-start(f32[3,64,16,128]{3,2,1,0:T(8,128)} %param.6) | copy-start | bytes 4718596
  17.2 4.4 %copy-start.1 = (f32[64,16,128]{2,1,0:T(8,128)S(1)}, f32[64,16,128]{2,1,0:T(8,128)}, u32[]{:S(2)}) copy-start(f32[64,16,128]{2,1,0:T(8,128)} %param.7) | copy-start | bytes 1572868
  29.1 13.1 %collective-permute-start.10 = (f32[384,128]{1,0:T(8,128)S(1)}, f32[384,128]{1,0:T(8,128)S(1)}, u32[]{:S(2)}, u32[]{:S(2)}) collective-permute-start(f32[384,128]{1,0:T(8,128)S(1)} %get-tuple-element.38), channel_id=1, source_target_pairs={{0,4},{4,8},{8,12},{12,0},{1,5},{5,9},{9,13},{13,1},{2,6},{6,10},{... | collective-permute-start | bytes 589832 | tf_op jit(solution)/shard_map/ppermute | solution.py:421
  29.2 13.1 %collective-permute-start.11 = (f32[384,128]{1,0:T(8,128)S(1)}, f32[384,128]{1,0:T(8,128)S(1)}, u32[]{:S(2)}, u32[]{:S(2)}) collective-permute-start(f32[384,128]{1,0:T(8,128)S(1)} %get-tuple-element.39), channel_id=1, source_target_pairs={{4,0},{8,4},{12,8},{0,12},{5,1},{9,5},{13,9},{1,13},{6,2},{10,6},{... | collective-permute-start | bytes 589832 | tf_op jit(solution)/shard_map/ppermute | solution.py:422
  31.8 5.9 %collective-permute-start.8 = (f32[96,128]{1,0:T(8,128)S(1)}, f32[96,128]{1,0:T(8,128)S(1)}, u32[]{:S(2)}, u32[]{:S(2)}) collective-permute-start(f32[96,128]{1,0:T(8,128)S(1)} %get-tuple-element.36), channel_id=1, source_target_pairs={{0,16},{16,0},{32,48},{48,32},{64,80},{80,64},{96,112},{112,96},{1... | collective-permute-start | bytes 147464 | tf_op jit(solution)/shard_map/ppermute | solution.py:432
  36.9 3.8 %collective-permute-start.9 = (f32[96,128]{1,0:T(8,128)S(1)}, f32[96,128]{1,0:T(8,128)S(1)}, u32[]{:S(2)}, u32[]{:S(2)}) collective-permute-start(f32[96,128]{1,0:T(8,128)S(1)} %get-tuple-element.37), channel_id=1, source_target_pairs={{16,32},{32,16},{48,64},{64,48},{80,96},{96,80},{112,128},{128,112... | collective-permute-start | bytes 147464 | tf_op jit(solution)/shard_map/ppermute | solution.py:432
  36.9 4.3 %collective-permute-start.13 = (f32[96,128]{1,0:T(8,128)S(1)}, f32[96,128]{1,0:T(8,128)S(1)}, u32[]{:S(2)}, u32[]{:S(2)}) collective-permute-start(f32[96,128]{1,0:T(8,128)S(1)} %get-tuple-element.40), channel_id=1, source_target_pairs={{1,0},{2,1},{3,2},{0,3},{5,4},{6,5},{7,6},{4,7},{9,8},{10,9},{11,1... | collective-permute-start | bytes 147464 | tf_op jit(solution)/shard_map/ppermute | solution.py:422
  37.8 4.4 %collective-permute-start.12 = (f32[96,128]{1,0:T(8,128)S(1)}, f32[96,128]{1,0:T(8,128)S(1)}, u32[]{:S(2)}, u32[]{:S(2)}) collective-permute-start(f32[96,128]{1,0:T(8,128)S(1)} %get-tuple-element.40), channel_id=1, source_target_pairs={{0,1},{1,2},{2,3},{3,0},{4,5},{5,6},{6,7},{7,4},{8,9},{9,10},{10,1... | collective-permute-start | bytes 147464 | tf_op jit(solution)/shard_map/ppermute | solution.py:421
  47.4 13.0 %collective-permute-start.16 = (f32[384,128]{1,0:T(8,128)S(1)}, f32[384,128]{1,0:T(8,128)S(1)}, u32[]{:S(2)}, u32[]{:S(2)}) collective-permute-start(f32[384,128]{1,0:T(8,128)S(1)} %get-tuple-element.44), channel_id=1, source_target_pairs={{0,4},{4,8},{8,12},{12,0},{1,5},{5,9},{9,13},{13,1},{2,6},{6,10},{... | collective-permute-start | bytes 589832 | tf_op jit(solution)/shard_map/ppermute | solution.py:421
  48.1 12.2 %collective-permute-start.17 = (f32[384,128]{1,0:T(8,128)S(1)}, f32[384,128]{1,0:T(8,128)S(1)}, u32[]{:S(2)}, u32[]{:S(2)}) collective-permute-start(f32[384,128]{1,0:T(8,128)S(1)} %get-tuple-element.45), channel_id=1, source_target_pairs={{4,0},{8,4},{12,8},{0,12},{5,1},{9,5},{13,9},{1,13},{6,2},{10,6},{... | collective-permute-start | bytes 589832 | tf_op jit(solution)/shard_map/ppermute | solution.py:422
  50.2 6.1 %collective-permute-start.14 = (f32[96,128]{1,0:T(8,128)S(1)}, f32[96,128]{1,0:T(8,128)S(1)}, u32[]{:S(2)}, u32[]{:S(2)}) collective-permute-start(f32[96,128]{1,0:T(8,128)S(1)} %get-tuple-element.42), channel_id=1, source_target_pairs={{0,16},{16,0},{32,48},{48,32},{64,80},{80,64},{96,112},{112,96},{1... | collective-permute-start | bytes 147464 | tf_op jit(solution)/shard_map/ppermute | solution.py:432
  55.3 3.8 %collective-permute-start.15 = (f32[96,128]{1,0:T(8,128)S(1)}, f32[96,128]{1,0:T(8,128)S(1)}, u32[]{:S(2)}, u32[]{:S(2)}) collective-permute-start(f32[96,128]{1,0:T(8,128)S(1)} %get-tuple-element.43), channel_id=1, source_target_pairs={{16,32},{32,16},{48,64},{64,48},{80,96},{96,80},{112,128},{128,112... | collective-permute-start | bytes 147464 | tf_op jit(solution)/shard_map/ppermute | solution.py:432
  55.3 3.8 %collective-permute-start.19 = (f32[96,128]{1,0:T(8,128)S(1)}, f32[96,128]{1,0:T(8,128)S(1)}, u32[]{:S(2)}, u32[]{:S(2)}) collective-permute-start(f32[96,128]{1,0:T(8,128)S(1)} %get-tuple-element.46), channel_id=1, source_target_pairs={{1,0},{2,1},{3,2},{0,3},{5,4},{6,5},{7,6},{4,7},{9,8},{10,9},{11,1... | collective-permute-start | bytes 147464 | tf_op jit(solution)/shard_map/ppermute | solution.py:422
  56.2 4.2 %collective-permute-start.18 = (f32[96,128]{1,0:T(8,128)S(1)}, f32[96,128]{1,0:T(8,128)S(1)}, u32[]{:S(2)}, u32[]{:S(2)}) collective-permute-start(f32[96,128]{1,0:T(8,128)S(1)} %get-tuple-element.46), channel_id=1, source_target_pairs={{0,1},{1,2},{2,3},{3,0},{4,5},{5,6},{6,7},{7,4},{8,9},{9,10},{10,1... | collective-permute-start | bytes 147464 | tf_op jit(solution)/shard_map/ppermute | solution.py:421
  69.9 2.9 %collective-permute-start.21 = (f32[9,8,128]{2,1,0:T(8,128)S(1)}, f32[9,8,128]{2,1,0:T(8,128)S(1)}, u32[]{:S(2)}, u32[]{:S(2)}) collective-permute-start(f32[9,8,128]{2,1,0:T(8,128)S(1)} %get-tuple-element.63), channel_id=1, source_target_pairs={{1,0},{2,1},{3,2},{0,3},{5,4},{6,5},{7,6},{4,7},{9,8},{10,9},{11,1... | collective-permute-start | bytes 110600 | tf_op jit(solution)/shard_map/ppermute | solution.py:422
  70.0 4.1 %collective-permute-start.20 = (f32[9,8,128]{2,1,0:T(8,128)S(1)}, f32[9,8,128]{2,1,0:T(8,128)S(1)}, u32[]{:S(2)}, u32[]{:S(2)}) collective-permute-start(f32[9,8,128]{2,1,0:T(8,128)S(1)} %get-tuple-element.64), channel_id=1, source_target_pairs={{0,1},{1,2},{2,3},{3,0},{4,5},{5,6},{6,7},{7,4},{8,9},{9,10},{10,1... | collective-permute-start | bytes 110600 | tf_op jit(solution)/shard_map/ppermute | solution.py:421
  76.5 2.9 %collective-permute-start.23 = (f32[3,3,8,128]{3,2,1,0:T(8,128)S(1)}, f32[3,3,8,128]{3,2,1,0:T(8,128)S(1)}, u32[]{:S(2)}, u32[]{:S(2)}) collective-permute-start(f32[3,3,8,128]{3,2,1,0:T(8,128)S(1)} %pad_maximum_fusion.6), channel_id=1, source_target_pairs={{4,0},{8,4},{12,8},{0,12},{5,1},{9,5},{13,9},{1,13},{6,2},{10,6},{... | collective-permute-start | bytes 110600 | tf_op jit(solution)/shard_map/ppermute | solution.py:422
  76.6 4.4 %collective-permute-start.22 = (f32[3,3,8,128]{3,2,1,0:T(8,128)S(1)}, f32[3,3,8,128]{3,2,1,0:T(8,128)S(1)}, u32[]{:S(2)}, u32[]{:S(2)}) collective-permute-start(f32[3,3,8,128]{3,2,1,0:T(8,128)S(1)} %pad_maximum_fusion.5), channel_id=1, source_target_pairs={{0,4},{4,8},{8,12},{12,0},{1,5},{5,9},{9,13},{13,1},{2,6},{6,10},{... | collective-permute-start | bytes 110600 | tf_op jit(solution)/shard_map/ppermute | solution.py:421
  81.0 5.0 %collective-permute-start.25 = (f32[9,8,128]{2,1,0:T(8,128)S(1)}, f32[9,8,128]{2,1,0:T(8,128)S(1)}, u32[]{:S(2)}, u32[]{:S(2)}) collective-permute-start(f32[9,8,128]{2,1,0:T(8,128)S(1)} %bitcast.75), channel_id=1, source_target_pairs={{16,32},{32,16},{48,64},{64,48},{80,96},{96,80},{112,128},{128,112... | collective-permute-start | bytes 110600 | tf_op jit(solution)/shard_map/ppermute | solution.py:432
  84.4 1.6 %collective-permute-start.24 = (f32[9,8,128]{2,1,0:T(8,128)S(1)}, f32[9,8,128]{2,1,0:T(8,128)S(1)}, u32[]{:S(2)}, u32[]{:S(2)}) collective-permute-start(f32[9,8,128]{2,1,0:T(8,128)S(1)} %bitcast.74), channel_id=1, source_target_pairs={{0,16},{16,0},{32,48},{48,32},{64,80},{80,64},{96,112},{112,96},{1... | collective-permute-start | bytes 110600 | tf_op jit(solution)/shard_map/ppermute | solution.py:432
